TPU v7x, 128 devices: a whole 4x4x4 slice. The times are simulated.
128 devices in a mesh: pipe: 4 (over x_lo, core), expert: 32 (over y, x_hi, z).
Axes of the slice: x: 4 (x_hi: 2, x_lo: 2; x = x_hi * 2 + x_lo), y: 4, z: 4, core: 2. Of those that a mesh axis runs over, the one named last changes fastest.
Arguments:
- fwd_boundary: bfloat16 [4, 2, 4096, 7168], P('pipe', None, 'expert'), may hold values from -6 to 6
- grad_boundary: bfloat16 [4, 2, 4096, 7168], P('pipe', None, 'expert'), may hold values from -6 to 6
- saved_inputs: bfloat16 [4, 2, 4096, 7168], P('pipe', None, 'expert'), may hold values from -6 to 6
- routes: int32 [4, 2, 4096, 1], P('pipe', None, 'expert'), may hold values from 0 to 7
- route_probs: float32 [4, 2, 4096, 1], P('pipe', None, 'expert'), may hold values from 0.1 to 1
- capacity: int32 [4, 8], P('pipe'), may hold values from 9 to 12, as said below
- roster: int32 [4, 2], replicated, may hold values from 0 to 1
- gate_weight: bfloat16 [4, 32, 7168, 256], P('pipe', 'expert'), may hold values from -0.0625 to 0.0625
- up_weight: bfloat16 [4, 32, 7168, 256], P('pipe', 'expert'), may hold values from -0.0625 to 0.0625
- down_weight: bfloat16 [4, 32, 256, 7168], P('pipe', 'expert'), may hold values from -0.1875 to 0.1875
Outputs:
- section_output: bfloat16 [4, 4096, 7168], P('pipe', 'expert')
- input_grad: bfloat16 [4, 4096, 7168], P('pipe', 'expert')
Inputs may be any that keep to these rules, and one draw needn't show every extreme that they name: `routes`: each token names exactly one expert. At every section some expert has capacity exactly 12.
All inputs are finite; a program needn't handle non-finite values.
Results may differ from a plain program's by a relative error of at most 0.0034.
Values may be sent and summed in bfloat16 or wider, within the bound.
No kernel may reach another device: no remote copies, remote signals or barrier semaphores. Data moves between devices by JAX's collectives and lax.ppermute only.
A program may use at most 192 MiB of HBM per device.

v0:
```python
import jax
import jax.numpy as jnp
from jax import lax
from jax.sharding import PartitionSpec as P

SPLIT = 4
CAP = 12


def from_behind(block, axis, distance):
    devices = range(lax.axis_size(axis))
    route = [((i - distance) % len(devices), i) for i in devices]
    return lax.ppermute(block, axis, route)


def route_plan(route_blk, prob_blk, limits, slots):
    token_count, route_top = route_blk.shape
    expert_count = limits.shape[0]
    flat_routes = route_blk.reshape(-1)
    onehot = (flat_routes[:, None] == jnp.arange(expert_count, dtype=jnp.int32)[None, :]).astype(
        jnp.int32
    )
    earlier = jnp.cumsum(onehot, axis=0) - onehot
    rank_of = jnp.sum(earlier * onehot, axis=1)
    bound_of = jnp.sum(onehot * limits[None, :], axis=1)
    target = jnp.where(rank_of < bound_of, flat_routes * slots + rank_of, -1).reshape(
        token_count, route_top
    )
    columns = jnp.arange(expert_count * slots, dtype=jnp.int32)
    hit_table = target[None, :, :] == columns[:, None, None]
    picker = jnp.sum(hit_table.astype(jnp.float32), axis=2)
    mixing = jnp.sum(jnp.where(hit_table, prob_blk[None, :, :], 0.0), axis=2).T
    return (picker, mixing)


def expert_work(slot_rows, gate_local, up_local, down_local):
    source_count, slot_count = (slot_rows.shape[0], slot_rows.shape[1])
    feature_dim = slot_rows.shape[3]
    fwd_rows = slot_rows[:, :, 0, :].reshape(-1, feature_dim)
    kept_rows = slot_rows[:, :, 1, :].reshape(-1, feature_dim)
    grad_rows = slot_rows[:, :, 2, :].reshape(-1, feature_dim)
    gate_act = jnp.dot(fwd_rows, gate_local, preferred_element_type=jnp.float32)
    up_act = jnp.dot(fwd_rows, up_local, preferred_element_type=jnp.float32)
    hidden = (jax.nn.silu(gate_act) * up_act).astype(jnp.bfloat16)
    out_part = jnp.dot(hidden, down_local, preferred_element_type=jnp.float32).astype(jnp.bfloat16)
    gate_back = jnp.dot(kept_rows, gate_local, preferred_element_type=jnp.float32)
    up_back = jnp.dot(kept_rows, up_local, preferred_element_type=jnp.float32)
    d_hidden = jnp.dot(grad_rows, down_local.T, preferred_element_type=jnp.float32)
    sigmoid_gate = jax.nn.sigmoid(gate_back)
    d_gate = (d_hidden * up_back * sigmoid_gate * (1.0 + gate_back * (1.0 - sigmoid_gate))).astype(
        jnp.bfloat16
    )
    d_up = (d_hidden * gate_back * sigmoid_gate).astype(jnp.bfloat16)
    in_part = (
        jnp.dot(d_gate, gate_local.T, preferred_element_type=jnp.float32)
        + jnp.dot(d_up, up_local.T, preferred_element_type=jnp.float32)
    ).astype(jnp.bfloat16)
    return jnp.stack([out_part, in_part], axis=1).reshape(source_count, slot_count, 2, feature_dim)


def pick_slot(stack, index):
    return lax.dynamic_index_in_dim(stack, index, 0, keepdims=False)


def body(
    fwd_boundary,
    grad_boundary,
    saved_inputs,
    routes,
    route_probs,
    capacity,
    roster,
    gate_weight,
    up_weight,
    down_weight,
):
    section_index = lax.axis_index("pipe")
    section_count = lax.axis_size("pipe")
    next_section = (section_index + 1) % section_count
    prev_section = (section_index + section_count - 1) % section_count
    outgoing = pick_slot(fwd_boundary[0], roster[next_section, 0])
    layer_input = from_behind(outgoing, "pipe", 1)
    returning = pick_slot(grad_boundary[0], roster[prev_section, 1])
    grad_input = from_behind(returning, "pipe", -1)
    fwd_micro = roster[section_index, 0]
    bwd_micro = roster[section_index, 1]
    kept_input = pick_slot(saved_inputs[0], bwd_micro)
    limits = capacity[0]
    expert_count = limits.shape[0]
    feature_dim = layer_input.shape[1]
    fwd_pick, fwd_mix = route_plan(
        pick_slot(routes[0], fwd_micro), pick_slot(route_probs[0], fwd_micro), limits, CAP
    )
    bwd_pick, bwd_mix = route_plan(
        pick_slot(routes[0], bwd_micro), pick_slot(route_probs[0], bwd_micro), limits, CAP
    )
    fwd_sel = fwd_pick.astype(jnp.bfloat16)
    bwd_sel = bwd_pick.astype(jnp.bfloat16)
    slot_fwd = jnp.dot(fwd_sel, layer_input, preferred_element_type=jnp.float32).astype(
        jnp.bfloat16
    )
    slot_kept = jnp.dot(bwd_sel, kept_input, preferred_element_type=jnp.float32).astype(
        jnp.bfloat16
    )
    slot_grad = jnp.dot(bwd_sel, grad_input, preferred_element_type=jnp.float32).astype(
        jnp.bfloat16
    )
    packed = jnp.stack([slot_fwd, slot_kept, slot_grad], axis=1).reshape(
        expert_count, CAP, 3, feature_dim
    )
    gate_local = gate_weight[0, 0]
    up_local = up_weight[0, 0]
    down_local = down_weight[0, 0]
    outbound = jnp.repeat(packed, SPLIT, axis=0)
    worked = expert_work(
        lax.all_to_all(outbound, "expert", split_axis=0, concat_axis=0, tiled=True),
        gate_local,
        up_local,
        down_local,
    )
    returned = lax.all_to_all(worked, "expert", split_axis=0, concat_axis=0, tiled=True)
    summed = (
        returned.reshape(expert_count, SPLIT, CAP, 2, feature_dim).astype(jnp.float32).sum(axis=1)
    )
    totals = lax.optimization_barrier(summed.astype(jnp.bfloat16))
    totals = totals.reshape(expert_count * CAP, 2, feature_dim).astype(jnp.float32)
    highest = lax.Precision.HIGHEST
    new_output = layer_input.astype(jnp.float32) + jnp.dot(
        fwd_mix, totals[:, 0, :], precision=highest, preferred_element_type=jnp.float32
    )
    new_grad = grad_input.astype(jnp.float32) + jnp.dot(
        bwd_mix, totals[:, 1, :], precision=highest, preferred_element_type=jnp.float32
    )
    return (new_output.astype(jnp.bfloat16)[None], new_grad.astype(jnp.bfloat16)[None])


def solution(mesh):
    in_specs = (
        P("pipe", None, "expert", None),
        P("pipe", None, "expert", None),
        P("pipe", None, "expert", None),
        P("pipe", None, "expert", None),
        P("pipe", None, "expert", None),
        P("pipe", None),
        P(),
        P("pipe", "expert", None, None),
        P("pipe", "expert", None, None),
        P("pipe", "expert", None, None),
    )
    out_specs = (P("pipe", "expert", None), P("pipe", "expert", None))
    return jax.shard_map(body, mesh=mesh, in_specs=in_specs, out_specs=out_specs, check_vma=False)
```

profile of v0, /device:TPU:18, one launch (start us, length us, event | category | flops | bytes accessed | tf_op | source)
XLA Modules:
  0.0 659.3 jit_solution(10787585604907872756)
XLA Ops:
  0.7 1.5 constant_dynamic-slice_fusion.7
  4.1 2.9 dynamic-slice_bitcast_fusion
  8.9 2.8 dynamic-slice_bitcast_fusion.1
  11.8 0.5 collective-permute-start
  16.1 0.1 fusion.47
  16.2 0.2 reduce_window_sum.18
  16.4 0.2 reduce_window_sum.17
  16.6 0.2 select_reduce_fusion.2
  16.8 2.0 convolution_convert_fusion.2
  18.8 1.4 stack.22
  20.3 21.7 %collective-permute-done.1 = bf16[128,7168]{1,0:T(8,128)(2,1)S(1)} collective-permute-done((bf16[128,7168]{1,0:T(8,128)(2,1)}, bf16[128,7168]{1,0:T(8,128)(2,1)S(1)}, u32[]{:S(2)}, u32[]{:S(2)}) %collective-permute-start.1) | collective-permute-done | bytes 1835040 | tf_op jit(solution)/shard_map/ppermute | solution.py:13
  41.9 0.5 convolution_convert_fusion.1
  42.5 1.4 stack.23
  43.9 5.7 collective-permute-done
  49.6 2.0 convolution_convert_fusion.3
  51.6 1.4 stack.21
  53.0 3.7 pad_maximum_fusion.1
  56.8 0.5 copy.13
  57.3 7.6 %broadcast_in_dim.41 = bf16[8,4,12,3,7168]{4,2,3,1,0:T(8,128)(2,1)} broadcast(bf16[8,12,3,7168]{3,1,2,0:T(8,128)(2,1)S(1)} %copy.13), dimensions={0,2,3,4} | broadcast | bytes 20643840 | tf_op jit(solution)/shard_map/broadcast_in_dim | solution.py:114
  65.0 255.3 %all_to_all.10 = bf16[32,12,3,7168]{3,1,2,0:T(8,128)(2,1)S(1)} all-to-all(bf16[32,12,3,7168]{3,1,2,0:T(8,128)(2,1)} %bitcast.93), channel_id=1, replica_groups=mesh['pipe'=4,'expert'=32] {'expert'}, dimensions={0} | all-to-all | bytes 33030144 | tf_op jit(solution)/shard_map/all_to_all | solution.py:116
  320.3 7.6 %fusion.72 = (bf16[32,12,1,7168]{3,1,2,0:T(8,128)(2,1)}, bf16[32,12,1,7168]{3,1,2,0:T(8,128)(2,1)}, bf16[32,12,1,7168]{3,1,2,0:T(8,128)(2,1)}) fusion(bf16[32,12,3,7168]{3,1,2,0:T(8,128)(2,1)S(1)} %all_to_all.10), kind=kLoop, calls=%fused_computation.92 | loop fusion | bytes 33030144 | tf_op jit(solution)/shard_map/slice | solution.py:39
  327.8 8.3 %reshape_squeeze.9 = bf16[384,7168]{1,0:T(8,128)(2,1)} reshape(bf16[32,12,1,7168]{3,1,2,0:T(8,128)(2,1)} %get-tuple-element.6) | data formatting | bytes 11010048 | tf_op jit(solution)/shard_map/reshape;squeeze | solution.py:39
  336.2 5.4 fusion.12
  341.6 0.9 copy-done.5
  342.5 1.6 fusion.43
  344.1 0.4 copy-done.7
  344.6 4.0 convolution_convert_fusion
  348.6 8.0 %stack.25 = bf16[32,12,1,7168]{3,1,0,2:T(8,128)(2,1)} reshape(bf16[384,7168]{1,0:T(8,128)(2,1)} %convolution_convert_fusion) | data formatting | bytes 11010048 | tf_op jit(solution)/shard_map/stack | solution.py:58
  356.6 8.3 %reshape_squeeze.11 = bf16[384,7168]{1,0:T(8,128)(2,1)} reshape(bf16[32,12,1,7168]{3,1,2,0:T(8,128)(2,1)} %get-tuple-element.7) | data formatting | bytes 11010048 | tf_op jit(solution)/shard_map/reshape;squeeze | solution.py:40
  365.0 5.3 fusion.10
  370.2 8.2 %reshape_squeeze.10 = bf16[384,7168]{1,0:T(8,128)(2,1)} reshape(bf16[32,12,1,7168]{3,1,2,0:T(8,128)(2,1)} %get-tuple-element.8) | data formatting | bytes 11010048 | tf_op jit(solution)/shard_map/reshape;squeeze | solution.py:41
  378.5 5.4 fusion
  383.9 0.9 copy-done.6
  384.8 1.6 fusion.40
  386.4 0.4 copy-done.4
  386.8 1.6 fusion.8
  388.5 4.0 add_convert_fusion
  392.5 8.0 %stack.26 = bf16[32,12,1,7168]{3,1,0,2:T(8,128)(2,1)} reshape(bf16[384,7168]{1,0:T(8,128)(2,1)} %add_convert_fusion) | data formatting | bytes 11010048 | tf_op jit(solution)/shard_map/stack | solution.py:58
  400.5 7.6 %pad_maximum_fusion = bf16[32,12,2,7168]{3,1,0,2:T(8,128)(2,1)S(1)} fusion(bf16[32,12,1,7168]{3,1,0,2:T(8,128)(2,1)} %stack.26, bf16[32,12,1,7168]{3,1,0,2:T(8,128)(2,1)} %stack.25), kind=kLoop, calls=%fused_computation | loop fusion | flops 5505024 | bytes 22020096 | tf_op jit(solution)/shard_map/stack | solution.py:58
  408.1 23.6 %copy.14 = bf16[32,12,2,7168]{3,2,1,0:T(2,128)(2,1)} copy(bf16[32,12,2,7168]{3,1,0,2:T(8,128)(2,1)S(1)} %pad_maximum_fusion) | data formatting | bytes 22020096 | tf_op jit(solution)/shard_map/stack | solution.py:58
  431.7 18.3 %all-to-all-start.1 = ((bf16[32,12,2,7168]{3,2,1,0:T(2,128)(2,1)}), bf16[32,12,2,7168]{3,2,1,0:T(2,128)(2,1)}, u32[]{:S(2)}, u32[]{:S(2)}) async-start(bf16[32,12,2,7168]{3,2,1,0:T(2,128)(2,1)} %copy.14), calls=%async_computation.1 | async-start | bytes 22020096 | tf_op jit(solution)/shard_map/all_to_all | solution.py:121
  450.1 178.5 %all-to-all-done.1 = bf16[32,12,2,7168]{3,2,1,0:T(2,128)(2,1)} async-done(((bf16[32,12,2,7168]{3,2,1,0:T(2,128)(2,1)}), bf16[32,12,2,7168]{3,2,1,0:T(2,128)(2,1)}, u32[]{:S(2)}, u32[]{:S(2)}) %all-to-all-start.1) | async-done | bytes 11010080 | tf_op jit(solution)/shard_map/all_to_all | solution.py:121
  628.6 15.6 %bitcast_reduce_fusion = bf16[8,12,2,7168]{3,2,1,0:T(2,128)(2,1)S(1)} fusion(bf16[32,12,2,7168]{3,2,1,0:T(2,128)(2,1)} %all-to-all-done.1), kind=kLoop, calls=%fused_computation.1 | loop fusion | flops 4128768 | bytes 13762560 | tf_op jit(solution)/shard_map/reduce_sum | solution.py:123
  644.2 0.7 copy.19
  645.0 2.8 copy.16
  647.8 3.8 fusion.73
  651.6 4.6 fusion.14
  656.2 3.1 fusion.15
  (23 shorter events, 0.1 us)
Async XLA Ops:
  4.1 12.0 %copy-start.8 = (s32[1,2,128,1]{2,3,1,0:T(1,128)S(1)}, s32[1,2,128,1]{2,3,1,0:T(1,128)}, u32[]{:S(2)}) copy-start(s32[1,2,128,1]{2,3,1,0:T(1,128)} %param.13) | copy-start | bytes 3076
  4.1 12.5 %copy-start.10 = (s32[1,8]{1,0:T(1,128)S(1)}, s32[1,8]{1,0:T(1,128)}, u32[]{:S(2)}) copy-start(s32[1,8]{1,0:T(1,128)} %param.15) | copy-start | bytes 100
  7.0 35.0 %collective-permute-start.1 = (bf16[128,7168]{1,0:T(8,128)(2,1)}, bf16[128,7168]{1,0:T(8,128)(2,1)S(1)}, u32[]{:S(2)}, u32[]{:S(2)}) collective-permute-start(bf16[128,7168]{1,0:T(8,128)(2,1)} %dynamic-slice_bitcast_fusion), channel_id=1, source_target_pairs={{32,0},{64,32},{96,64},{0,96},{33,1},{65,33},{97,65},{1,97},{34,2}... | collective-permute-start | bytes 5505032 | tf_op jit(solution)/shard_map/ppermute | solution.py:13
  11.8 37.8 %collective-permute-start = (bf16[128,7168]{1,0:T(8,128)(2,1)}, bf16[128,7168]{1,0:T(8,128)(2,1)}, u32[]{:S(2)}, u32[]{:S(2)}) collective-permute-start(bf16[128,7168]{1,0:T(8,128)(2,1)} %dynamic-slice_bitcast_fusion.1), channel_id=1, source_target_pairs={{96,0},{0,32},{32,64},{64,96},{97,1},{1,33},{33,65},{65,97},{98,2}... | collective-permute-start | bytes 5505032 | tf_op jit(solution)/shard_map/ppermute | solution.py:13
  41.9 9.7 %copy-start = (bf16[128,7168]{1,0:T(8,128)(2,1)}, bf16[128,7168]{1,0:T(8,128)(2,1)S(1)}, u32[]{:S(2)}) copy-start(bf16[128,7168]{1,0:T(8,128)(2,1)S(1)} %collective-permute-done.1) | copy-start | bytes 5505028
  336.2 5.4 copy-start.3
  336.2 6.3 copy-start.5
  342.5 2.0 copy-start.7
  378.5 5.4 copy-start.2
  378.5 6.3 copy-start.6
  384.8 2.0 copy-start.4
  431.7 18.3 %copy-start.9 = (f32[1,2,128,1]{2,3,1,0:T(1,128)S(1)}, f32[1,2,128,1]{2,3,1,0:T(1,128)}, u32[]{:S(2)}) copy-start(f32[1,2,128,1]{2,3,1,0:T(1,128)} %param.14) | copy-start | bytes 3076
  431.7 196.9 %all-to-all-start.1 = ((bf16[32,12,2,7168]{3,2,1,0:T(2,128)(2,1)}), bf16[32,12,2,7168]{3,2,1,0:T(2,128)(2,1)}, u32[]{:S(2)}, u32[]{:S(2)}) async-start(bf16[32,12,2,7168]{3,2,1,0:T(2,128)(2,1)} %copy.14), calls=%async_computation.1 | async-start | bytes 22020096 | tf_op jit(solution)/shard_map/all_to_all | solution.py:121
  651.6 4.6 copy-start.1
where the time goes:
time: 661 us; the launch traced here: 659 us
  blocking collectives  255 us (39%)
  waiting for transfers between devices  206 us (31%)
  local copies, waits for them, and re-layouts  102 us (15%)
  matrix products  41.1 us (6%)
  other arithmetic  27.6 us (4%)
  starting transfers between devices  18.8 us (3%)
  between operations  8.6 us (1%)
    all_to_all x1, blocking collectives, body(): lax.all_to_all(outbound, 'expert', split_axis=0, concat_axis=0, tiled=True)  255 us
    all_to_all x1, waiting for transfers between devices, body(): lax.all_to_all(worked, 'expert', split_axis=0, concat_axis=0, tiled=True)  179 us
    another operation x3, local copies, waits for them, and re-layouts, expert_work(): jnp.stack([out_part, in_part], axis=1)  39.7 us
    ppermute x2, waiting for transfers between devices, from_behind(): return lax.ppermute(block, axis, route)  27.4 us
    all_to_all x1, starting transfers between devices, body(): lax.all_to_all(worked, 'expert', split_axis=0, concat_axis=0, tiled=True)  18.3 us
    reduce_sum x1, other arithmetic, body(): returned.reshape(expert_count, SPLIT, CAP, 2, feature_dim)  15.6 us
  transfers between devices with their start and end apart: 3, of which 3 were waited for; matrix products, arithmetic and copies ran while one was open for 1% of the time, Pallas kernels for 0%

commit v1 on v0

v1 whole, which is shorter than its diff:
```python
import functools

import jax
import jax.numpy as jnp
from jax import lax
from jax.experimental import pallas as pl
from jax.experimental.pallas import tpu as pltpu
from jax.sharding import Mesh, PartitionSpec as P

CAP = 12
EXPERTS = 8
RING = 4
TOK = 128
D = 7168
HALF = D // 2
FF = 256
MSG = 2 * CAP
ROWS = EXPERTS * MSG
TILE = 512
STEPS = HALF // TILE
F32 = jnp.float32
BF16 = jnp.bfloat16
NT = (((1,), (1,)), ((), ()))
VMEM = 50 * 2**20


def slot_and_half(r):
    half = ((r >= 8) & (r < 16)) | (r >= 20)
    slot = jnp.where(r < 16, r & 7, 8 + (r & 3))
    return slot, half


def kept_ranks(routes, caps_ref):
    experts = lax.broadcasted_iota(jnp.int32, (EXPERTS, TOK), 0)
    onehot = (routes == experts).astype(F32)
    before = lax.broadcasted_iota(jnp.int32, (TOK, TOK), 0) < lax.broadcasted_iota(jnp.int32, (TOK, TOK), 1)
    earlier = jnp.dot(onehot.astype(BF16), before.astype(F32).astype(BF16), preferred_element_type=F32)
    rank = jnp.sum(onehot * earlier, axis=0, keepdims=True).astype(jnp.int32)
    bound = jnp.zeros((1, TOK), jnp.int32)
    for e in range(EXPERTS):
        bound = jnp.where(routes == e, caps_ref[e], bound)
    return jnp.where(rank < bound, rank, 99)


def pick_kernel(sel_ref, caps_ref, routes_ref, lo_ref, hi_ref, out_ref, pick_ref):
    @pl.when(pl.program_id(0) == 0)
    def _():
        routes = routes_ref[0]
        rank = kept_ranks(routes, caps_ref)
        shape = (EXPERTS, MSG, TOK)
        expert = lax.broadcasted_iota(jnp.int32, shape, 0)
        slot, half = slot_and_half(lax.broadcasted_iota(jnp.int32, shape, 1))
        hit = (routes[None] == expert) & (rank[None] == slot)
        lo = jnp.where(hit & ~half, 1.0, 0.0).reshape(ROWS, TOK)
        hi = jnp.where(hit & half, 1.0, 0.0).reshape(ROWS, TOK)
        pick_ref[...] = jnp.concatenate([lo, hi], axis=1).astype(BF16)

    rows = jnp.concatenate([lo_ref[0], hi_ref[0]], axis=0)
    out_ref[...] = jnp.dot(pick_ref[...], rows, preferred_element_type=F32).astype(BF16)


def pick(micro, caps, routes, x):
    tile = HALF // 2
    own = x.shape[0] > 1
    return pl.pallas_call(
        pick_kernel,
        out_shape=jax.ShapeDtypeStruct((ROWS, HALF), BF16),
        grid_spec=pltpu.PrefetchScalarGridSpec(
            num_scalar_prefetch=2,
            grid=(2,),
            in_specs=[
                pl.BlockSpec((1, 1, TOK), lambda i, s, c: (s[0], 0, 0)),
                pl.BlockSpec((1, TOK, tile), lambda i, s, c: (s[0] if own else 0, 0, i)),
                pl.BlockSpec((1, TOK, tile), lambda i, s, c: (s[0] if own else 0, 0, i + 2)),
            ],
            out_specs=pl.BlockSpec((ROWS, tile), lambda i, s, c: (0, i)),
            scratch_shapes=[pltpu.VMEM((ROWS, 2 * TOK), BF16)],
        ),
        compiler_params=pltpu.CompilerParams(vmem_limit_bytes=VMEM),
        cost_estimate=pl.CostEstimate(flops=2 * ROWS * 256 * HALF, bytes_accessed=2 * (TOK * D + ROWS * HALF), transcendentals=0),
        name="pick",
    )(micro, caps, routes, x, x)


def halves_mask(rows):
    r = lax.broadcasted_iota(jnp.int32, (rows // MSG, MSG, FF), 1)
    return slot_and_half(r)[1].reshape(rows, FF)


def pair_sum(v):
    v = v.reshape(-1, 3, 8, FF)
    both = v[:, 0] + v[:, 1]
    last = v[:, 2] + jnp.concatenate([v[:, 2, 4:], v[:, 2, :4]], axis=1)
    return jnp.concatenate([both[:, None], both[:, None], last[:, None]], axis=1).reshape(-1, FF)


def gate_up_step(i, xs, g_lo, g_hi, u_lo, u_hi, acc):
    x = jnp.concatenate([r[...] for r in xs], axis=0)
    for n, w in enumerate((g_lo, g_hi, u_lo, u_hi)):
        part = jnp.dot(x, w[...], preferred_element_type=F32)

        @pl.when(i == 0)
        def _():
            acc[n] = part

        @pl.when(i > 0)
        def _():
            acc[n] += part


def gate_up(acc):
    half = halves_mask(acc.shape[1])
    gate = pair_sum(jnp.where(half, acc[1], acc[0]))
    up = pair_sum(jnp.where(half, acc[3], acc[2]))
    return gate, up


def saved_kernel(x0, x1, x2, x3, x4, g_lo, g_hi, u_lo, u_hi, gate_ref, up_ref, acc):
    i = pl.program_id(0)
    gate_up_step(i, (x0, x1, x2, x3, x4), g_lo, g_hi, u_lo, u_hi, acc)

    @pl.when(i == STEPS - 1)
    def _():
        gate, up = gate_up(acc)
        gate_ref[...] = gate
        up_ref[...] = up


PIECES = (ROWS, ROWS, ROWS, ROWS // 2, ROWS // 2)
TOTAL = sum(PIECES)


def row_specs(last):
    return [pl.BlockSpec((n, TILE), lambda i: (0, jnp.minimum(i, last))) for n in PIECES]


def saved_side(xs, gate_w, up_w):
    w = [pl.BlockSpec((TILE, FF), lambda i, k=k: (i + k * STEPS, 0)) for k in (0, 1, 0, 1)]
    return pl.pallas_call(
        saved_kernel,
        out_shape=(jax.ShapeDtypeStruct((TOTAL, FF), F32),) * 2,
        grid=(STEPS,),
        in_specs=row_specs(STEPS - 1) + w,
        out_specs=(pl.BlockSpec((TOTAL, FF), lambda i: (0, 0)),) * 2,
        scratch_shapes=[pltpu.VMEM((4, TOTAL, FF), F32)],
        compiler_params=pltpu.CompilerParams(vmem_limit_bytes=VMEM),
        cost_estimate=pl.CostEstimate(
            flops=8 * TOTAL * HALF * FF, bytes_accessed=2 * (TOTAL * HALF + 2 * D * FF), transcendentals=0
        ),
        name="saved_side",
    )(*xs, gate_w, gate_w, up_w, up_w)


def split_rows(tile, outs):
    at = 0
    for o in outs:
        o[...] = tile[at : at + o.shape[0]]
        at += o.shape[0]


def forward_kernel(x0, x1, x2, x3, x4, g_lo, g_hi, u_lo, u_hi, w_lo, w_hi, o0, o1, o2, o3, o4, acc, mid):
    i = pl.program_id(0)

    @pl.when(i < STEPS)
    def _():
        gate_up_step(i, (x0, x1, x2, x3, x4), g_lo, g_hi, u_lo, u_hi, acc)

    @pl.when(i == STEPS - 1)
    def _():
        gate, up = gate_up(acc)
        hidden = gate / (1.0 + jnp.exp(-gate)) * up
        half = halves_mask(TOTAL)
        mid[0] = jnp.where(half, 0.0, hidden).astype(BF16)
        mid[1] = jnp.where(half, hidden, 0.0).astype(BF16)

    @pl.when(i >= STEPS)
    def _():
        tile = jnp.dot(mid[0], w_lo[...], preferred_element_type=F32)
        tile += jnp.dot(mid[1], w_hi[...], preferred_element_type=F32)
        split_rows(tile.astype(BF16), (o0, o1, o2, o3, o4))


def forward_side(xs, gate_w, up_w, down_w):
    first = lambda i: jnp.minimum(i, STEPS - 1)
    second = lambda i: jnp.maximum(i - STEPS, 0)
    w = [pl.BlockSpec((TILE, FF), lambda i, k=k: (first(i) + k * STEPS, 0)) for k in (0, 1, 0, 1)]
    w += [pl.BlockSpec((FF, TILE), lambda i, k=k: (0, second(i) + k * STEPS)) for k in (0, 1)]
    return pl.pallas_call(
        forward_kernel,
        out_shape=tuple(jax.ShapeDtypeStruct((n, HALF), BF16) for n in PIECES),
        grid=(2 * STEPS,),
        in_specs=row_specs(STEPS - 1) + w,
        out_specs=tuple(pl.BlockSpec((n, TILE), lambda i: (0, second(i))) for n in PIECES),
        scratch_shapes=[pltpu.VMEM((4, TOTAL, FF), F32), pltpu.VMEM((2, TOTAL, FF), BF16)],
        compiler_params=pltpu.CompilerParams(vmem_limit_bytes=VMEM),
        cost_estimate=pl.CostEstimate(
            flops=12 * TOTAL * HALF * FF, bytes_accessed=2 * (2 * TOTAL * HALF + 3 * D * FF), transcendentals=TOTAL * FF
        ),
        name="forward_side",
    )(*xs, gate_w, gate_w, up_w, up_w, down_w, down_w)


def backward_kernel(
    x0, x1, x2, x3, x4, w_lo, w_hi, gate_ref, up_ref, g_lo, g_hi, u_lo, u_hi, o0, o1, o2, o3, o4, acc, mid
):
    i = pl.program_id(0)

    @pl.when(i < STEPS)
    def _():
        x = jnp.concatenate([r[...] for r in (x0, x1, x2, x3, x4)], axis=0)
        for n, w in enumerate((w_lo, w_hi)):
            part = lax.dot_general(x, w[...], NT, preferred_element_type=F32)

            @pl.when(i == 0)
            def _():
                acc[n] = part

            @pl.when(i > 0)
            def _():
                acc[n] += part

    @pl.when(i == STEPS - 1)
    def _():
        half = halves_mask(TOTAL)
        dh = pair_sum(jnp.where(half, acc[1], acc[0]))
        gate, up = gate_ref[...], up_ref[...]
        sg = 1.0 / (1.0 + jnp.exp(-gate))
        d_gate = dh * up * sg * (1.0 + gate * (1.0 - sg))
        d_up = dh * gate * sg
        mid[0] = jnp.where(half, 0.0, d_gate).astype(BF16)
        mid[1] = jnp.where(half, d_gate, 0.0).astype(BF16)
        mid[2] = jnp.where(half, 0.0, d_up).astype(BF16)
        mid[3] = jnp.where(half, d_up, 0.0).astype(BF16)

    @pl.when(i >= STEPS)
    def _():
        tile = lax.dot_general(mid[0], g_lo[...], NT, preferred_element_type=F32)
        tile += lax.dot_general(mid[1], g_hi[...], NT, preferred_element_type=F32)
        tile += lax.dot_general(mid[2], u_lo[...], NT, preferred_element_type=F32)
        tile += lax.dot_general(mid[3], u_hi[...], NT, preferred_element_type=F32)
        split_rows(tile.astype(BF16), (o0, o1, o2, o3, o4))


def backward_side(xs, gate, up, gate_w, up_w, down_w):
    first = lambda i: jnp.minimum(i, STEPS - 1)
    second = lambda i: jnp.maximum(i - STEPS, 0)
    w = [pl.BlockSpec((FF, TILE), lambda i, k=k: (0, first(i) + k * STEPS)) for k in (0, 1)]
    w += [pl.BlockSpec((TOTAL, FF), lambda i: (0, 0))] * 2
    w += [pl.BlockSpec((TILE, FF), lambda i, k=k: (second(i) + k * STEPS, 0)) for k in (0, 1, 0, 1)]
    return pl.pallas_call(
        backward_kernel,
        out_shape=tuple(jax.ShapeDtypeStruct((n, HALF), BF16) for n in PIECES),
        grid=(2 * STEPS,),
        in_specs=row_specs(STEPS - 1) + w,
        out_specs=tuple(pl.BlockSpec((n, TILE), lambda i: (0, second(i))) for n in PIECES),
        scratch_shapes=[pltpu.VMEM((2, TOTAL, FF), F32), pltpu.VMEM((4, TOTAL, FF), BF16)],
        compiler_params=pltpu.CompilerParams(vmem_limit_bytes=VMEM),
        cost_estimate=pl.CostEstimate(
            flops=12 * TOTAL * HALF * FF, bytes_accessed=2 * (2 * TOTAL * HALF + 3 * D * FF), transcendentals=TOTAL * FF
        ),
        name="backward_side",
    )(*xs, down_w, down_w, gate, up, gate_w, gate_w, up_w, up_w)


def mix_kernel(sel_ref, caps_ref, routes_ref, probs_ref, total_ref, x_ref, out_ref, spread_ref, prob_ref):
    h = pl.program_id(1)

    @pl.when((pl.program_id(0) == 0) & (h == 0))
    def _():
        routes = routes_ref[0]
        rank = kept_ranks(routes, caps_ref)
        eye = lax.broadcasted_iota(jnp.int32, (TOK, TOK), 0) == lax.broadcasted_iota(jnp.int32, (TOK, TOK), 1)
        column = lambda row: jnp.sum(jnp.where(eye, row, 0.0), axis=1, keepdims=True)
        route_col = column(routes.astype(F32)).astype(jnp.int32)
        rank_col = column(rank.astype(F32)).astype(jnp.int32)
        prob_ref[...] = jnp.broadcast_to(column(probs_ref[0]), (TOK, TOK))
        lane = lax.broadcasted_iota(jnp.int32, (TOK, ROWS), 1)
        expert = (lane * 2731) >> 16
        slot, half = slot_and_half(lane - expert * MSG)
        hit = (route_col == expert) & (rank_col == slot)
        spread_ref[0] = jnp.where(hit & ~half, 1.0, 0.0).astype(BF16)
        spread_ref[1] = jnp.where(hit & half, 1.0, 0.0).astype(BF16)

    found = jnp.dot(spread_ref[h], total_ref[...], preferred_element_type=F32)
    prob = prob_ref[:, :1]
    out_ref[...] = (x_ref[...].astype(F32) + prob * found).astype(BF16)


def mix(micro, caps, routes, probs, totals, x):
    tiles = 2
    tile = HALF // tiles
    return pl.pallas_call(
        mix_kernel,
        out_shape=jax.ShapeDtypeStruct((TOK, D), BF16),
        grid_spec=pltpu.PrefetchScalarGridSpec(
            num_scalar_prefetch=2,
            grid=(tiles, 2),
            in_specs=[
                pl.BlockSpec((1, 1, TOK), lambda n, h, s, c: (s[0], 0, 0)),
                pl.BlockSpec((1, 1, TOK), lambda n, h, s, c: (s[0], 0, 0)),
                pl.BlockSpec((ROWS, tile), lambda n, h, s, c: (0, n)),
                pl.BlockSpec((TOK, tile), lambda n, h, s, c: (0, h * tiles + n)),
            ],
            out_specs=pl.BlockSpec((TOK, tile), lambda n, h, s, c: (0, h * tiles + n)),
            scratch_shapes=[pltpu.VMEM((2, TOK, ROWS), BF16), pltpu.VMEM((TOK, TOK), F32)],
        ),
        compiler_params=pltpu.CompilerParams(vmem_limit_bytes=VMEM),
        cost_estimate=pl.CostEstimate(
            flops=4 * ROWS * TOK * HALF, bytes_accessed=2 * (2 * TOK * D + ROWS * HALF), transcendentals=0
        ),
        name="mix",
    )(micro, caps, routes, probs, totals, x)


def shift(x, axis, by):
    n = lax.axis_size(axis)
    return lax.ppermute(x, axis, [(i, (i + by) % n) for i in range(n)])


def exchange(x):
    return lax.all_to_all(x, ("y", "xh"), 0, 0, tiled=True)


def gather_ring(x):
    left = shift(x, "z", 1)
    right = shift(x, "z", -1)
    half = ROWS // 2
    return x, left, right, shift(left[:half], "z", 1), shift(right[half:], "z", -1)


def add(*terms):
    return sum(t.astype(F32) for t in terms).astype(BF16)


def scatter_ring(own, left, right, far_lo, far_hi):
    half = ROWS // 2
    a = shift(far_lo, "z", 1)
    b = shift(far_hi, "z", -1)
    r_hi = shift(right[half:], "z", 1)
    l_lo = shift(left[:half], "z", -1)
    r_lo = shift(add(right[:half], a), "z", 1)
    l_hi = shift(add(left[half:], b), "z", -1)
    return jnp.concatenate([add(own[:half], r_lo, l_lo), add(own[half:], r_hi, l_hi)], axis=0)


def body(
    fwd_boundary,
    grad_boundary,
    saved_inputs,
    routes,
    route_probs,
    capacity,
    roster,
    gate_weight,
    up_weight,
    down_weight,
):
    section = lax.axis_index("pipe")
    sections = lax.axis_size("pipe")
    after = (section + 1) % sections
    before = (section + sections - 1) % sections
    take = lambda stack, index: lax.dynamic_index_in_dim(stack, index, 0, keepdims=False)
    layer_input = shift(take(fwd_boundary[0], roster[after, 0]), "pipe", 1)
    grad_input = shift(take(grad_boundary[0], roster[before, 1]), "pipe", -1)
    fwd_micro = roster[section, 0].reshape(1)
    bwd_micro = roster[section, 1].reshape(1)
    caps = capacity[0]
    route_rows = routes.reshape(2, 1, TOK)
    prob_rows = route_probs.reshape(2, 1, TOK)
    gate_w, up_w, down_w = gate_weight[0, 0], up_weight[0, 0], down_weight[0, 0]

    kept = gather_ring(exchange(pick(bwd_micro, caps, route_rows, saved_inputs[0])))
    fwd = gather_ring(exchange(pick(fwd_micro, caps, route_rows, layer_input[None])))
    grad = gather_ring(exchange(pick(bwd_micro, caps, route_rows, grad_input[None])))
    gate, up = saved_side(kept, gate_w, up_w)
    own, left, right, far_lo, far_hi = forward_side(fwd, gate_w, up_w, down_w)
    fwd_total = exchange(scatter_ring(own, left, right, far_lo, far_hi))
    own, left, right, far_lo, far_hi = backward_side(grad, gate, up, gate_w, up_w, down_w)
    bwd_total = exchange(scatter_ring(own, left, right, far_lo, far_hi))
    new_output = mix(fwd_micro, caps, route_rows, prob_rows, fwd_total, layer_input)
    new_grad = mix(bwd_micro, caps, route_rows, prob_rows, bwd_total, grad_input)
    return new_output[None], new_grad[None]


def solution(mesh):
    grid = Mesh(mesh.devices.reshape(4, 4, 2, 4), ("pipe", "y", "xh", "z"))
    expert = ("y", "xh", "z")
    rows = P("pipe", None, expert, None)
    weight = P("pipe", expert, None, None)
    in_specs = (rows,) * 5 + (P("pipe", None), P()) + (weight,) * 3
    out_specs = (P("pipe", expert, None),) * 2
    return jax.shard_map(body, mesh=grid, in_specs=in_specs, out_specs=out_specs, check_vma=False)
```

time: 661 us -> 356 us (0.54)
  the two profiles are of different devices: /device:TPU:18 before, /device:TPU:64 now
where the time goes in v1:
time: 356 us; the launch traced here: 354 us
  waiting for transfers between devices  179 us (50%)
  Pallas kernels  90.2 us (25%)
  starting transfers between devices  55.5 us (16%)
  local copies, waits for them, and re-layouts  16.6 us (5%)
  other arithmetic  7.96 us (2%)
  between operations  4.91 us (1%)
    ppermute x26, waiting for transfers between devices, shift(): return lax.ppermute(x, axis, [(i, (i + by) % n) for i in range(n)])  97.4 us
    all_to_all x5, waiting for transfers between devices, exchange(): return lax.all_to_all(x, ('y', 'xh'), 0, 0, tiled=True)  81.9 us
    ppermute x26, starting transfers between devices, shift(): return lax.ppermute(x, axis, [(i, (i + by) % n) for i in range(n)])  30.1 us
    pallas_call x1, Pallas kernels, forward_side(): pl.pallas_call(forward_kernel, out_shape=tuple((jax.ShapeDtypeStruct((n,...  27.2 us
    all_to_all x5, starting transfers between devices, exchange(): return lax.all_to_all(x, ('y', 'xh'), 0, 0, tiled=True)  25.4 us
    pallas_call x1, Pallas kernels, backward_side(): pl.pallas_call(backward_kernel, out_shape=tuple((jax.ShapeDtypeStruct((n,...  22 us
    pallas_call x1, Pallas kernels, saved_side(): pl.pallas_call(saved_kernel, out_shape=(jax.ShapeDtypeStruct((TOTAL, FF),...  19.6 us
    pallas_call x3, Pallas kernels, pick(): pl.pallas_call(pick_kernel, out_shape=jax.ShapeDtypeStruct((ROWS, HALF),...  11.4 us
  transfers between devices with their start and end apart: 31, of which 13 were waited for; matrix products, arithmetic and copies ran while one was open for 6% of the time, Pallas kernels for 24%

profile of v1, /device:TPU:64, one launch (start us, length us, event | category | flops | bytes accessed | tf_op | source)
XLA Modules:
  0.0 354.5 jit_solution(18151431287234670373)
XLA Ops:
  0.7 1.5 constant_dynamic-slice_fusion.2
  4.1 2.9 dynamic-slice_bitcast_fusion
  7.9 4.2 %pick.5 = bf16[192,3584]{1,0:T(8,128)(2,1)} custom-call(s32[1]{0:T(128)} %bitcast.15.sel_ref, s32[8]{0:T(128)S(1)} %bitcast.37, s32[2,1,128]{2,1,0:T(1,128)S(1)} %bitcast.32, bf16[2,128,7168]{2,1,0:T(8,128)(2,1)} %bitcast.44, bf16[2,128,7168]{2,1,0:T(8,128)(2,1)} %bitcast.45), custom_call_target="tpu_custom_call" | custom-call | flops 352321536 | bytes 3211264 | tf_op jit(solution)/shard_map/pick/pallas_call | solution.py:65
  12.1 6.6 %all-to-all-start.3 = ((bf16[8,24,3584]{2,1,0:T(8,128)(2,1)}), bf16[8,24,3584]{2,1,0:T(8,128)(2,1)}, u32[]{:S(2)}, u32[]{:S(2)}) async-start(bf16[8,24,3584]{2,1,0:T(8,128)(2,1)} %bitcast.22), calls=%async_computation.3 | async-start | bytes 2752512 | tf_op jit(solution)/shard_map/all_to_all | solution.py:321
  20.8 2.9 dynamic-slice_bitcast_fusion.1
  23.7 15.2 %collective-permute-done.11.x_ref = bf16[128,7168]{1,0:T(8,128)(2,1)S(1)} collective-permute-done((bf16[128,7168]{1,0:T(8,128)(2,1)}, bf16[128,7168]{1,0:T(8,128)(2,1)S(1)}, u32[]{:S(2)}, u32[]{:S(2)}) %collective-permute-start.11) | collective-permute-done | bytes 1835040 | tf_op jit(solution)/shard_map/ppermute | solution.py:317
  38.8 3.1 pick.4
  41.9 17.1 %all-to-all-done.3 = bf16[8,24,3584]{2,1,0:T(8,128)(2,1)} async-done(((bf16[8,24,3584]{2,1,0:T(8,128)(2,1)}), bf16[8,24,3584]{2,1,0:T(8,128)(2,1)}, u32[]{:S(2)}, u32[]{:S(2)}) %all-to-all-start.3) | async-done | bytes 1376288 | tf_op jit(solution)/shard_map/all_to_all | solution.py:321
  59.0 4.3 %all-to-all-start.2 = ((bf16[8,24,3584]{2,1,0:T(8,128)(2,1)}), bf16[8,24,3584]{2,1,0:T(8,128)(2,1)}, u32[]{:S(2)}, u32[]{:S(2)}) async-start(bf16[8,24,3584]{2,1,0:T(8,128)(2,1)} %bitcast.19), calls=%async_computation.2 | async-start | bytes 2752512 | tf_op jit(solution)/shard_map/all_to_all | solution.py:321
  63.3 1.7 collective-permute-start.16
  65.4 18.4 %all-to-all-done.2 = bf16[8,24,3584]{2,1,0:T(8,128)(2,1)} async-done(((bf16[8,24,3584]{2,1,0:T(8,128)(2,1)}), bf16[8,24,3584]{2,1,0:T(8,128)(2,1)}, u32[]{:S(2)}, u32[]{:S(2)}) %all-to-all-start.2) | async-done | bytes 1376288 | tf_op jit(solution)/shard_map/all_to_all | solution.py:321
  83.8 1.6 collective-permute-start.12
  85.4 4.1 %pick.3 = bf16[192,3584]{1,0:T(8,128)(2,1)} custom-call(s32[1]{0:T(128)} %bitcast.sel_ref, s32[8]{0:T(128)S(1)} %bitcast.39, s32[2,1,128]{2,1,0:T(1,128)S(1)} %bitcast.34, bf16[1,128,7168]{2,1,0:T(8,128)(2,1)} %bitcast.6.lo_ref.hi_ref, bf16[1,128,7168]{2,1,0:T(8,128)(2,1)} %bitcast.6.lo_ref.hi_ref), custom_call_target="tpu_custom_call" | custom-call | flops 352321536 | bytes 3211264 | tf_op jit(solution)/shard_map/pick/pallas_call | solution.py:65
  89.5 3.6 %all-to-all-start = ((bf16[8,24,3584]{2,1,0:T(8,128)(2,1)}), bf16[8,24,3584]{2,1,0:T(8,128)(2,1)S(1)}, u32[]{:S(2)}, u32[]{:S(2)}) async-start(bf16[8,24,3584]{2,1,0:T(8,128)(2,1)} %bitcast.7), calls=%async_computation | async-start | bytes 2752512 | tf_op jit(solution)/shard_map/all_to_all | solution.py:321
  93.5 18.7 %all-to-all-done = bf16[8,24,3584]{2,1,0:T(8,128)(2,1)S(1)} async-done(((bf16[8,24,3584]{2,1,0:T(8,128)(2,1)}), bf16[8,24,3584]{2,1,0:T(8,128)(2,1)S(1)}, u32[]{:S(2)}, u32[]{:S(2)}) %all-to-all-start) | async-done | bytes 1376288 | tf_op jit(solution)/shard_map/all_to_all | solution.py:321
  112.5 1.7 collective-permute-start.2
  114.3 1.1 slice.76
  115.8 1.1 slice.77
  117.2 1.6 collective-permute-start.19
  118.8 1.1 slice.74
  119.9 6.6 %collective-permute-done.13.x2 = bf16[192,3584]{1,0:T(8,128)(2,1)} collective-permute-done((bf16[192,3584]{1,0:T(8,128)(2,1)}, bf16[192,3584]{1,0:T(8,128)(2,1)}, u32[]{:S(2)}, u32[]{:S(2)}) %collective-permute-start.13) | collective-permute-done | bytes 1376288 | tf_op jit(solution)/shard_map/ppermute | solution.py:317
  126.6 1.2 collective-permute-start.14
  127.8 1.1 slice.75
  128.9 32.4 %collective-permute-done.18.x3 = bf16[96,3584]{1,0:T(8,128)(2,1)S(1)} collective-permute-done((bf16[96,3584]{1,0:T(8,128)(2,1)S(1)}, bf16[96,3584]{1,0:T(8,128)(2,1)S(1)}, u32[]{:S(2)}, u32[]{:S(2)}) %collective-permute-start.18) | collective-permute-done | bytes 688160 | tf_op jit(solution)/shard_map/ppermute | solution.py:317
  161.3 9.3 %collective-permute-done.19.x4 = bf16[96,3584]{1,0:T(8,128)(2,1)S(1)} collective-permute-done((bf16[96,3584]{1,0:T(8,128)(2,1)S(1)}, bf16[96,3584]{1,0:T(8,128)(2,1)S(1)}, u32[]{:S(2)}, u32[]{:S(2)}) %collective-permute-start.19) | collective-permute-done | bytes 688160 | tf_op jit(solution)/shard_map/ppermute | solution.py:317
  170.7 19.6 %saved_side.1 = (f32[768,256]{1,0:T(8,128)S(1)}, f32[768,256]{1,0:T(8,128)S(1)}) custom-call(bf16[192,3584]{1,0:T(8,128)(2,1)} %bitcast.23.x0, bf16[192,3584]{1,0:T(8,128)(2,1)} %collective-permute-done.16.x1, bf16[192,3584]{1,0:T(8,128)(2,1)} %collective-permute-done.17.x2, bf16[96,3584]{1,0:T(8,128)(2,1)S(1)} %collective-permute-done.18.x3, ...), custom_call_target="tpu_custom_call" | custom-call | flops 5637144576 | bytes 12845056 | tf_op jit(solution)/shard_map/saved_side/pallas_call | solution.py:139
  190.4 1.3 collective-permute-start.3
  192.6 22.0 %backward_side.1 = (bf16[192,3584]{1,0:T(8,128)(2,1)}, bf16[192,3584]{1,0:T(8,128)(2,1)}, bf16[192,3584]{1,0:T(8,128)(2,1)}, bf16[96,3584]{1,0:T(8,128)(2,1)S(1)}, bf16[96,3584]{1,0:T(8,128)(2,1)S(1)}) custom-call(bf16[192,3584]{1,0:T(8,128)(2,1)} %bitcast.20.x0, bf16[192,3584]{1,0:T(8,128)(2,1)} %collective-permute-done.12.x1, ...), custom_call_target="tpu_custom_call" | custom-call | flops 8455716864 | bytes 22020096 | tf_op jit(solution)/shard_map/backward_side/pallas_call | solution.py:250
  215.3 1.6 collective-permute-start.20
  216.9 1.1 slice.68
  218.6 2.1 collective-permute-start.23
  220.7 27.2 %forward_side.1 = (bf16[192,3584]{1,0:T(8,128)(2,1)S(1)}, bf16[192,3584]{1,0:T(8,128)(2,1)}, bf16[192,3584]{1,0:T(8,128)(2,1)}, bf16[96,3584]{1,0:T(8,128)(2,1)S(1)}, bf16[96,3584]{1,0:T(8,128)(2,1)S(1)}) custom-call(bf16[192,3584]{1,0:T(8,128)(2,1)} %bitcast.52, bf16[192,3584]{1,0:T(8,128)(2,1)} %copy-done.11, bf16[192,3584]{1,0:T(8,128)(2,1)} %copy-done.12, ...), custom_call_target="tpu_custom_call" | custom-call | flops 8455716864 | bytes 22020096 | tf_op jit(solution)/shard_map/forward_side/pallas_call | solution.py:188
  248.0 2.5 slice.58
  251.4 3.2 collective-permute-start.5
  255.1 12.4 %collective-permute-done.9 = bf16[96,3584]{1,0:T(8,128)(2,1)S(1)} collective-permute-done((bf16[96,3584]{1,0:T(8,128)(2,1)S(1)}, bf16[96,3584]{1,0:T(8,128)(2,1)S(1)}, u32[]{:S(2)}, u32[]{:S(2)}) %collective-permute-start.9) | collective-permute-done | bytes 688160 | tf_op jit(solution)/shard_map/ppermute | solution.py:317
  268.6 3.2 collective-permute-start.21
  272.9 3.2 collective-permute-start.8
  276.1 20.7 %collective-permute-done.25 = bf16[96,3584]{1,0:T(8,128)(2,1)S(1)} collective-permute-done((bf16[96,3584]{1,0:T(8,128)(2,1)S(1)}, bf16[96,3584]{1,0:T(8,128)(2,1)S(1)}, u32[]{:S(2)}, u32[]{:S(2)}) %collective-permute-start.25) | collective-permute-done | bytes 688160 | tf_op jit(solution)/shard_map/ppermute | solution.py:317
  296.8 3.0 collective-permute-start.6
  300.3 1.2 pad_maximum_fusion.1
  301.5 6.5 %all-to-all-start.4 = ((bf16[8,24,3584]{2,1,0:T(8,128)(2,1)}), bf16[8,24,3584]{2,1,0:T(8,128)(2,1)S(1)}, u32[]{:S(2)}, u32[]{:S(2)}) async-start(bf16[8,24,3584]{2,1,0:T(8,128)(2,1)} %bitcast.46), calls=%async_computation.4 | async-start | bytes 2752512 | tf_op jit(solution)/shard_map/all_to_all | solution.py:321
  308.5 2.6 add_convert_fusion.6
  311.1 1.2 pad_maximum_fusion
  312.3 17.1 %all-to-all-done.4 = bf16[8,24,3584]{2,1,0:T(8,128)(2,1)S(1)} async-done(((bf16[8,24,3584]{2,1,0:T(8,128)(2,1)}), bf16[8,24,3584]{2,1,0:T(8,128)(2,1)S(1)}, u32[]{:S(2)}, u32[]{:S(2)}) %all-to-all-start.4) | async-done | bytes 1376288 | tf_op jit(solution)/shard_map/all_to_all | solution.py:321
  329.4 4.4 %all-to-all-start.1 = ((bf16[8,24,3584]{2,1,0:T(8,128)(2,1)}), bf16[8,24,3584]{2,1,0:T(8,128)(2,1)}, u32[]{:S(2)}, u32[]{:S(2)}) async-start(bf16[8,24,3584]{2,1,0:T(8,128)(2,1)} %bitcast.47), calls=%async_computation.1 | async-start | bytes 2752512 | tf_op jit(solution)/shard_map/all_to_all | solution.py:321
  333.8 4.1 %mix.3 = bf16[128,7168]{1,0:T(8,128)(2,1)} custom-call(s32[1]{0:T(128)} %bitcast.15.sel_ref, s32[8]{0:T(128)S(1)} %bitcast.40, s32[2,1,128]{2,1,0:T(1,128)S(1)} %bitcast.35, f32[2,1,128]{2,1,0:T(1,128)S(1)} %bitcast.42, bf16[192,3584]{1,0:T(8,128)(2,1)S(1)} %bitcast.31, bf16[128,7168]{1,0:T(8,128)(2,1)S(1)} %collective-permute-done.11.x_ref), custom_call_target="tpu_custom_call" | custom-call | flops 352321536 | bytes 5046272 | tf_op jit(solution)/shard_map/mix/pallas_call | solution.py:292
  338.0 10.6 %all-to-all-done.1 = bf16[8,24,3584]{2,1,0:T(8,128)(2,1)} async-done(((bf16[8,24,3584]{2,1,0:T(8,128)(2,1)}), bf16[8,24,3584]{2,1,0:T(8,128)(2,1)}, u32[]{:S(2)}, u32[]{:S(2)}) %all-to-all-start.1) | async-done | bytes 1376288 | tf_op jit(solution)/shard_map/all_to_all | solution.py:321
  348.6 5.9 %mix.2 = bf16[128,7168]{1,0:T(8,128)(2,1)} custom-call(s32[1]{0:T(128)} %bitcast.sel_ref, s32[8]{0:T(128)S(1)} %bitcast.41, s32[2,1,128]{2,1,0:T(1,128)S(1)} %bitcast.36, f32[2,1,128]{2,1,0:T(1,128)S(1)} %bitcast.43, bf16[192,3584]{1,0:T(8,128)(2,1)} %bitcast.13.total_ref, bf16[128,7168]{1,0:T(8,128)(2,1)} %collective-permute-done.x_ref), custom_call_target="tpu_custom_call" | custom-call | flops 352321536 | bytes 5046272 | tf_op jit(solution)/shard_map/mix/pallas_call | solution.py:292
  (69 shorter events, 9.5 us)
Async XLA Ops:
  4.1 3.8 %copy-start.1 = (s32[1,2,128,1]{2,3,1,0:T(1,128)S(1)}, s32[1,2,128,1]{2,3,1,0:T(1,128)}, u32[]{:S(2)}) copy-start(s32[1,2,128,1]{2,3,1,0:T(1,128)} %param.13) | copy-start | bytes 3076
  4.1 3.8 %copy-start.2 = (s32[1,8]{1,0:T(1,128)S(1)}, s32[1,8]{1,0:T(1,128)}, u32[]{:S(2)}) copy-start(s32[1,8]{1,0:T(1,128)} %param.15) | copy-start | bytes 100
  7.0 31.8 %collective-permute-start.11 = (bf16[128,7168]{1,0:T(8,128)(2,1)}, bf16[128,7168]{1,0:T(8,128)(2,1)S(1)}, u32[]{:S(2)}, u32[]{:S(2)}) collective-permute-start(bf16[128,7168]{1,0:T(8,128)(2,1)} %dynamic-slice_bitcast_fusion), channel_id=1, source_target_pairs={{0,96},{32,0},{64,32},{96,64},{1,97},{33,1},{65,33},{97,65},{2,98}... | collective-permute-start | bytes 5505032 | tf_op jit(solution)/shard_map/ppermute | solution.py:317
  12.1 46.9 %all-to-all-start.3 = ((bf16[8,24,3584]{2,1,0:T(8,128)(2,1)}), bf16[8,24,3584]{2,1,0:T(8,128)(2,1)}, u32[]{:S(2)}, u32[]{:S(2)}) async-start(bf16[8,24,3584]{2,1,0:T(8,128)(2,1)} %bitcast.22), calls=%async_computation.3 | async-start | bytes 2752512 | tf_op jit(solution)/shard_map/all_to_all | solution.py:321
  23.7 61.7 %collective-permute-start = (bf16[128,7168]{1,0:T(8,128)(2,1)}, bf16[128,7168]{1,0:T(8,128)(2,1)}, u32[]{:S(2)}, u32[]{:S(2)}) collective-permute-start(bf16[128,7168]{1,0:T(8,128)(2,1)} %dynamic-slice_bitcast_fusion.1), channel_id=1, source_target_pairs={{0,32},{32,64},{64,96},{96,0},{1,33},{33,65},{65,97},{97,1},{2,34}... | collective-permute-start | bytes 5505032 | tf_op jit(solution)/shard_map/ppermute | solution.py:317
  59.0 24.8 %all-to-all-start.2 = ((bf16[8,24,3584]{2,1,0:T(8,128)(2,1)}), bf16[8,24,3584]{2,1,0:T(8,128)(2,1)}, u32[]{:S(2)}, u32[]{:S(2)}) async-start(bf16[8,24,3584]{2,1,0:T(8,128)(2,1)} %bitcast.19), calls=%async_computation.2 | async-start | bytes 2752512 | tf_op jit(solution)/shard_map/all_to_all | solution.py:321
  63.3 49.2 %collective-permute-start.16 = (bf16[192,3584]{1,0:T(8,128)(2,1)}, bf16[192,3584]{1,0:T(8,128)(2,1)}, u32[]{:S(2)}, u32[]{:S(2)}) collective-permute-start(bf16[192,3584]{1,0:T(8,128)(2,1)} %bitcast.23.x0), channel_id=1, source_target_pairs={{0,1},{1,2},{2,3},{3,0},{4,5},{5,6},{6,7},{7,4},{8,9},{9,10},{10,1... | collective-permute-start | bytes 4128776 | tf_op jit(solution)/shard_map/ppermute | solution.py:317
  65.0 50.4 %collective-permute-start.17 = (bf16[192,3584]{1,0:T(8,128)(2,1)}, bf16[192,3584]{1,0:T(8,128)(2,1)}, u32[]{:S(2)}, u32[]{:S(2)}) collective-permute-start(bf16[192,3584]{1,0:T(8,128)(2,1)} %bitcast.23.x0), channel_id=1, source_target_pairs={{0,3},{1,0},{2,1},{3,2},{4,7},{5,4},{6,5},{7,6},{8,11},{9,8},{10,9... | collective-permute-start | bytes 4128776 | tf_op jit(solution)/shard_map/ppermute | solution.py:317
  83.8 33.4 %collective-permute-start.12 = (bf16[192,3584]{1,0:T(8,128)(2,1)}, bf16[192,3584]{1,0:T(8,128)(2,1)}, u32[]{:S(2)}, u32[]{:S(2)}) collective-permute-start(bf16[192,3584]{1,0:T(8,128)(2,1)} %bitcast.20.x0), channel_id=1, source_target_pairs={{0,1},{1,2},{2,3},{3,0},{4,5},{5,6},{6,7},{7,4},{8,9},{9,10},{10,1... | collective-permute-start | bytes 4128776 | tf_op jit(solution)/shard_map/ppermute | solution.py:317
  89.5 22.8 %all-to-all-start = ((bf16[8,24,3584]{2,1,0:T(8,128)(2,1)}), bf16[8,24,3584]{2,1,0:T(8,128)(2,1)S(1)}, u32[]{:S(2)}, u32[]{:S(2)}) async-start(bf16[8,24,3584]{2,1,0:T(8,128)(2,1)} %bitcast.7), calls=%async_computation | async-start | bytes 2752512 | tf_op jit(solution)/shard_map/all_to_all | solution.py:321
  93.0 33.5 %collective-permute-start.13 = (bf16[192,3584]{1,0:T(8,128)(2,1)}, bf16[192,3584]{1,0:T(8,128)(2,1)}, u32[]{:S(2)}, u32[]{:S(2)}) collective-permute-start(bf16[192,3584]{1,0:T(8,128)(2,1)} %bitcast.20.x0), channel_id=1, source_target_pairs={{0,3},{1,0},{2,1},{3,2},{4,7},{5,4},{6,5},{7,6},{8,11},{9,8},{10,9... | collective-permute-start | bytes 4128776 | tf_op jit(solution)/shard_map/ppermute | solution.py:317
  112.2 4.7 %copy-start.5 = (bf16[8,24,3584]{2,1,0:T(8,128)(2,1)}, bf16[8,24,3584]{2,1,0:T(8,128)(2,1)S(1)}, u32[]{:S(2)}) copy-start(bf16[8,24,3584]{2,1,0:T(8,128)(2,1)S(1)} %all-to-all-done) | copy-start | bytes 4128772
  112.2 78.0 %collective-permute-start.1 = (bf16[192,3584]{1,0:T(8,128)(2,1)S(1)}, bf16[192,3584]{1,0:T(8,128)(2,1)S(1)}, u32[]{:S(2)}, u32[]{:S(2)}) collective-permute-start(bf16[192,3584]{1,0:T(8,128)(2,1)S(1)} %bitcast.50), channel_id=1, source_target_pairs={{0,1},{1,2},{2,3},{3,0},{4,5},{5,6},{6,7},{7,4},{8,9},{9,10},{10,1... | collective-permute-start | bytes 4128776 | tf_op jit(solution)/shard_map/ppermute | solution.py:317
  112.5 79.1 %collective-permute-start.2 = (bf16[192,3584]{1,0:T(8,128)(2,1)S(1)}, bf16[192,3584]{1,0:T(8,128)(2,1)S(1)}, u32[]{:S(2)}, u32[]{:S(2)}) collective-permute-start(bf16[192,3584]{1,0:T(8,128)(2,1)S(1)} %bitcast.51), channel_id=1, source_target_pairs={{0,3},{1,0},{2,1},{3,2},{4,7},{5,4},{6,5},{7,6},{8,11},{9,8},{10,9... | collective-permute-start | bytes 4128776 | tf_op jit(solution)/shard_map/ppermute | solution.py:317
  115.4 45.9 %collective-permute-start.18 = (bf16[96,3584]{1,0:T(8,128)(2,1)S(1)}, bf16[96,3584]{1,0:T(8,128)(2,1)S(1)}, u32[]{:S(2)}, u32[]{:S(2)}) collective-permute-start(bf16[96,3584]{1,0:T(8,128)(2,1)S(1)} %slice.76), channel_id=1, source_target_pairs={{0,1},{1,2},{2,3},{3,0},{4,5},{5,6},{6,7},{7,4},{8,9},{9,10},{10,1... | collective-permute-start | bytes 2064392 | tf_op jit(solution)/shard_map/ppermute | solution.py:317
  117.2 53.5 %collective-permute-start.19 = (bf16[96,3584]{1,0:T(8,128)(2,1)S(1)}, bf16[96,3584]{1,0:T(8,128)(2,1)S(1)}, u32[]{:S(2)}, u32[]{:S(2)}) collective-permute-start(bf16[96,3584]{1,0:T(8,128)(2,1)S(1)} %slice.77), channel_id=1, source_target_pairs={{0,3},{1,0},{2,1},{3,2},{4,7},{5,4},{6,5},{7,6},{8,11},{9,8},{10,9... | collective-permute-start | bytes 2064392 | tf_op jit(solution)/shard_map/ppermute | solution.py:317
  126.6 66.0 %collective-permute-start.14 = (bf16[96,3584]{1,0:T(8,128)(2,1)S(1)}, bf16[96,3584]{1,0:T(8,128)(2,1)S(1)}, u32[]{:S(2)}, u32[]{:S(2)}) collective-permute-start(bf16[96,3584]{1,0:T(8,128)(2,1)S(1)} %slice.74), channel_id=1, source_target_pairs={{0,1},{1,2},{2,3},{3,0},{4,5},{5,6},{6,7},{7,4},{8,9},{9,10},{10,1... | collective-permute-start | bytes 2064392 | tf_op jit(solution)/shard_map/ppermute | solution.py:317
  161.3 31.2 %collective-permute-start.15 = (bf16[96,3584]{1,0:T(8,128)(2,1)S(1)}, bf16[96,3584]{1,0:T(8,128)(2,1)S(1)}, u32[]{:S(2)}, u32[]{:S(2)}) collective-permute-start(bf16[96,3584]{1,0:T(8,128)(2,1)S(1)} %slice.75), channel_id=1, source_target_pairs={{0,3},{1,0},{2,1},{3,2},{4,7},{5,4},{6,5},{7,6},{8,11},{9,8},{10,9... | collective-permute-start | bytes 2064392 | tf_op jit(solution)/shard_map/ppermute | solution.py:317
  190.3 2.3 copy-start.4
  190.3 2.3 copy-start.11
  190.4 28.2 %collective-permute-start.3 = (bf16[96,3584]{1,0:T(8,128)(2,1)S(1)}, bf16[96,3584]{1,0:T(8,128)(2,1)S(1)}, u32[]{:S(2)}, u32[]{:S(2)}) collective-permute-start(bf16[96,3584]{1,0:T(8,128)(2,1)S(1)} %slice.72), channel_id=1, source_target_pairs={{0,1},{1,2},{2,3},{3,0},{4,5},{5,6},{6,7},{7,4},{8,9},{9,10},{10,1... | collective-permute-start | bytes 2064392 | tf_op jit(solution)/shard_map/ppermute | solution.py:317
  191.6 23.0 %copy-start.12 = (bf16[192,3584]{1,0:T(8,128)(2,1)}, bf16[192,3584]{1,0:T(8,128)(2,1)S(1)}, u32[]{:S(2)}) copy-start(bf16[192,3584]{1,0:T(8,128)(2,1)S(1)} %collective-permute-done.2.x2) | copy-start | bytes 4128772
  191.7 29.0 %collective-permute-start.4 = (bf16[96,3584]{1,0:T(8,128)(2,1)S(1)}, bf16[96,3584]{1,0:T(8,128)(2,1)S(1)}, u32[]{:S(2)}, u32[]{:S(2)}) collective-permute-start(bf16[96,3584]{1,0:T(8,128)(2,1)S(1)} %slice.73), channel_id=1, source_target_pairs={{0,3},{1,0},{2,1},{3,2},{4,7},{5,4},{6,5},{7,6},{8,11},{9,8},{10,9... | collective-permute-start | bytes 2064392 | tf_op jit(solution)/shard_map/ppermute | solution.py:317
  214.6 3.9 %copy-start.7 = (bf16[192,3584]{1,0:T(8,128)(2,1)S(1)}, bf16[192,3584]{1,0:T(8,128)(2,1)}, u32[]{:S(2)}) copy-start(bf16[192,3584]{1,0:T(8,128)(2,1)} %get-tuple-element.22) | copy-start | bytes 4128772
  214.6 36.8 %collective-permute-start.24 = (bf16[96,3584]{1,0:T(8,128)(2,1)S(1)}, bf16[96,3584]{1,0:T(8,128)(2,1)S(1)}, u32[]{:S(2)}, u32[]{:S(2)}) collective-permute-start(bf16[96,3584]{1,0:T(8,128)(2,1)S(1)} %get-tuple-element.25), channel_id=1, source_target_pairs={{0,3},{1,0},{2,1},{3,2},{4,7},{5,4},{6,5},{7,6},{8,11},{9,8},{10,9... | collective-permute-start | bytes 2064392 | tf_op jit(solution)/shard_map/ppermute | solution.py:317
  215.3 39.6 %collective-permute-start.20 = (bf16[96,3584]{1,0:T(8,128)(2,1)S(1)}, bf16[96,3584]{1,0:T(8,128)(2,1)S(1)}, u32[]{:S(2)}, u32[]{:S(2)}) collective-permute-start(bf16[96,3584]{1,0:T(8,128)(2,1)S(1)} %get-tuple-element.23), channel_id=1, source_target_pairs={{0,1},{1,2},{2,3},{3,0},{4,5},{5,6},{6,7},{7,4},{8,9},{9,10},{10,1... | collective-permute-start | bytes 2064392 | tf_op jit(solution)/shard_map/ppermute | solution.py:317
  218.0 54.8 %collective-permute-start.22 = (bf16[96,3584]{1,0:T(8,128)(2,1)S(1)}, bf16[96,3584]{1,0:T(8,128)(2,1)S(1)}, u32[]{:S(2)}, u32[]{:S(2)}) collective-permute-start(bf16[96,3584]{1,0:T(8,128)(2,1)S(1)} %slice.68), channel_id=1, source_target_pairs={{0,3},{1,0},{2,1},{3,2},{4,7},{5,4},{6,5},{7,6},{8,11},{9,8},{10,9... | collective-permute-start | bytes 2064392 | tf_op jit(solution)/shard_map/ppermute | solution.py:317
  218.6 57.5 %collective-permute-start.23 = (bf16[96,3584]{1,0:T(8,128)(2,1)S(1)}, bf16[96,3584]{1,0:T(8,128)(2,1)S(1)}, u32[]{:S(2)}, u32[]{:S(2)}) collective-permute-start(bf16[96,3584]{1,0:T(8,128)(2,1)S(1)} %slice.70), channel_id=1, source_target_pairs={{0,1},{1,2},{2,3},{3,0},{4,5},{5,6},{6,7},{7,4},{8,9},{9,10},{10,1... | collective-permute-start | bytes 2064392 | tf_op jit(solution)/shard_map/ppermute | solution.py:317
  247.9 3.6 %copy-start = (bf16[192,3584]{1,0:T(8,128)(2,1)}, bf16[192,3584]{1,0:T(8,128)(2,1)S(1)}, u32[]{:S(2)}) copy-start(bf16[192,3584]{1,0:T(8,128)(2,1)S(1)} %get-tuple-element.14) | copy-start | bytes 4128772
  247.9 2.6 copy-start.9
  247.9 19.6 %collective-permute-start.9 = (bf16[96,3584]{1,0:T(8,128)(2,1)S(1)}, bf16[96,3584]{1,0:T(8,128)(2,1)S(1)}, u32[]{:S(2)}, u32[]{:S(2)}) collective-permute-start(bf16[96,3584]{1,0:T(8,128)(2,1)S(1)} %get-tuple-element.18), channel_id=1, source_target_pairs={{0,3},{1,0},{2,1},{3,2},{4,7},{5,4},{6,5},{7,6},{8,11},{9,8},{10,9... | collective-permute-start | bytes 2064392 | tf_op jit(solution)/shard_map/ppermute | solution.py:317
  248.0 6.7 %copy-start.8 = (bf16[192,3584]{1,0:T(8,128)(2,1)S(1)}, bf16[192,3584]{1,0:T(8,128)(2,1)}, u32[]{:S(2)}) copy-start(bf16[192,3584]{1,0:T(8,128)(2,1)} %get-tuple-element.24) | copy-start | bytes 4128772
  251.4 17.2 %collective-permute-start.5 = (bf16[96,3584]{1,0:T(8,128)(2,1)S(1)}, bf16[96,3584]{1,0:T(8,128)(2,1)S(1)}, u32[]{:S(2)}, u32[]{:S(2)}) collective-permute-start(bf16[96,3584]{1,0:T(8,128)(2,1)S(1)} %get-tuple-element.16), channel_id=1, source_target_pairs={{0,1},{1,2},{2,3},{3,0},{4,5},{5,6},{6,7},{7,4},{8,9},{9,10},{10,1... | collective-permute-start | bytes 2064392 | tf_op jit(solution)/shard_map/ppermute | solution.py:317
  254.8 12.7 %copy-start.10 = (bf16[192,3584]{1,0:T(8,128)(2,1)S(1)}, bf16[192,3584]{1,0:T(8,128)(2,1)}, u32[]{:S(2)}) copy-start(bf16[192,3584]{1,0:T(8,128)(2,1)} %get-tuple-element.17) | copy-start | bytes 4128772
  254.8 53.1 %collective-permute-start.7 = (bf16[96,3584]{1,0:T(8,128)(2,1)}, bf16[96,3584]{1,0:T(8,128)(2,1)}, u32[]{:S(2)}, u32[]{:S(2)}) collective-permute-start(bf16[96,3584]{1,0:T(8,128)(2,1)} %slice.58), channel_id=1, source_target_pairs={{0,3},{1,0},{2,1},{3,2},{4,7},{5,4},{6,5},{7,6},{8,11},{9,8},{10,9... | collective-permute-start | bytes 2064392 | tf_op jit(solution)/shard_map/ppermute | solution.py:317
  267.5 29.2 %collective-permute-start.25 = (bf16[96,3584]{1,0:T(8,128)(2,1)S(1)}, bf16[96,3584]{1,0:T(8,128)(2,1)S(1)}, u32[]{:S(2)}, u32[]{:S(2)}) collective-permute-start(bf16[96,3584]{1,0:T(8,128)(2,1)S(1)} %add_convert_fusion.1), channel_id=1, source_target_pairs={{0,3},{1,0},{2,1},{3,2},{4,7},{5,4},{6,5},{7,6},{8,11},{9,8},{10,9... | collective-permute-start | bytes 2064392 | tf_op jit(solution)/shard_map/ppermute | solution.py:317
  268.6 31.1 %copy-start.6 = (bf16[192,3584]{1,0:T(8,128)(2,1)S(1)}, bf16[192,3584]{1,0:T(8,128)(2,1)}, u32[]{:S(2)}) copy-start(bf16[192,3584]{1,0:T(8,128)(2,1)} %get-tuple-element.21) | copy-start | bytes 4128772
  268.6 31.1 %collective-permute-start.21 = (bf16[96,3584]{1,0:T(8,128)(2,1)S(1)}, bf16[96,3584]{1,0:T(8,128)(2,1)S(1)}, u32[]{:S(2)}, u32[]{:S(2)}) collective-permute-start(bf16[96,3584]{1,0:T(8,128)(2,1)S(1)} %add_convert_fusion.3), channel_id=1, source_target_pairs={{0,1},{1,2},{2,3},{3,0},{4,5},{5,6},{6,7},{7,4},{8,9},{9,10},{10,1... | collective-permute-start | bytes 2064392 | tf_op jit(solution)/shard_map/ppermute | solution.py:317
  272.9 35.1 %collective-permute-start.8 = (bf16[96,3584]{1,0:T(8,128)(2,1)}, bf16[96,3584]{1,0:T(8,128)(2,1)}, u32[]{:S(2)}, u32[]{:S(2)}) collective-permute-start(bf16[96,3584]{1,0:T(8,128)(2,1)} %slice.60), channel_id=1, source_target_pairs={{0,1},{1,2},{2,3},{3,0},{4,5},{5,6},{6,7},{7,4},{8,9},{9,10},{10,1... | collective-permute-start | bytes 2064392 | tf_op jit(solution)/shard_map/ppermute | solution.py:317
  276.1 31.9 %collective-permute-start.10 = (bf16[96,3584]{1,0:T(8,128)(2,1)}, bf16[96,3584]{1,0:T(8,128)(2,1)}, u32[]{:S(2)}, u32[]{:S(2)}) collective-permute-start(bf16[96,3584]{1,0:T(8,128)(2,1)} %add_convert_fusion.5), channel_id=1, source_target_pairs={{0,3},{1,0},{2,1},{3,2},{4,7},{5,4},{6,5},{7,6},{8,11},{9,8},{10,9... | collective-permute-start | bytes 2064392 | tf_op jit(solution)/shard_map/ppermute | solution.py:317
  296.8 11.7 %collective-permute-start.6 = (bf16[96,3584]{1,0:T(8,128)(2,1)}, bf16[96,3584]{1,0:T(8,128)(2,1)}, u32[]{:S(2)}, u32[]{:S(2)}) collective-permute-start(bf16[96,3584]{1,0:T(8,128)(2,1)} %add_convert_fusion.7), channel_id=1, source_target_pairs={{0,1},{1,2},{2,3},{3,0},{4,5},{5,6},{6,7},{7,4},{8,9},{9,10},{10,1... | collective-permute-start | bytes 2064392 | tf_op jit(solution)/shard_map/ppermute | solution.py:317
  301.5 27.9 %all-to-all-start.4 = ((bf16[8,24,3584]{2,1,0:T(8,128)(2,1)}), bf16[8,24,3584]{2,1,0:T(8,128)(2,1)S(1)}, u32[]{:S(2)}, u32[]{:S(2)}) async-start(bf16[8,24,3584]{2,1,0:T(8,128)(2,1)} %bitcast.46), calls=%async_computation.4 | async-start | bytes 2752512 | tf_op jit(solution)/shard_map/all_to_all | solution.py:321
  329.4 4.4 %copy-start.3 = (f32[1,2,128,1]{2,3,1,0:T(1,128)S(1)}, f32[1,2,128,1]{2,3,1,0:T(1,128)}, u32[]{:S(2)}) copy-start(f32[1,2,128,1]{2,3,1,0:T(1,128)} %param.14) | copy-start | bytes 3076
  329.4 19.2 %all-to-all-start.1 = ((bf16[8,24,3584]{2,1,0:T(8,128)(2,1)}), bf16[8,24,3584]{2,1,0:T(8,128)(2,1)}, u32[]{:S(2)}, u32[]{:S(2)}) async-start(bf16[8,24,3584]{2,1,0:T(8,128)(2,1)} %bitcast.47), calls=%async_computation.1 | async-start | bytes 2752512 | tf_op jit(solution)/shard_map/all_to_all | solution.py:321

commit v2 on v1

v2 whole, which is shorter than its diff:
```python
import functools

import jax
import jax.numpy as jnp
from jax import lax
from jax.experimental import pallas as pl
from jax.experimental.pallas import tpu as pltpu
from jax.sharding import Mesh, PartitionSpec as P

CAP = 12
EXPERTS = 8
RING = 4
TOK = 128
D = 7168
HALF = D // 2
FF = 256
MSG = 2 * CAP
ROWS = EXPERTS * MSG
TILE = 1792
STEPS = HALF // TILE
F32 = jnp.float32
BF16 = jnp.bfloat16
NT = (((1,), (1,)), ((), ()))
VMEM = 50 * 2**20
SPAN = 1000


def slot_and_half(r):
    half = ((r >= 8) & (r < 16)) | (r >= 20)
    slot = jnp.where(r < 16, r & 7, 8 + (r & 3))
    return slot, half


def kept_ranks(routes, caps_ref):
    experts = lax.broadcasted_iota(jnp.int32, (EXPERTS, TOK), 0)
    onehot = (routes == experts).astype(F32)
    before = lax.broadcasted_iota(jnp.int32, (TOK, TOK), 0) < lax.broadcasted_iota(jnp.int32, (TOK, TOK), 1)
    earlier = jnp.dot(onehot.astype(BF16), before.astype(F32).astype(BF16), preferred_element_type=F32)
    rank = jnp.sum(onehot * earlier, axis=0, keepdims=True).astype(jnp.int32)
    bound = jnp.zeros((1, TOK), jnp.int32)
    for e in range(EXPERTS):
        bound = jnp.where(routes == e, caps_ref[e], bound)
    return jnp.where(rank < bound, rank, 99)


def pick_kernel(sel_ref, caps_ref, routes_ref, lo_ref, hi_ref, *refs):
    outs, pick_ref = refs[:-1], refs[-1]
    i = pl.program_id(0)

    @pl.when(i == 0)
    def _():
        routes = routes_ref[0]
        rank = kept_ranks(routes, caps_ref)
        shape = (EXPERTS, MSG, TOK)
        expert = lax.broadcasted_iota(jnp.int32, shape, 0)
        slot, half = slot_and_half(lax.broadcasted_iota(jnp.int32, shape, 1))
        hit = (routes[None] == expert) & (rank[None] == slot)
        lo = jnp.where(hit & ~half, 1.0, 0.0).reshape(ROWS, TOK)
        hi = jnp.where(hit & half, 1.0, 0.0).reshape(ROWS, TOK)
        pick_ref[...] = jnp.concatenate([lo, hi], axis=1).astype(BF16)

    rows = jnp.concatenate([lo_ref[0], hi_ref[0]], axis=0)
    tile = jnp.dot(pick_ref[...], rows, preferred_element_type=F32).astype(BF16)
    if len(outs) == 1:
        outs[0][...] = tile
    else:
        for n, out in enumerate(outs):

            @pl.when(i == n)
            def _():
                out[...] = tile


def pick(micro, caps, routes, x, cut):
    own = x.shape[0] > 1
    if cut:
        shapes = [jax.ShapeDtypeStruct((ROWS, TILE), BF16)] * STEPS
        specs = [pl.BlockSpec((ROWS, TILE), lambda i, s, c: (0, 0))] * STEPS
    else:
        shapes = [jax.ShapeDtypeStruct((ROWS, HALF), BF16)]
        specs = [pl.BlockSpec((ROWS, TILE), lambda i, s, c: (0, i))]
    return pl.pallas_call(
        pick_kernel,
        out_shape=shapes + [jax.ShapeDtypeStruct((ROWS, 2 * TOK), BF16)],
        grid_spec=pltpu.PrefetchScalarGridSpec(
            num_scalar_prefetch=2,
            grid=(STEPS,),
            in_specs=[
                pl.BlockSpec((1, 1, TOK), lambda i, s, c: (s[0], 0, 0)),
                pl.BlockSpec((1, TOK, TILE), lambda i, s, c: (s[0] if own else 0, 0, i)),
                pl.BlockSpec((1, TOK, TILE), lambda i, s, c: (s[0] if own else 0, 0, i + STEPS)),
            ],
            out_specs=specs + [pl.BlockSpec((ROWS, 2 * TOK), lambda i, s, c: (0, 0))],
        ),
        compiler_params=pltpu.CompilerParams(vmem_limit_bytes=VMEM),
        cost_estimate=pl.CostEstimate(flops=SPAN * 2 * ROWS * 256 * HALF, bytes_accessed=2 * (TOK * D + ROWS * HALF), transcendentals=0),
        name="pick",
    )(micro, caps, routes, x, x)


def pick_again_kernel(pick_ref, lo_ref, hi_ref, out_ref):
    rows = jnp.concatenate([lo_ref[...], hi_ref[...]], axis=0)
    out_ref[...] = jnp.dot(pick_ref[...], rows, preferred_element_type=F32).astype(BF16)


def pick_again(picker, x):
    tile = HALF // 2
    return pl.pallas_call(
        pick_again_kernel,
        out_shape=jax.ShapeDtypeStruct((ROWS, HALF), BF16),
        grid=(2,),
        in_specs=[
            pl.BlockSpec((ROWS, 2 * TOK), lambda i: (0, 0)),
            pl.BlockSpec((TOK, tile), lambda i: (0, i)),
            pl.BlockSpec((TOK, tile), lambda i: (0, i + 2)),
        ],
        out_specs=pl.BlockSpec((ROWS, tile), lambda i: (0, i)),
        compiler_params=pltpu.CompilerParams(vmem_limit_bytes=VMEM),
        cost_estimate=pl.CostEstimate(flops=SPAN * 2 * ROWS * 256 * HALF, bytes_accessed=2 * (TOK * D + ROWS * HALF), transcendentals=0),
        name="pick_again",
    )(picker, x, x)


TOTAL = RING * ROWS
PACK = TOTAL // MSG * 16
RECEIVED = (ROWS, ROWS, ROWS, ROWS // 2, ROWS // 2)


def unpack_rows(refs):
    if len(refs) == 1:
        refs = [refs[0][:, p * MSG : p * MSG + MSG].astype(F32).reshape(ROWS, -1) for p in range(RING)]
    else:
        refs = [r[...].astype(F32) for r in refs]
    x = jnp.concatenate(refs, axis=0)
    x = x.reshape(TOTAL // MSG, 3, 8, x.shape[1])
    lo = jnp.concatenate([x[:, 0:1], x[:, 2:3]], axis=1).reshape(PACK, x.shape[3])
    hi = jnp.concatenate([x[:, 1:2], x[:, 2:3]], axis=1).reshape(PACK, x.shape[3])
    return lo.astype(BF16), hi.astype(BF16)


def pack_rows(lo, hi, outs):
    n = lo.shape[1]
    lo = lo.reshape(TOTAL // MSG, 2, 8, n)
    hi = hi.reshape(TOTAL // MSG, 2, 8, n)
    upper = lax.broadcasted_iota(jnp.int32, (TOTAL // MSG, 1, 8, n), 2) < 4
    last = jnp.where(upper, lo[:, 1:2], hi[:, 1:2])
    tile = jnp.concatenate([lo[:, 0:1], hi[:, 0:1], last], axis=1).reshape(TOTAL, n).astype(BF16)
    if len(outs) == 1:
        for p in range(RING):
            outs[0][:, p * MSG : p * MSG + MSG] = tile[p * ROWS : p * ROWS + ROWS].reshape(EXPERTS, MSG, n)
        return
    at = 0
    for o in outs:
        o[...] = tile[at : at + o.shape[0]]
        at += o.shape[0]


def both_halves(lo, hi):
    lo = lo.reshape(TOTAL // MSG, 2, 8, FF)
    hi = hi.reshape(TOTAL // MSG, 2, 8, FF)
    upper = lax.broadcasted_iota(jnp.int32, (TOTAL // MSG, 8, FF), 1) < 4
    last = jnp.where(upper, lo[:, 1], hi[:, 1])
    last = last + jnp.concatenate([last[:, 4:], last[:, :4]], axis=1)
    return jnp.concatenate([(lo[:, 0] + hi[:, 0])[:, None], last[:, None]], axis=1).reshape(PACK, FF)


def accumulate(i, acc, parts):
    @pl.when(i == 0)
    def _():
        for n, part in enumerate(parts):
            acc[n] = part

    @pl.when(i > 0)
    def _():
        for n, part in enumerate(parts):
            acc[n] += part


def gate_up_step(i, rows, g_lo, g_hi, u_lo, u_hi, acc):
    lo, hi = rows
    dot = lambda x, w: jnp.dot(x, w[...], preferred_element_type=F32)
    accumulate(i, acc, (dot(lo, g_lo), dot(hi, g_hi), dot(lo, u_lo), dot(hi, u_hi)))


def gate_up(acc):
    return both_halves(acc[0], acc[1]), both_halves(acc[2], acc[3])


def saved_kernel(*refs):
    xs, (g_lo, g_hi, u_lo, u_hi, gate_ref, up_ref, acc) = refs[:-7], refs[-7:]
    i = pl.program_id(0)
    for n in range(STEPS):

        @pl.when(i == n)
        def _():
            gate_up_step(i, unpack_rows(xs[:1] if n == 0 else xs[1:]), g_lo, g_hi, u_lo, u_hi, acc)

    @pl.when(i == STEPS - 1)
    def _():
        gate, up = gate_up(acc)
        gate_ref[...] = gate
        up_ref[...] = up


def row_specs(pieces):
    return [pl.BlockSpec((n, TILE), lambda i: (0, jnp.minimum(i, STEPS - 1))) for n in pieces]


def saved_side(xs, gate_w, up_w):
    w = [pl.BlockSpec((TILE, FF), lambda i, k=k: (i + k * STEPS, 0)) for k in (0, 1, 0, 1)]
    return pl.pallas_call(
        saved_kernel,
        out_shape=(jax.ShapeDtypeStruct((PACK, FF), F32),) * 2,
        grid=(STEPS,),
        in_specs=[pl.BlockSpec(x.shape, lambda i, n=x.ndim: (0,) * n) for x in xs] + w,
        out_specs=(pl.BlockSpec((PACK, FF), lambda i: (0, 0)),) * 2,
        scratch_shapes=[pltpu.VMEM((4, PACK, FF), F32)],
        compiler_params=pltpu.CompilerParams(vmem_limit_bytes=VMEM),
        cost_estimate=pl.CostEstimate(
            flops=SPAN * 8 * PACK * HALF * FF, bytes_accessed=2 * (TOTAL * HALF + 2 * D * FF), transcendentals=0
        ),
        name="saved_side",
    )(*xs, gate_w, gate_w, up_w, up_w)


def forward_kernel(x0, x1, x2, x3, x4, g_lo, g_hi, u_lo, u_hi, w_lo, w_hi, o0, o1, o2, o3, o4, acc, mid):
    i = pl.program_id(0)

    @pl.when(i < STEPS)
    def _():
        gate_up_step(i, unpack_rows((x0, x1, x2, x3, x4)), g_lo, g_hi, u_lo, u_hi, acc)

    @pl.when(i == STEPS - 1)
    def _():
        gate, up = gate_up(acc)
        mid[...] = (gate / (1.0 + jnp.exp(-gate)) * up).astype(BF16)

    @pl.when(i >= STEPS)
    def _():
        lo = jnp.dot(mid[...], w_lo[...], preferred_element_type=F32)
        hi = jnp.dot(mid[...], w_hi[...], preferred_element_type=F32)
        pack_rows(lo, hi, (o0, o1, o2, o3, o4))


def forward_side(xs, gate_w, up_w, down_w):
    first = lambda i: jnp.minimum(i, STEPS - 1)
    second = lambda i: jnp.maximum(i - STEPS, 0)
    w = [pl.BlockSpec((TILE, FF), lambda i, k=k: (first(i) + k * STEPS, 0)) for k in (0, 1, 0, 1)]
    w += [pl.BlockSpec((FF, TILE), lambda i, k=k: (0, second(i) + k * STEPS)) for k in (0, 1)]
    return pl.pallas_call(
        forward_kernel,
        out_shape=tuple(jax.ShapeDtypeStruct((n, HALF), BF16) for n in RECEIVED),
        grid=(2 * STEPS,),
        in_specs=row_specs(RECEIVED) + w,
        out_specs=tuple(pl.BlockSpec((n, TILE), lambda i: (0, second(i))) for n in RECEIVED),
        scratch_shapes=[pltpu.VMEM((4, PACK, FF), F32), pltpu.VMEM((PACK, FF), BF16)],
        compiler_params=pltpu.CompilerParams(vmem_limit_bytes=VMEM),
        cost_estimate=pl.CostEstimate(
            flops=SPAN * 12 * PACK * HALF * FF, bytes_accessed=2 * (2 * TOTAL * HALF + 3 * D * FF), transcendentals=PACK * FF
        ),
        name="forward_side",
    )(*xs, gate_w, gate_w, up_w, up_w, down_w, down_w)


def backward_kernel(x0, x1, x2, x3, x4, w_lo, w_hi, gate_ref, up_ref, g_lo, g_hi, u_lo, u_hi, *refs):
    outs, (acc, mid) = refs[:-2], refs[-2:]
    i = pl.program_id(0)
    dot = lambda x, w: lax.dot_general(x, w[...], NT, preferred_element_type=F32)

    @pl.when(i < STEPS)
    def _():
        lo, hi = unpack_rows((x0, x1, x2, x3, x4))
        accumulate(i, acc, (dot(lo, w_lo), dot(hi, w_hi)))

    @pl.when(i == STEPS - 1)
    def _():
        dh = both_halves(acc[0], acc[1])
        gate, up = gate_ref[...], up_ref[...]
        sg = 1.0 / (1.0 + jnp.exp(-gate))
        mid[0] = (dh * up * sg * (1.0 + gate * (1.0 - sg))).astype(BF16)
        mid[1] = (dh * gate * sg).astype(BF16)

    @pl.when(i >= STEPS)
    def _():
        lo = dot(mid[0], g_lo) + dot(mid[1], u_lo)
        hi = dot(mid[0], g_hi) + dot(mid[1], u_hi)
        for n in range(STEPS):

            @pl.when(i == STEPS + n)
            def _():
                pack_rows(lo, hi, outs[:5] if n == 0 else outs[5:])


def backward_side(xs, gate, up, gate_w, up_w, down_w):
    first = lambda i: jnp.minimum(i, STEPS - 1)
    second = lambda i: jnp.maximum(i - STEPS, 0)
    w = [pl.BlockSpec((FF, TILE), lambda i, k=k: (0, first(i) + k * STEPS)) for k in (0, 1)]
    w += [pl.BlockSpec((PACK, FF), lambda i: (0, 0))] * 2
    w += [pl.BlockSpec((TILE, FF), lambda i, k=k: (second(i) + k * STEPS, 0)) for k in (0, 1, 0, 1)]
    shapes = [(n, TILE) for n in RECEIVED] + [(EXPERTS, RING * MSG, TILE)]
    return pl.pallas_call(
        backward_kernel,
        out_shape=tuple(jax.ShapeDtypeStruct(n, BF16) for n in shapes),
        grid=(2 * STEPS,),
        in_specs=row_specs(RECEIVED) + w,
        out_specs=tuple(pl.BlockSpec(n, lambda i, k=len(n): (0,) * k) for n in shapes),
        scratch_shapes=[pltpu.VMEM((2, PACK, FF), F32), pltpu.VMEM((2, PACK, FF), BF16)],
        compiler_params=pltpu.CompilerParams(vmem_limit_bytes=VMEM),
        cost_estimate=pl.CostEstimate(
            flops=SPAN * 12 * PACK * HALF * FF, bytes_accessed=2 * (2 * TOTAL * HALF + 3 * D * FF), transcendentals=PACK * FF
        ),
        name="backward_side",
    )(*xs, down_w, down_w, gate, up, gate_w, gate_w, up_w, up_w)


def spread_kernel(sel_ref, caps_ref, routes_ref, probs_ref, spread_ref, prob_ref):
    routes = routes_ref[0]
    rank = kept_ranks(routes, caps_ref)
    eye = lax.broadcasted_iota(jnp.int32, (TOK, TOK), 0) == lax.broadcasted_iota(jnp.int32, (TOK, TOK), 1)
    column = lambda row: jnp.sum(jnp.where(eye, row, 0.0), axis=1, keepdims=True)
    route_col = column(routes.astype(F32)).astype(jnp.int32)
    rank_col = column(rank.astype(F32)).astype(jnp.int32)
    prob_ref[...] = jnp.broadcast_to(column(probs_ref[0]), (TOK, TOK))
    lane = lax.broadcasted_iota(jnp.int32, (TOK, ROWS), 1)
    expert = (lane * 2731) >> 16
    slot, half = slot_and_half(lane - expert * MSG)
    hit = (route_col == expert) & (rank_col == slot)
    spread_ref[0] = jnp.where(hit & ~half, 1.0, 0.0).astype(BF16)
    spread_ref[1] = jnp.where(hit & half, 1.0, 0.0).astype(BF16)


def spread(micro, caps, routes, probs):
    return pl.pallas_call(
        spread_kernel,
        out_shape=(jax.ShapeDtypeStruct((2, TOK, ROWS), BF16), jax.ShapeDtypeStruct((TOK, TOK), F32)),
        grid_spec=pltpu.PrefetchScalarGridSpec(
            num_scalar_prefetch=2,
            grid=(1,),
            in_specs=[pl.BlockSpec((1, 1, TOK), lambda i, s, c: (s[0], 0, 0))] * 2,
            out_specs=(
                pl.BlockSpec((2, TOK, ROWS), lambda i, s, c: (0, 0, 0)),
                pl.BlockSpec((TOK, TOK), lambda i, s, c: (0, 0)),
            ),
        ),
        name="spread",
    )(micro, caps, routes, probs)


def mix_kernel(count, spread_ref, prob_ref, x_ref, *refs):
    total = refs[0][...]
    if count > 1:
        total = sum(r[...].astype(F32) for r in refs[:count]).astype(BF16)
    found = jnp.dot(spread_ref[0], total, preferred_element_type=F32)
    refs[-1][...] = (x_ref[...].astype(F32) + prob_ref[:, :1] * found).astype(BF16)


def mix(plan, parts, x, first=0, into=None):
    tiles = parts[0].shape[1] // TILE
    into = () if into is None else (into,)
    return pl.pallas_call(
        functools.partial(mix_kernel, len(parts)),
        out_shape=jax.ShapeDtypeStruct((TOK, D), BF16),
        grid=(tiles, 2),
        in_specs=[
            pl.BlockSpec((1, TOK, ROWS), lambda n, h: (h, 0, 0)),
            pl.BlockSpec((TOK, TOK), lambda n, h: (0, 0)),
            pl.BlockSpec((TOK, TILE), lambda n, h: (0, h * STEPS + first + n)),
        ]
        + [pl.BlockSpec((ROWS, TILE), lambda n, h: (0, n)) for _ in parts]
        + [pl.BlockSpec(memory_space=pl.ANY) for _ in into],
        out_specs=pl.BlockSpec((TOK, TILE), lambda n, h: (0, h * STEPS + first + n)),
        input_output_aliases={3 + len(parts): 0} if into else {},
        compiler_params=pltpu.CompilerParams(vmem_limit_bytes=VMEM),
        cost_estimate=pl.CostEstimate(
            flops=SPAN * 4 * ROWS * TOK * TILE * tiles, bytes_accessed=2 * (4 * TOK + ROWS) * TILE * tiles, transcendentals=0
        ),
        name="mix",
    )(*plan, x, *parts, *into)


def shift(x, axis, by):
    n = lax.axis_size(axis)
    return lax.ppermute(x, axis, [(i, (i + by) % n) for i in range(n)])


def labelled(f):
    def call(name, *args):
        with jax.named_scope(name):
            return f(*args)

    return call


@labelled
def exchange(x):
    return lax.all_to_all(x, ("y", "xh"), 0, 0, tiled=True)


@labelled
def gather_ring(x, *first):
    left = shift(x, "z", 1)
    right = shift(x, "z", -1)
    if first:
        left, right, _ = lax.optimization_barrier((left, right, first))
    half = ROWS // 2
    return x, left, right, shift(left[:half], "z", 1), shift(right[half:], "z", -1)


def add(*terms):
    return sum(t.astype(F32) for t in terms).astype(BF16)


def after(x, *others):
    return lax.optimization_barrier((x, others))[0]


@labelled
def scatter_far(far_lo, far_hi):
    return shift(far_lo, "z", 1), shift(far_hi, "z", -1)


@labelled
def scatter_near(left, right, far):
    half = ROWS // 2
    right = jnp.concatenate([add(right[:half], far[0]), right[half:]], axis=0)
    left = jnp.concatenate([left[:half], add(left[half:], far[1])], axis=0)
    return shift(right, "z", 1), shift(left, "z", -1)


def body(
    fwd_boundary,
    grad_boundary,
    saved_inputs,
    routes,
    route_probs,
    capacity,
    roster,
    gate_weight,
    up_weight,
    down_weight,
):
    section = lax.axis_index("pipe")
    sections = lax.axis_size("pipe")
    after_ = (section + 1) % sections
    before = (section + sections - 1) % sections
    take = lambda stack, index: lax.dynamic_index_in_dim(stack, index, 0, keepdims=False)
    fwd_micro = roster[section, 0].reshape(1)
    bwd_micro = roster[section, 1].reshape(1)
    caps = capacity[0]
    route_rows = routes.reshape(2, 1, TOK)
    prob_rows = route_probs.reshape(2, 1, TOK)
    gate_w, up_w, down_w = gate_weight[0, 0], up_weight[0, 0], down_weight[0, 0]

    outgoing = take(fwd_boundary[0], roster[after_, 0])
    layer_input = shift(outgoing, "pipe", 1)
    saved_a, saved_b, bwd_pick = pick(after(bwd_micro, outgoing), caps, route_rows, saved_inputs[0], True)
    back_index, saved_a, saved_b = lax.optimization_barrier((roster[before, 1], saved_a, saved_b))
    returning = take(grad_boundary[0], back_index)
    grad_input = shift(returning, "pipe", -1)
    own, left, right, far_lo, far_hi = gather_ring("saved_ring_a", saved_a)
    plane_b = exchange("saved_plane_b", saved_b)
    fwd_rows, _ = pick(fwd_micro, caps, route_rows, after(layer_input, plane_b, left, right)[None], False)
    kept_b = gather_ring("saved_ring_b", plane_b)
    input_plane = exchange("input_plane", fwd_rows)
    grad_rows = pick_again(bwd_pick, after(grad_input, fwd_rows, kept_b[1], kept_b[2], far_lo, far_hi))
    grad_plane = exchange("grad_plane", grad_rows)
    wide = jnp.stack([own, left, right, jnp.concatenate([far_lo, far_hi], axis=0)]).reshape(RING, EXPERTS, MSG, TILE)
    wide = wide.transpose(1, 0, 2, 3).reshape(EXPERTS, RING * MSG, TILE)
    kept_a = exchange("saved_plane_a", after(wide, grad_plane))
    gate, up = saved_side((kept_a, *kept_b), gate_w, up_w)
    fwd = gather_ring("input_ring", input_plane, grad_plane)
    own, left, right, far_lo, far_hi = forward_side(fwd, gate_w, up_w, down_w)
    far = scatter_far("output_far", far_lo, far_hi)
    grad = gather_ring("grad_ring", grad_plane, own, gate)
    gate = after(gate, *far)
    parts = backward_side(grad, gate, up, gate_w, up_w, down_w)
    near = scatter_near("output_near", left, right, far)
    far_a = scatter_far("back_far_a", *parts[3:5])
    planes = exchange("back_plane_b", parts[5]).reshape(EXPERTS, RING, MSG, TILE)
    fwd_total = exchange("output_plane", after(add(own, *near), planes))
    near_a = scatter_near("back_near_a", *parts[1:3], far_a)
    own, left, right, far = (planes[:, p].reshape(ROWS, TILE) for p in range(RING))
    far_b = scatter_far("back_far_b", far[: ROWS // 2], far[ROWS // 2 :])
    near_b = scatter_near("back_near_b", left, right, far_b)
    total_a = exchange("back_plane_a", after(add(parts[0], *near_a), fwd_total))

    fwd_plan = spread(fwd_micro, caps, route_rows, prob_rows)
    bwd_plan = spread(bwd_micro, caps, route_rows, prob_rows)
    new_output = mix(fwd_plan, (fwd_total,), layer_input)
    new_grad = mix(bwd_plan, (total_a,), grad_input)
    new_grad = mix(bwd_plan, (own, *near_b), grad_input, 1, new_grad)
    return new_output[None], new_grad[None]


def solution(mesh):
    grid = Mesh(mesh.devices.reshape(4, 4, 2, 4), ("pipe", "y", "xh", "z"))
    expert = ("y", "xh", "z")
    rows = P("pipe", None, expert, None)
    weight = P("pipe", expert, None, None)
    in_specs = (rows,) * 5 + (P("pipe", None), P()) + (weight,) * 3
    out_specs = (P("pipe", expert, None),) * 2
    return jax.shard_map(body, mesh=grid, in_specs=in_specs, out_specs=out_specs, check_vma=False)
```

time: 356 us -> 323 us (0.907)
  the two profiles are of different devices: /device:TPU:64 before, /device:TPU:18 now
where the time goes in v2:
time: 323 us; the launch traced here: 318 us
  waiting for transfers between devices  99.8 us (31%)
  starting transfers between devices  85 us (26%)
  Pallas kernels  59 us (18%)
  local copies, waits for them, and re-layouts  26.7 us (8%)
  blocking collectives  22.2 us (7%)
  other arithmetic  20.4 us (6%)
  between operations  4.93 us (2%)
    ppermute x30, waiting for transfers between devices, shift(): return lax.ppermute(x, axis, [(i, (i + by) % n) for i in range(n)])  71.6 us
    all_to_all x6, starting transfers between devices, exchange(): return lax.all_to_all(x, ('y', 'xh'), 0, 0, tiled=True)  45.6 us
    ppermute x30, starting transfers between devices, shift(): return lax.ppermute(x, axis, [(i, (i + by) % n) for i in range(n)])  39.3 us
    all_to_all x6, waiting for transfers between devices, exchange(): return lax.all_to_all(x, ('y', 'xh'), 0, 0, tiled=True)  28.2 us
    all_to_all x1, blocking collectives, exchange(): return lax.all_to_all(x, ('y', 'xh'), 0, 0, tiled=True)  22.2 us
    pallas_call x1, Pallas kernels, backward_side(): pl.pallas_call(backward_kernel, out_shape=tuple((jax.ShapeDtypeStruct(n,...  13 us
    pallas_call x1, Pallas kernels, forward_side(): pl.pallas_call(forward_kernel, out_shape=tuple((jax.ShapeDtypeStruct((n,...  12.1 us
    convert_element_type x8, other arithmetic, add(): return sum((t.astype(F32) for t in terms)).astype(BF16)  11.5 us
  transfers between devices with their start and end apart: 36, of which 18 were waited for; matrix products, arithmetic and copies ran while one was open for 12% of the time, Pallas kernels for 18%

profile of v2, /device:TPU:18, one launch (start us, length us, event | category | flops | bytes accessed | tf_op | source)
XLA Modules:
  0.0 317.9 jit_solution(8936350585311759703)
XLA Ops:
  4.1 2.9 dynamic-slice_bitcast_fusion.1
  7.0 4.2 %pick.2 = (bf16[192,1792]{1,0:T(8,128)(2,1)S(1)}, bf16[192,1792]{1,0:T(8,128)(2,1)}, bf16[192,256]{1,0:T(8,128)(2,1)S(1)}) custom-call(s32[1]{0:T(128)} %bitcast.7.sel_ref, s32[8]{0:T(128)S(1)} %bitcast.82, s32[2,1,128]{2,1,0:T(1,128)S(1)} %bitcast.78, bf16[2,128,7168]{2,1,0:T(8,128)(2,1)} %bitcast.93, bf16[2,128,7168]{2,1,0:T(8,128)(2,1)} %bitcast.94), custom_call_target="tpu_custom_call" | custom-call | flops 352321536000 | bytes 3211264 | tf_op jit(solution)/shard_map/pick/pallas_call | solution.py:82
  11.2 4.0 %collective-permute-start.2 = (bf16[192,1792]{1,0:T(8,128)(2,1)S(1)}, bf16[192,1792]{1,0:T(8,128)(2,1)S(1)}, u32[]{:S(2)}, u32[]{:S(2)}) collective-permute-start(bf16[192,1792]{1,0:T(8,128)(2,1)S(1)} %get-tuple-element.43), channel_id=1, source_target_pairs={{0,3},{1,0},{2,1},{3,2},{4,7},{5,4},{6,5},{7,6},{8,11},{9,8},{10,9... | collective-permute-start | bytes 2064392 | tf_op jit(solution)/shard_map/saved_ring_a/ppermute | solution.py:383
  15.2 6.4 %all-to-all-start = ((bf16[8,24,1792]{2,1,0:T(8,128)(2,1)}), bf16[8,24,1792]{2,1,0:T(8,128)(2,1)S(1)}, u32[]{:S(2)}, u32[]{:S(2)}) async-start(bf16[8,24,1792]{2,1,0:T(8,128)(2,1)} %bitcast.9), calls=%async_computation | async-start | bytes 1376256 | tf_op jit(solution)/shard_map/saved_plane_b/all_to_all | solution.py:396
  23.6 2.8 dynamic-slice_bitcast_fusion
  27.9 5.9 %all-to-all-done = bf16[8,24,1792]{2,1,0:T(8,128)(2,1)S(1)} async-done(((bf16[8,24,1792]{2,1,0:T(8,128)(2,1)}), bf16[8,24,1792]{2,1,0:T(8,128)(2,1)S(1)}, u32[]{:S(2)}, u32[]{:S(2)}) %all-to-all-start) | async-done | bytes 688160 | tf_op jit(solution)/shard_map/saved_plane_b/all_to_all | solution.py:396
  34.9 4.1 %pick.3 = (bf16[192,3584]{1,0:T(8,128)(2,1)}, bf16[192,256]{1,0:T(8,128)(2,1)}) custom-call(s32[1]{0:T(128)} %bitcast.sel_ref, s32[8]{0:T(128)S(1)} %bitcast.83, s32[2,1,128]{2,1,0:T(1,128)S(1)} %bitcast.79, bf16[1,128,7168]{2,1,0:T(8,128)(2,1)} %bitcast.11.lo_ref.hi_ref, bf16[1,128,7168]{2,1,0:T(8,128)(2,1)} %bitcast.11.lo_ref.hi_ref), custom_call_target="tpu_custom_call" | custom-call | flops 352321536000 | bytes 3211264 | tf_op jit(solution)/shard_map/pick/pallas_call | solution.py:82
  39.1 6.3 %all-to-all-start.1 = ((bf16[8,24,3584]{2,1,0:T(8,128)(2,1)}), bf16[8,24,3584]{2,1,0:T(8,128)(2,1)}, u32[]{:S(2)}, u32[]{:S(2)}) async-start(bf16[8,24,3584]{2,1,0:T(8,128)(2,1)} %bitcast.12), calls=%async_computation.1 | async-start | bytes 2752512 | tf_op jit(solution)/shard_map/input_plane/all_to_all | solution.py:396
  45.4 4.8 %collective-permute-start.7 = (bf16[192,1792]{1,0:T(8,128)(2,1)S(1)}, bf16[192,1792]{1,0:T(8,128)(2,1)S(1)}, u32[]{:S(2)}, u32[]{:S(2)}) collective-permute-start(bf16[192,1792]{1,0:T(8,128)(2,1)S(1)} %bitcast.71), channel_id=1, source_target_pairs={{0,3},{1,0},{2,1},{3,2},{4,7},{5,4},{6,5},{7,6},{8,11},{9,8},{10,9... | collective-permute-start | bytes 2064392 | tf_op jit(solution)/shard_map/saved_ring_b/ppermute | solution.py:383
  50.2 3.3 %collective-permute-start.9 = (bf16[96,1792]{1,0:T(8,128)(2,1)S(1)}, bf16[96,1792]{1,0:T(8,128)(2,1)S(1)}, u32[]{:S(2)}, u32[]{:S(2)}) collective-permute-start(bf16[96,1792]{1,0:T(8,128)(2,1)S(1)} %slice.120), channel_id=1, source_target_pairs={{0,3},{1,0},{2,1},{3,2},{4,7},{5,4},{6,5},{7,6},{8,11},{9,8},{10,9... | collective-permute-start | bytes 1032200 | tf_op jit(solution)/shard_map/saved_ring_a/ppermute | solution.py:383
  53.6 12.6 %collective-permute-done.9 = bf16[96,1792]{1,0:T(8,128)(2,1)S(1)} collective-permute-done((bf16[96,1792]{1,0:T(8,128)(2,1)S(1)}, bf16[96,1792]{1,0:T(8,128)(2,1)S(1)}, u32[]{:S(2)}, u32[]{:S(2)}) %collective-permute-start.9) | collective-permute-done | bytes 344096 | tf_op jit(solution)/shard_map/saved_ring_a/ppermute | solution.py:383
  66.2 4.0 %collective-permute-done.8 = bf16[96,1792]{1,0:T(8,128)(2,1)S(1)} collective-permute-done((bf16[96,1792]{1,0:T(8,128)(2,1)S(1)}, bf16[96,1792]{1,0:T(8,128)(2,1)S(1)}, u32[]{:S(2)}, u32[]{:S(2)}) %collective-permute-start.8) | collective-permute-done | bytes 344096 | tf_op jit(solution)/shard_map/saved_ring_a/ppermute | solution.py:383
  72.5 3.4 %collective-permute-start.4 = (bf16[192,3584]{1,0:T(8,128)(2,1)}, bf16[192,3584]{1,0:T(8,128)(2,1)}, u32[]{:S(2)}, u32[]{:S(2)}) collective-permute-start(bf16[192,3584]{1,0:T(8,128)(2,1)} %bitcast.13.x0), channel_id=1, source_target_pairs={{0,3},{1,0},{2,1},{3,2},{4,7},{5,4},{6,5},{7,6},{8,11},{9,8},{10,9... | collective-permute-start | bytes 4128776 | tf_op jit(solution)/shard_map/input_ring/ppermute | solution.py:383
  77.9 22.2 %all_to_all.65 = bf16[8,24,3584]{2,1,0:T(8,128)(2,1)} all-to-all(bf16[8,24,3584]{2,1,0:T(8,128)(2,1)S(1)} %bitcast.70), channel_id=1, replica_groups=mesh['pipe'=4,'y'=4,'xh'=2,'z'=4] {'y','xh'}, dimensions={0} | all-to-all | bytes 2752512 | tf_op jit(solution)/shard_map/grad_plane/all_to_all | solution.py:396
  100.1 4.3 %collective-permute-done.4.x2 = bf16[192,3584]{1,0:T(8,128)(2,1)} collective-permute-done((bf16[192,3584]{1,0:T(8,128)(2,1)}, bf16[192,3584]{1,0:T(8,128)(2,1)}, u32[]{:S(2)}, u32[]{:S(2)}) %collective-permute-start.4) | collective-permute-done | bytes 1376288 | tf_op jit(solution)/shard_map/input_ring/ppermute | solution.py:383
  104.4 4.0 %collective-permute-done.3.x1 = bf16[192,3584]{1,0:T(8,128)(2,1)} collective-permute-done((bf16[192,3584]{1,0:T(8,128)(2,1)}, bf16[192,3584]{1,0:T(8,128)(2,1)}, u32[]{:S(2)}, u32[]{:S(2)}) %collective-permute-start.3) | collective-permute-done | bytes 1376288 | tf_op jit(solution)/shard_map/input_ring/ppermute | solution.py:383
  110.4 2.1 slice.94
  114.4 2.9 spread.3
  117.3 2.9 spread.2
  126.7 2.6 collective-permute-start.17
  129.3 9.2 %all-to-all-start.3 = ((bf16[8,96,1792]{2,1,0:T(8,128)(2,1)}), bf16[8,96,1792]{2,1,0:T(8,128)(2,1)}, u32[]{:S(2)}, u32[]{:S(2)}) async-start(bf16[8,96,1792]{2,1,0:T(8,128)(2,1)} %bitcast.84), calls=%async_computation.3 | async-start | bytes 5505024 | tf_op jit(solution)/shard_map/saved_plane_a/all_to_all | solution.py:396
  138.5 12.1 %forward_side.1 = (bf16[192,3584]{1,0:T(8,128)(2,1)S(1)}, bf16[192,3584]{1,0:T(8,128)(2,1)}, bf16[192,3584]{1,0:T(8,128)(2,1)}, bf16[96,3584]{1,0:T(8,128)(2,1)}, bf16[96,3584]{1,0:T(8,128)(2,1)}) custom-call(bf16[192,3584]{1,0:T(8,128)(2,1)} %bitcast.13.x0, bf16[192,3584]{1,0:T(8,128)(2,1)} %collective-permute-done.3.x1, ...), custom_call_target="tpu_custom_call" | custom-call | flops 5637144576000 | bytes 22020096 | tf_op jit(solution)/shard_map/forward_side/pallas_call | solution.py:250
  150.5 2.2 slice.97
  152.7 2.0 slice.98
  154.7 3.2 %collective-permute-start.14 = (bf16[96,3584]{1,0:T(8,128)(2,1)}, bf16[96,3584]{1,0:T(8,128)(2,1)}, u32[]{:S(2)}, u32[]{:S(2)}) collective-permute-start(bf16[96,3584]{1,0:T(8,128)(2,1)} %get-tuple-element.55), channel_id=1, source_target_pairs={{0,3},{1,0},{2,1},{3,2},{4,7},{5,4},{6,5},{7,6},{8,11},{9,8},{10,9... | collective-permute-start | bytes 2064392 | tf_op jit(solution)/shard_map/output_far/ppermute | solution.py:383
  158.0 12.2 %all-to-all-done.3.refs_0_ = bf16[8,96,1792]{2,1,0:T(8,128)(2,1)} async-done(((bf16[8,96,1792]{2,1,0:T(8,128)(2,1)}), bf16[8,96,1792]{2,1,0:T(8,128)(2,1)}, u32[]{:S(2)}, u32[]{:S(2)}) %all-to-all-start.3) | async-done | bytes 2752544 | tf_op jit(solution)/shard_map/saved_plane_a/all_to_all | solution.py:396
  170.2 7.8 %saved_side.1 = (f32[512,256]{1,0:T(8,128)S(1)}, f32[512,256]{1,0:T(8,128)S(1)}) custom-call(bf16[8,96,1792]{2,1,0:T(8,128)(2,1)} %all-to-all-done.3.refs_0_, bf16[192,1792]{1,0:T(8,128)(2,1)S(1)} %bitcast.73, bf16[192,1792]{1,0:T(8,128)(2,1)S(1)} %copy-done.10, bf16[192,1792]{1,0:T(8,128)(2,1)S(1)} %copy-done.7, ...), custom_call_target="tpu_custom_call" | custom-call | flops 3758096384000 | bytes 12845056 | tf_op jit(solution)/shard_map/saved_side/pallas_call | solution.py:211
  182.6 4.8 %collective-permute-done.12 = bf16[96,3584]{1,0:T(8,128)(2,1)} collective-permute-done((bf16[96,3584]{1,0:T(8,128)(2,1)}, bf16[96,3584]{1,0:T(8,128)(2,1)}, u32[]{:S(2)}, u32[]{:S(2)}) %collective-permute-start.12) | collective-permute-done | bytes 688160 | tf_op jit(solution)/shard_map/output_far/ppermute | solution.py:383
  190.6 2.1 add_convert_fusion.3
  192.7 6.3 %collective-permute-done.21.x4 = bf16[96,3584]{1,0:T(8,128)(2,1)S(1)} collective-permute-done((bf16[96,3584]{1,0:T(8,128)(2,1)S(1)}, bf16[96,3584]{1,0:T(8,128)(2,1)S(1)}, u32[]{:S(2)}, u32[]{:S(2)}) %collective-permute-start.21) | collective-permute-done | bytes 688160 | tf_op jit(solution)/shard_map/grad_ring/ppermute | solution.py:383
  200.4 13.0 %backward_side.1 = (bf16[192,1792]{1,0:T(8,128)(2,1)S(1)}, bf16[192,1792]{1,0:T(8,128)(2,1)S(1)}, bf16[192,1792]{1,0:T(8,128)(2,1)S(1)}, bf16[96,1792]{1,0:T(8,1...) custom-call(bf16[192,3584]{1,0:T(8,128)(2,1)} %bitcast.16.x0, ...), custom_call_target="tpu_custom_call" | custom-call | flops 5637144576000 | bytes 22020096 | tf_op jit(solution)/shard_map/backward_side/pallas_call | solution.py:301
  216.7 7.2 %all-to-all-start.4 = ((bf16[8,96,1792]{2,1,0:T(8,128)(2,1)}), bf16[8,96,1792]{2,1,0:T(8,128)(2,1)}, u32[]{:S(2)}, u32[]{:S(2)}) async-start(bf16[8,96,1792]{2,1,0:T(8,128)(2,1)} %get-tuple-element.62), calls=%async_computation.4 | async-start | bytes 5505024 | tf_op jit(solution)/shard_map/back_plane_b/all_to_all | solution.py:396
  224.0 8.3 %collective-permute-done.28 = bf16[96,1792]{1,0:T(8,128)(2,1)} collective-permute-done((bf16[96,1792]{1,0:T(8,128)(2,1)}, bf16[96,1792]{1,0:T(8,128)(2,1)}, u32[]{:S(2)}, u32[]{:S(2)}) %collective-permute-start.28) | collective-permute-done | bytes 344096 | tf_op jit(solution)/shard_map/back_far_a/ppermute | solution.py:383
  236.1 17.0 %collective-permute-done.26 = bf16[96,1792]{1,0:T(8,128)(2,1)S(1)} collective-permute-done((bf16[96,1792]{1,0:T(8,128)(2,1)}, bf16[96,1792]{1,0:T(8,128)(2,1)S(1)}, u32[]{:S(2)}, u32[]{:S(2)}) %collective-permute-start.26) | collective-permute-done | bytes 344096 | tf_op jit(solution)/shard_map/back_far_a/ppermute | solution.py:383
  254.6 3.3 %add_convert_fusion = bf16[192,3584]{1,0:T(8,128)(2,1)} fusion(bf16[192,3584]{1,0:T(8,128)(2,1)} %collective-permute-done.15, bf16[192,3584]{1,0:T(8,128)(2,1)} %collective-permute-done.13, bf16[192,3584]{1,0:T(8,128)(2,1)S(1)} %get-tuple-element.51), kind=kLoop, calls=%fused_computation.1 | loop fusion | flops 4128768 | bytes 5505024 | tf_op jit(solution)/shard_map/convert_element_type | solution.py:410
  257.9 2.5 fusion.2
  260.4 2.7 collective-permute-start.24
  263.1 5.3 %collective-permute-done.27 = bf16[192,1792]{1,0:T(8,128)(2,1)} collective-permute-done((bf16[192,1792]{1,0:T(8,128)(2,1)}, bf16[192,1792]{1,0:T(8,128)(2,1)}, u32[]{:S(2)}, u32[]{:S(2)}) %collective-permute-start.27) | collective-permute-done | bytes 688160 | tf_op jit(solution)/shard_map/back_near_a/ppermute | solution.py:383
  268.5 2.4 add_convert_fusion.1
  272.0 9.8 %all-to-all-start.5 = ((bf16[8,24,3584]{2,1,0:T(8,128)(2,1)}), bf16[8,24,3584]{2,1,0:T(8,128)(2,1)S(1)}, u32[]{:S(2)}, u32[]{:S(2)}) async-start(bf16[8,24,3584]{2,1,0:T(8,128)(2,1)} %bitcast.31), calls=%async_computation.5 | async-start | bytes 2752512 | tf_op jit(solution)/shard_map/output_plane/all_to_all | solution.py:396
  283.9 3.2 %collective-permute-start.25 = (bf16[192,1792]{1,0:T(8,128)(2,1)}, bf16[192,1792]{1,0:T(8,128)(2,1)}, u32[]{:S(2)}, u32[]{:S(2)}) collective-permute-start(bf16[192,1792]{1,0:T(8,128)(2,1)} %pad_maximum_fusion.5), channel_id=1, source_target_pairs={{0,3},{1,0},{2,1},{3,2},{4,7},{5,4},{6,5},{7,6},{8,11},{9,8},{10,9... | collective-permute-start | bytes 2064392 | tf_op jit(solution)/shard_map/back_near_b/ppermute | solution.py:383
  287.1 3.4 %collective-permute-done.22 = bf16[96,1792]{1,0:T(8,128)(2,1)S(1)} collective-permute-done((bf16[96,1792]{1,0:T(8,128)(2,1)}, bf16[96,1792]{1,0:T(8,128)(2,1)S(1)}, u32[]{:S(2)}, u32[]{:S(2)}) %collective-permute-start.22) | collective-permute-done | bytes 344096 | tf_op jit(solution)/shard_map/back_far_b/ppermute | solution.py:383
  291.5 5.4 %all-to-all-done.5 = bf16[8,24,3584]{2,1,0:T(8,128)(2,1)S(1)} async-done(((bf16[8,24,3584]{2,1,0:T(8,128)(2,1)}), bf16[8,24,3584]{2,1,0:T(8,128)(2,1)S(1)}, u32[]{:S(2)}, u32[]{:S(2)}) %all-to-all-start.5) | async-done | bytes 1376288 | tf_op jit(solution)/shard_map/output_plane/all_to_all | solution.py:396
  296.9 6.8 %all-to-all-start.6 = ((bf16[8,24,1792]{2,1,0:T(8,128)(2,1)}), bf16[8,24,1792]{2,1,0:T(8,128)(2,1)}, u32[]{:S(2)}, u32[]{:S(2)}) async-start(bf16[8,24,1792]{2,1,0:T(8,128)(2,1)} %bitcast.41), calls=%async_computation.6 | async-start | bytes 1376256 | tf_op jit(solution)/shard_map/back_plane_a/all_to_all | solution.py:396
  303.7 4.2 %mix.3 = bf16[128,7168]{1,0:T(8,128)(2,1)} custom-call(bf16[2,128,192]{2,1,0:T(8,128)(2,1)S(1)} %copy-done.15, f32[128,128]{1,0:T(8,128)S(1)} %copy-done.17, bf16[128,7168]{1,0:T(8,128)(2,1)} %collective-permute-done.x_ref, bf16[192,3584]{1,0:T(8,128)(2,1)S(1)} %bitcast.69), custom_call_target="tpu_custom_call" | custom-call | flops 352321536000 | bytes 5046272 | tf_op jit(solution)/shard_map/mix/pallas_call | solution.py:360
  307.9 4.2 %all-to-all-done.6 = bf16[8,24,1792]{2,1,0:T(8,128)(2,1)} async-done(((bf16[8,24,1792]{2,1,0:T(8,128)(2,1)}), bf16[8,24,1792]{2,1,0:T(8,128)(2,1)}, u32[]{:S(2)}, u32[]{:S(2)}) %all-to-all-start.6) | async-done | bytes 688160 | tf_op jit(solution)/shard_map/back_plane_a/all_to_all | solution.py:396
  312.2 2.6 mix.4.refs_3_
  314.8 3.1 mix.5
  (135 shorter events, 40.9 us)
Async XLA Ops:
  7.0 27.9 %collective-permute-start = (bf16[128,7168]{1,0:T(8,128)(2,1)}, bf16[128,7168]{1,0:T(8,128)(2,1)}, u32[]{:S(2)}, u32[]{:S(2)}) collective-permute-start(bf16[128,7168]{1,0:T(8,128)(2,1)} %dynamic-slice_bitcast_fusion.1), channel_id=1, source_target_pairs={{0,32},{32,64},{64,96},{96,0},{1,33},{33,65},{65,97},{97,1},{2,34}... | collective-permute-start | bytes 5505032 | tf_op jit(solution)/shard_map/ppermute | solution.py:383
  11.2 15.2 %copy-start.3 = (bf16[192,1792]{1,0:T(8,128)(2,1)}, bf16[192,1792]{1,0:T(8,128)(2,1)S(1)}, u32[]{:S(2)}) copy-start(bf16[192,1792]{1,0:T(8,128)(2,1)S(1)} %get-tuple-element.43) | copy-start | bytes 2064388
  11.2 22.6 %collective-permute-start.2 = (bf16[192,1792]{1,0:T(8,128)(2,1)S(1)}, bf16[192,1792]{1,0:T(8,128)(2,1)S(1)}, u32[]{:S(2)}, u32[]{:S(2)}) collective-permute-start(bf16[192,1792]{1,0:T(8,128)(2,1)S(1)} %get-tuple-element.43), channel_id=1, source_target_pairs={{0,3},{1,0},{2,1},{3,2},{4,7},{5,4},{6,5},{7,6},{8,11},{9,8},{10,9... | collective-permute-start | bytes 2064392 | tf_op jit(solution)/shard_map/saved_ring_a/ppermute | solution.py:383
  15.2 18.9 %collective-permute-start.1 = (bf16[192,1792]{1,0:T(8,128)(2,1)S(1)}, bf16[192,1792]{1,0:T(8,128)(2,1)S(1)}, u32[]{:S(2)}, u32[]{:S(2)}) collective-permute-start(bf16[192,1792]{1,0:T(8,128)(2,1)S(1)} %get-tuple-element.43), channel_id=1, source_target_pairs={{0,1},{1,2},{2,3},{3,0},{4,5},{5,6},{6,7},{7,4},{8,9},{9,10},{10,1... | collective-permute-start | bytes 2064392 | tf_op jit(solution)/shard_map/saved_ring_a/ppermute | solution.py:383
  15.2 18.5 %all-to-all-start = ((bf16[8,24,1792]{2,1,0:T(8,128)(2,1)}), bf16[8,24,1792]{2,1,0:T(8,128)(2,1)S(1)}, u32[]{:S(2)}, u32[]{:S(2)}) async-start(bf16[8,24,1792]{2,1,0:T(8,128)(2,1)} %bitcast.9), calls=%async_computation | async-start | bytes 1376256 | tf_op jit(solution)/shard_map/saved_plane_b/all_to_all | solution.py:396
  26.4 45.6 %collective-permute-start.5 = (bf16[128,7168]{1,0:T(8,128)(2,1)}, bf16[128,7168]{1,0:T(8,128)(2,1)}, u32[]{:S(2)}, u32[]{:S(2)}) collective-permute-start(bf16[128,7168]{1,0:T(8,128)(2,1)} %dynamic-slice_bitcast_fusion), channel_id=1, source_target_pairs={{0,96},{32,0},{64,32},{96,64},{1,97},{33,1},{65,33},{97,65},{2,98}... | collective-permute-start | bytes 5505032 | tf_op jit(solution)/shard_map/ppermute | solution.py:383
  39.1 11.1 %copy-start.22 = (bf16[192,1792]{1,0:T(8,128)(2,1)S(1)}, bf16[192,1792]{1,0:T(8,128)(2,1)}, u32[]{:S(2)}) copy-start(bf16[192,1792]{1,0:T(8,128)(2,1)} %copy-done.21) | copy-start | bytes 2064388
  39.1 14.5 %copy-start.25 = (bf16[192,1792]{1,0:T(8,128)(2,1)S(1)}, bf16[192,1792]{1,0:T(8,128)(2,1)}, u32[]{:S(2)}) copy-start(bf16[192,1792]{1,0:T(8,128)(2,1)} %copy-done.24) | copy-start | bytes 2064388
  39.1 33.4 %all-to-all-start.1 = ((bf16[8,24,3584]{2,1,0:T(8,128)(2,1)}), bf16[8,24,3584]{2,1,0:T(8,128)(2,1)}, u32[]{:S(2)}, u32[]{:S(2)}) async-start(bf16[8,24,3584]{2,1,0:T(8,128)(2,1)} %bitcast.12), calls=%async_computation.1 | async-start | bytes 2752512 | tf_op jit(solution)/shard_map/input_plane/all_to_all | solution.py:396
  45.4 24.8 %collective-permute-start.7 = (bf16[192,1792]{1,0:T(8,128)(2,1)S(1)}, bf16[192,1792]{1,0:T(8,128)(2,1)S(1)}, u32[]{:S(2)}, u32[]{:S(2)}) collective-permute-start(bf16[192,1792]{1,0:T(8,128)(2,1)S(1)} %bitcast.71), channel_id=1, source_target_pairs={{0,3},{1,0},{2,1},{3,2},{4,7},{5,4},{6,5},{7,6},{8,11},{9,8},{10,9... | collective-permute-start | bytes 2064392 | tf_op jit(solution)/shard_map/saved_ring_b/ppermute | solution.py:383
  50.2 20.0 %collective-permute-start.6 = (bf16[192,1792]{1,0:T(8,128)(2,1)S(1)}, bf16[192,1792]{1,0:T(8,128)(2,1)S(1)}, u32[]{:S(2)}, u32[]{:S(2)}) collective-permute-start(bf16[192,1792]{1,0:T(8,128)(2,1)S(1)} %bitcast.72), channel_id=1, source_target_pairs={{0,1},{1,2},{2,3},{3,0},{4,5},{5,6},{6,7},{7,4},{8,9},{9,10},{10,1... | collective-permute-start | bytes 2064392 | tf_op jit(solution)/shard_map/saved_ring_b/ppermute | solution.py:383
  50.2 16.0 %collective-permute-start.9 = (bf16[96,1792]{1,0:T(8,128)(2,1)S(1)}, bf16[96,1792]{1,0:T(8,128)(2,1)S(1)}, u32[]{:S(2)}, u32[]{:S(2)}) collective-permute-start(bf16[96,1792]{1,0:T(8,128)(2,1)S(1)} %slice.120), channel_id=1, source_target_pairs={{0,3},{1,0},{2,1},{3,2},{4,7},{5,4},{6,5},{7,6},{8,11},{9,8},{10,9... | collective-permute-start | bytes 1032200 | tf_op jit(solution)/shard_map/saved_ring_a/ppermute | solution.py:383
  53.6 16.6 %collective-permute-start.8 = (bf16[96,1792]{1,0:T(8,128)(2,1)S(1)}, bf16[96,1792]{1,0:T(8,128)(2,1)S(1)}, u32[]{:S(2)}, u32[]{:S(2)}) collective-permute-start(bf16[96,1792]{1,0:T(8,128)(2,1)S(1)} %slice.119), channel_id=1, source_target_pairs={{0,1},{1,2},{2,3},{3,0},{4,5},{5,6},{6,7},{7,4},{8,9},{9,10},{10,1... | collective-permute-start | bytes 1032200 | tf_op jit(solution)/shard_map/saved_ring_a/ppermute | solution.py:383
  66.2 11.7 %copy-start.29 = (bf16[96,1792]{1,0:T(8,128)(2,1)}, bf16[96,1792]{1,0:T(8,128)(2,1)S(1)}, u32[]{:S(2)}) copy-start(bf16[96,1792]{1,0:T(8,128)(2,1)S(1)} %collective-permute-done.9) | copy-start | bytes 1032196
  72.5 31.9 %collective-permute-start.4 = (bf16[192,3584]{1,0:T(8,128)(2,1)}, bf16[192,3584]{1,0:T(8,128)(2,1)}, u32[]{:S(2)}, u32[]{:S(2)}) collective-permute-start(bf16[192,3584]{1,0:T(8,128)(2,1)} %bitcast.13.x0), channel_id=1, source_target_pairs={{0,3},{1,0},{2,1},{3,2},{4,7},{5,4},{6,5},{7,6},{8,11},{9,8},{10,9... | collective-permute-start | bytes 4128776 | tf_op jit(solution)/shard_map/input_ring/ppermute | solution.py:383
  75.9 32.5 %collective-permute-start.3 = (bf16[192,3584]{1,0:T(8,128)(2,1)}, bf16[192,3584]{1,0:T(8,128)(2,1)}, u32[]{:S(2)}, u32[]{:S(2)}) collective-permute-start(bf16[192,3584]{1,0:T(8,128)(2,1)} %bitcast.13.x0), channel_id=1, source_target_pairs={{0,1},{1,2},{2,3},{3,0},{4,5},{5,6},{6,7},{7,4},{8,9},{9,10},{10,1... | collective-permute-start | bytes 4128776 | tf_op jit(solution)/shard_map/input_ring/ppermute | solution.py:383
  110.4 11.0 %copy-start.26 = (bf16[192,1792]{1,0:T(8,128)(2,1)S(1)}, bf16[192,1792]{1,0:T(8,128)(2,1)}, u32[]{:S(2)}) copy-start(bf16[192,1792]{1,0:T(8,128)(2,1)} %copy-done.24) | copy-start | bytes 2064388
  110.4 28.1 %collective-permute-start.11 = (bf16[96,3584]{1,0:T(8,128)(2,1)}, bf16[96,3584]{1,0:T(8,128)(2,1)S(1)}, u32[]{:S(2)}, u32[]{:S(2)}) collective-permute-start(bf16[96,3584]{1,0:T(8,128)(2,1)} %slice.95), channel_id=1, source_target_pairs={{0,3},{1,0},{2,1},{3,2},{4,7},{5,4},{6,5},{7,6},{8,11},{9,8},{10,9... | collective-permute-start | bytes 2064392 | tf_op jit(solution)/shard_map/input_ring/ppermute | solution.py:383
  112.5 25.9 %collective-permute-start.10 = (bf16[96,3584]{1,0:T(8,128)(2,1)}, bf16[96,3584]{1,0:T(8,128)(2,1)S(1)}, u32[]{:S(2)}, u32[]{:S(2)}) collective-permute-start(bf16[96,3584]{1,0:T(8,128)(2,1)} %slice.94), channel_id=1, source_target_pairs={{0,1},{1,2},{2,3},{3,0},{4,5},{5,6},{6,7},{7,4},{8,9},{9,10},{10,1... | collective-permute-start | bytes 2064392 | tf_op jit(solution)/shard_map/input_ring/ppermute | solution.py:383
  123.9 30.8 %collective-permute-start.19 = (bf16[96,1792]{1,0:T(8,128)(2,1)}, bf16[96,1792]{1,0:T(8,128)(2,1)}, u32[]{:S(2)}, u32[]{:S(2)}) collective-permute-start(bf16[96,1792]{1,0:T(8,128)(2,1)} %slice.122), channel_id=1, source_target_pairs={{0,3},{1,0},{2,1},{3,2},{4,7},{5,4},{6,5},{7,6},{8,11},{9,8},{10,9... | collective-permute-start | bytes 1032200 | tf_op jit(solution)/shard_map/saved_ring_b/ppermute | solution.py:383
  126.0 31.9 %collective-permute-start.18 = (bf16[96,1792]{1,0:T(8,128)(2,1)}, bf16[96,1792]{1,0:T(8,128)(2,1)}, u32[]{:S(2)}, u32[]{:S(2)}) collective-permute-start(bf16[96,1792]{1,0:T(8,128)(2,1)} %slice.121), channel_id=1, source_target_pairs={{0,1},{1,2},{2,3},{3,0},{4,5},{5,6},{6,7},{7,4},{8,9},{9,10},{10,1... | collective-permute-start | bytes 1032200 | tf_op jit(solution)/shard_map/saved_ring_b/ppermute | solution.py:383
  126.7 51.4 %collective-permute-start.17 = (bf16[192,3584]{1,0:T(8,128)(2,1)}, bf16[192,3584]{1,0:T(8,128)(2,1)}, u32[]{:S(2)}, u32[]{:S(2)}) collective-permute-start(bf16[192,3584]{1,0:T(8,128)(2,1)} %bitcast.16.x0), channel_id=1, source_target_pairs={{0,3},{1,0},{2,1},{3,2},{4,7},{5,4},{6,5},{7,6},{8,11},{9,8},{10,9... | collective-permute-start | bytes 4128776 | tf_op jit(solution)/shard_map/grad_ring/ppermute | solution.py:383
  129.3 40.9 %all-to-all-start.3 = ((bf16[8,96,1792]{2,1,0:T(8,128)(2,1)}), bf16[8,96,1792]{2,1,0:T(8,128)(2,1)}, u32[]{:S(2)}, u32[]{:S(2)}) async-start(bf16[8,96,1792]{2,1,0:T(8,128)(2,1)} %bitcast.84), calls=%async_computation.3 | async-start | bytes 5505024 | tf_op jit(solution)/shard_map/saved_plane_a/all_to_all | solution.py:396
  138.4 39.6 %collective-permute-start.16 = (bf16[192,3584]{1,0:T(8,128)(2,1)}, bf16[192,3584]{1,0:T(8,128)(2,1)}, u32[]{:S(2)}, u32[]{:S(2)}) collective-permute-start(bf16[192,3584]{1,0:T(8,128)(2,1)} %bitcast.16.x0), channel_id=1, source_target_pairs={{0,1},{1,2},{2,3},{3,0},{4,5},{5,6},{6,7},{7,4},{8,9},{9,10},{10,1... | collective-permute-start | bytes 4128776 | tf_op jit(solution)/shard_map/grad_ring/ppermute | solution.py:383
  150.5 19.7 %copy-start.2 = (bf16[8,24,1792]{2,1,0:T(8,128)(2,1)S(1)}, bf16[8,24,1792]{2,1,0:T(8,128)(2,1)}, u32[]{:S(2)}) copy-start(bf16[8,24,1792]{2,1,0:T(8,128)(2,1)} %copy-done) | copy-start | bytes 2064388
  150.5 19.7 %copy-start.7 = (bf16[192,1792]{1,0:T(8,128)(2,1)S(1)}, bf16[192,1792]{1,0:T(8,128)(2,1)}, u32[]{:S(2)}) copy-start(bf16[192,1792]{1,0:T(8,128)(2,1)} %copy-done.5) | copy-start | bytes 2064388
  150.5 19.7 %copy-start.10 = (bf16[192,1792]{1,0:T(8,128)(2,1)S(1)}, bf16[192,1792]{1,0:T(8,128)(2,1)}, u32[]{:S(2)}) copy-start(bf16[192,1792]{1,0:T(8,128)(2,1)} %copy-done.8) | copy-start | bytes 2064388
  154.7 32.8 %collective-permute-start.12 = (bf16[96,3584]{1,0:T(8,128)(2,1)}, bf16[96,3584]{1,0:T(8,128)(2,1)}, u32[]{:S(2)}, u32[]{:S(2)}) collective-permute-start(bf16[96,3584]{1,0:T(8,128)(2,1)} %get-tuple-element.53), channel_id=1, source_target_pairs={{0,1},{1,2},{2,3},{3,0},{4,5},{5,6},{6,7},{7,4},{8,9},{9,10},{10,1... | collective-permute-start | bytes 2064392 | tf_op jit(solution)/shard_map/output_far/ppermute | solution.py:383
  154.7 32.8 %collective-permute-start.14 = (bf16[96,3584]{1,0:T(8,128)(2,1)}, bf16[96,3584]{1,0:T(8,128)(2,1)}, u32[]{:S(2)}, u32[]{:S(2)}) collective-permute-start(bf16[96,3584]{1,0:T(8,128)(2,1)} %get-tuple-element.55), channel_id=1, source_target_pairs={{0,3},{1,0},{2,1},{3,2},{4,7},{5,4},{6,5},{7,6},{8,11},{9,8},{10,9... | collective-permute-start | bytes 2064392 | tf_op jit(solution)/shard_map/output_far/ppermute | solution.py:383
  180.6 18.4 %collective-permute-start.21 = (bf16[96,3584]{1,0:T(8,128)(2,1)S(1)}, bf16[96,3584]{1,0:T(8,128)(2,1)S(1)}, u32[]{:S(2)}, u32[]{:S(2)}) collective-permute-start(bf16[96,3584]{1,0:T(8,128)(2,1)S(1)} %slice.103), channel_id=1, source_target_pairs={{0,3},{1,0},{2,1},{3,2},{4,7},{5,4},{6,5},{7,6},{8,11},{9,8},{10,9... | collective-permute-start | bytes 2064392 | tf_op jit(solution)/shard_map/grad_ring/ppermute | solution.py:383
  180.9 18.6 %collective-permute-start.20 = (bf16[96,3584]{1,0:T(8,128)(2,1)S(1)}, bf16[96,3584]{1,0:T(8,128)(2,1)S(1)}, u32[]{:S(2)}, u32[]{:S(2)}) collective-permute-start(bf16[96,3584]{1,0:T(8,128)(2,1)S(1)} %slice.102), channel_id=1, source_target_pairs={{0,1},{1,2},{2,3},{3,0},{4,5},{5,6},{6,7},{7,4},{8,9},{9,10},{10,1... | collective-permute-start | bytes 2064392 | tf_op jit(solution)/shard_map/grad_ring/ppermute | solution.py:383
  190.0 64.6 %collective-permute-start.15 = (bf16[192,3584]{1,0:T(8,128)(2,1)}, bf16[192,3584]{1,0:T(8,128)(2,1)}, u32[]{:S(2)}, u32[]{:S(2)}) collective-permute-start(bf16[192,3584]{1,0:T(8,128)(2,1)} %pad_maximum_fusion.2), channel_id=1, source_target_pairs={{0,3},{1,0},{2,1},{3,2},{4,7},{5,4},{6,5},{7,6},{8,11},{9,8},{10,9... | collective-permute-start | bytes 4128776 | tf_op jit(solution)/shard_map/output_near/ppermute | solution.py:383
  200.4 14.3 %copy-start.18 = (bf16[96,3584]{1,0:T(8,128)(2,1)S(1)}, bf16[96,3584]{1,0:T(8,128)(2,1)}, u32[]{:S(2)}) copy-start(bf16[96,3584]{1,0:T(8,128)(2,1)} %slice.97) | copy-start | bytes 2064388
  200.4 14.3 %copy-start.20 = (bf16[96,3584]{1,0:T(8,128)(2,1)S(1)}, bf16[96,3584]{1,0:T(8,128)(2,1)}, u32[]{:S(2)}) copy-start(bf16[96,3584]{1,0:T(8,128)(2,1)} %add_convert_fusion.3) | copy-start | bytes 2064388
  213.4 18.9 %collective-permute-start.28 = (bf16[96,1792]{1,0:T(8,128)(2,1)}, bf16[96,1792]{1,0:T(8,128)(2,1)}, u32[]{:S(2)}, u32[]{:S(2)}) collective-permute-start(bf16[96,1792]{1,0:T(8,128)(2,1)} %get-tuple-element.70), channel_id=1, source_target_pairs={{0,3},{1,0},{2,1},{3,2},{4,7},{5,4},{6,5},{7,6},{8,11},{9,8},{10,9... | collective-permute-start | bytes 1032200 | tf_op jit(solution)/shard_map/back_far_a/ppermute | solution.py:383
  215.8 38.7 %collective-permute-start.13 = (bf16[192,3584]{1,0:T(8,128)(2,1)}, bf16[192,3584]{1,0:T(8,128)(2,1)}, u32[]{:S(2)}, u32[]{:S(2)}) collective-permute-start(bf16[192,3584]{1,0:T(8,128)(2,1)} %pad_maximum_fusion.1), channel_id=1, source_target_pairs={{0,1},{1,2},{2,3},{3,0},{4,5},{5,6},{6,7},{7,4},{8,9},{9,10},{10,1... | collective-permute-start | bytes 4128776 | tf_op jit(solution)/shard_map/output_near/ppermute | solution.py:383
  216.7 41.2 %all-to-all-start.4 = ((bf16[8,96,1792]{2,1,0:T(8,128)(2,1)}), bf16[8,96,1792]{2,1,0:T(8,128)(2,1)}, u32[]{:S(2)}, u32[]{:S(2)}) async-start(bf16[8,96,1792]{2,1,0:T(8,128)(2,1)} %get-tuple-element.62), calls=%async_computation.4 | async-start | bytes 5505024 | tf_op jit(solution)/shard_map/back_plane_b/all_to_all | solution.py:396
  224.0 29.1 %collective-permute-start.26 = (bf16[96,1792]{1,0:T(8,128)(2,1)}, bf16[96,1792]{1,0:T(8,128)(2,1)S(1)}, u32[]{:S(2)}, u32[]{:S(2)}) collective-permute-start(bf16[96,1792]{1,0:T(8,128)(2,1)} %copy-done.13), channel_id=1, source_target_pairs={{0,1},{1,2},{2,3},{3,0},{4,5},{5,6},{6,7},{7,4},{8,9},{9,10},{10,1... | collective-permute-start | bytes 1032200 | tf_op jit(solution)/shard_map/back_far_a/ppermute | solution.py:383
  234.3 28.8 %collective-permute-start.29 = (bf16[192,1792]{1,0:T(8,128)(2,1)}, bf16[192,1792]{1,0:T(8,128)(2,1)}, u32[]{:S(2)}, u32[]{:S(2)}) collective-permute-start(bf16[192,1792]{1,0:T(8,128)(2,1)} %pad_maximum_fusion.7), channel_id=1, source_target_pairs={{0,3},{1,0},{2,1},{3,2},{4,7},{5,4},{6,5},{7,6},{8,11},{9,8},{10,9... | collective-permute-start | bytes 2064392 | tf_op jit(solution)/shard_map/back_near_a/ppermute | solution.py:383
  254.1 14.4 %collective-permute-start.27 = (bf16[192,1792]{1,0:T(8,128)(2,1)}, bf16[192,1792]{1,0:T(8,128)(2,1)}, u32[]{:S(2)}, u32[]{:S(2)}) collective-permute-start(bf16[192,1792]{1,0:T(8,128)(2,1)} %pad_maximum_fusion.6), channel_id=1, source_target_pairs={{0,1},{1,2},{2,3},{3,0},{4,5},{5,6},{6,7},{7,4},{8,9},{9,10},{10,1... | collective-permute-start | bytes 2064392 | tf_op jit(solution)/shard_map/back_near_a/ppermute | solution.py:383
  260.4 21.4 %collective-permute-start.24 = (bf16[96,1792]{1,0:T(8,128)(2,1)}, bf16[96,1792]{1,0:T(8,128)(2,1)}, u32[]{:S(2)}, u32[]{:S(2)}) collective-permute-start(bf16[96,1792]{1,0:T(8,128)(2,1)} %bitcast.40), channel_id=1, source_target_pairs={{0,3},{1,0},{2,1},{3,2},{4,7},{5,4},{6,5},{7,6},{8,11},{9,8},{10,9... | collective-permute-start | bytes 1032200 | tf_op jit(solution)/shard_map/back_far_b/ppermute | solution.py:383
  272.0 24.9 %all-to-all-start.5 = ((bf16[8,24,3584]{2,1,0:T(8,128)(2,1)}), bf16[8,24,3584]{2,1,0:T(8,128)(2,1)S(1)}, u32[]{:S(2)}, u32[]{:S(2)}) async-start(bf16[8,24,3584]{2,1,0:T(8,128)(2,1)} %bitcast.31), calls=%async_computation.5 | async-start | bytes 2752512 | tf_op jit(solution)/shard_map/output_plane/all_to_all | solution.py:396
  281.8 8.7 %collective-permute-start.22 = (bf16[96,1792]{1,0:T(8,128)(2,1)}, bf16[96,1792]{1,0:T(8,128)(2,1)S(1)}, u32[]{:S(2)}, u32[]{:S(2)}) collective-permute-start(bf16[96,1792]{1,0:T(8,128)(2,1)} %bitcast.90), channel_id=1, source_target_pairs={{0,1},{1,2},{2,3},{3,0},{4,5},{5,6},{6,7},{7,4},{8,9},{9,10},{10,1... | collective-permute-start | bytes 1032200 | tf_op jit(solution)/shard_map/back_far_b/ppermute | solution.py:383
  283.9 30.9 %collective-permute-start.25 = (bf16[192,1792]{1,0:T(8,128)(2,1)}, bf16[192,1792]{1,0:T(8,128)(2,1)}, u32[]{:S(2)}, u32[]{:S(2)}) collective-permute-start(bf16[192,1792]{1,0:T(8,128)(2,1)} %pad_maximum_fusion.5), channel_id=1, source_target_pairs={{0,3},{1,0},{2,1},{3,2},{4,7},{5,4},{6,5},{7,6},{8,11},{9,8},{10,9... | collective-permute-start | bytes 2064392 | tf_op jit(solution)/shard_map/back_near_b/ppermute | solution.py:383
  290.6 13.1 %copy-start.15 = (bf16[2,128,192]{2,1,0:T(8,128)(2,1)S(1)}, bf16[2,128,192]{2,1,0:T(8,128)(2,1)}, u32[]{:S(2)}) copy-start(bf16[2,128,192]{2,1,0:T(8,128)(2,1)} %get-tuple-element.37.spread_ref) | copy-start | bytes 294916
  290.6 13.1 %copy-start.17 = (f32[128,128]{1,0:T(8,128)S(1)}, f32[128,128]{1,0:T(8,128)}, u32[]{:S(2)}) copy-start(f32[128,128]{1,0:T(8,128)} %get-tuple-element.38.prob_ref) | copy-start | bytes 196612
  291.5 23.3 %collective-permute-start.23 = (bf16[192,1792]{1,0:T(8,128)(2,1)}, bf16[192,1792]{1,0:T(8,128)(2,1)}, u32[]{:S(2)}, u32[]{:S(2)}) collective-permute-start(bf16[192,1792]{1,0:T(8,128)(2,1)} %pad_maximum_fusion.4), channel_id=1, source_target_pairs={{0,1},{1,2},{2,3},{3,0},{4,5},{5,6},{6,7},{7,4},{8,9},{9,10},{10,1... | collective-permute-start | bytes 2064392 | tf_op jit(solution)/shard_map/back_near_b/ppermute | solution.py:383
  296.9 15.3 %all-to-all-start.6 = ((bf16[8,24,1792]{2,1,0:T(8,128)(2,1)}), bf16[8,24,1792]{2,1,0:T(8,128)(2,1)}, u32[]{:S(2)}, u32[]{:S(2)}) async-start(bf16[8,24,1792]{2,1,0:T(8,128)(2,1)} %bitcast.41), calls=%async_computation.6 | async-start | bytes 1376256 | tf_op jit(solution)/shard_map/back_plane_a/all_to_all | solution.py:396
  (21 other events, 99.6 us)

commit v3 on v2

--- a/solution.py
+++ b/solution.py
@@ -18,6 +18,7 @@
 ROWS = EXPERTS * MSG
 TILE = 1792
 STEPS = HALF // TILE
+NEAR = 10**6
 F32 = jnp.float32
 BF16 = jnp.bfloat16
 NT = (((1,), (1,)), ((), ()))
@@ -145,10 +146,6 @@
     upper = lax.broadcasted_iota(jnp.int32, (TOTAL // MSG, 1, 8, n), 2) < 4
     last = jnp.where(upper, lo[:, 1:2], hi[:, 1:2])
     tile = jnp.concatenate([lo[:, 0:1], hi[:, 0:1], last], axis=1).reshape(TOTAL, n).astype(BF16)
-    if len(outs) == 1:
-        for p in range(RING):
-            outs[0][:, p * MSG : p * MSG + MSG] = tile[p * ROWS : p * ROWS + ROWS].reshape(EXPERTS, MSG, n)
-        return
     at = 0
     for o in outs:
         o[...] = tile[at : at + o.shape[0]]
@@ -284,11 +281,7 @@
     def _():
         lo = dot(mid[0], g_lo) + dot(mid[1], u_lo)
         hi = dot(mid[0], g_hi) + dot(mid[1], u_hi)
-        for n in range(STEPS):
-
-            @pl.when(i == STEPS + n)
-            def _():
-                pack_rows(lo, hi, outs[:5] if n == 0 else outs[5:])
+        pack_rows(lo, hi, outs)
 
 
 def backward_side(xs, gate, up, gate_w, up_w, down_w):
@@ -297,13 +290,12 @@
     w = [pl.BlockSpec((FF, TILE), lambda i, k=k: (0, first(i) + k * STEPS)) for k in (0, 1)]
     w += [pl.BlockSpec((PACK, FF), lambda i: (0, 0))] * 2
     w += [pl.BlockSpec((TILE, FF), lambda i, k=k: (second(i) + k * STEPS, 0)) for k in (0, 1, 0, 1)]
-    shapes = [(n, TILE) for n in RECEIVED] + [(EXPERTS, RING * MSG, TILE)]
     return pl.pallas_call(
         backward_kernel,
-        out_shape=tuple(jax.ShapeDtypeStruct(n, BF16) for n in shapes),
+        out_shape=tuple(jax.ShapeDtypeStruct((n, HALF), BF16) for n in RECEIVED),
         grid=(2 * STEPS,),
         in_specs=row_specs(RECEIVED) + w,
-        out_specs=tuple(pl.BlockSpec(n, lambda i, k=len(n): (0,) * k) for n in shapes),
+        out_specs=tuple(pl.BlockSpec((n, TILE), lambda i: (0, second(i))) for n in RECEIVED),
         scratch_shapes=[pltpu.VMEM((2, PACK, FF), F32), pltpu.VMEM((2, PACK, FF), BF16)],
         compiler_params=pltpu.CompilerParams(vmem_limit_bytes=VMEM),
         cost_estimate=pl.CostEstimate(
@@ -419,11 +411,27 @@
     return shift(far_lo, "z", 1), shift(far_hi, "z", -1)
 
 
+def near_kernel(left_ref, right_ref, lo_ref, hi_ref, right_out, left_out):
+    half = ROWS // 2
+    right_out[:half] = (right_ref[:half].astype(F32) + lo_ref[...].astype(F32)).astype(BF16)
+    right_out[half:] = right_ref[half:]
+    left_out[:half] = left_ref[:half]
+    left_out[half:] = (left_ref[half:].astype(F32) + hi_ref[...].astype(F32)).astype(BF16)
+
+
 @labelled
 def scatter_near(left, right, far):
-    half = ROWS // 2
-    right = jnp.concatenate([add(right[:half], far[0]), right[half:]], axis=0)
-    left = jnp.concatenate([left[:half], add(left[half:], far[1])], axis=0)
+    spec = lambda n: pl.BlockSpec((n, TILE), lambda i: (0, i))
+    right, left = pl.pallas_call(
+        near_kernel,
+        out_shape=(jax.ShapeDtypeStruct(left.shape, BF16),) * 2,
+        grid=(left.shape[1] // TILE,),
+        in_specs=[spec(ROWS), spec(ROWS), spec(ROWS // 2), spec(ROWS // 2)],
+        out_specs=(spec(ROWS),) * 2,
+        compiler_params=pltpu.CompilerParams(vmem_limit_bytes=VMEM),
+        cost_estimate=pl.CostEstimate(flops=NEAR * 10**6, bytes_accessed=10 * left.size, transcendentals=0),
+        name="near",
+    )(left, right, *far)
     return shift(right, "z", 1), shift(left, "z", -1)
 
 
@@ -454,13 +462,14 @@
     outgoing = take(fwd_boundary[0], roster[after_, 0])
     layer_input = shift(outgoing, "pipe", 1)
     saved_a, saved_b, bwd_pick = pick(after(bwd_micro, outgoing), caps, route_rows, saved_inputs[0], True)
-    back_index, saved_a, saved_b = lax.optimization_barrier((roster[before, 1], saved_a, saved_b))
-    returning = take(grad_boundary[0], back_index)
-    grad_input = shift(returning, "pipe", -1)
     own, left, right, far_lo, far_hi = gather_ring("saved_ring_a", saved_a)
     plane_b = exchange("saved_plane_b", saved_b)
     fwd_rows, _ = pick(fwd_micro, caps, route_rows, after(layer_input, plane_b, left, right)[None], False)
     kept_b = gather_ring("saved_ring_b", plane_b)
+    _, left_b, right_b, lo_b, hi_b = kept_b
+    back_index, fwd_rows, far_lo, far_hi = lax.optimization_barrier((roster[before, 1], fwd_rows, far_lo, far_hi))
+    kept_b = (plane_b, left_b, right_b, lo_b, hi_b)
+    grad_input = shift(take(grad_boundary[0], back_index), "pipe", -1)
     input_plane = exchange("input_plane", fwd_rows)
     grad_rows = pick_again(bwd_pick, after(grad_input, fwd_rows, kept_b[1], kept_b[2], far_lo, far_hi))
     grad_plane = exchange("grad_plane", grad_rows)
@@ -472,23 +481,18 @@
     own, left, right, far_lo, far_hi = forward_side(fwd, gate_w, up_w, down_w)
     far = scatter_far("output_far", far_lo, far_hi)
     grad = gather_ring("grad_ring", grad_plane, own, gate)
-    gate = after(gate, *far)
+    gate, late_routes = lax.optimization_barrier((gate, route_rows))
     parts = backward_side(grad, gate, up, gate_w, up_w, down_w)
     near = scatter_near("output_near", left, right, far)
-    far_a = scatter_far("back_far_a", *parts[3:5])
-    planes = exchange("back_plane_b", parts[5]).reshape(EXPERTS, RING, MSG, TILE)
-    fwd_total = exchange("output_plane", after(add(own, *near), planes))
-    near_a = scatter_near("back_near_a", *parts[1:3], far_a)
-    own, left, right, far = (planes[:, p].reshape(ROWS, TILE) for p in range(RING))
-    far_b = scatter_far("back_far_b", far[: ROWS // 2], far[ROWS // 2 :])
-    near_b = scatter_near("back_near_b", left, right, far_b)
-    total_a = exchange("back_plane_a", after(add(parts[0], *near_a), fwd_total))
-
-    fwd_plan = spread(fwd_micro, caps, route_rows, prob_rows)
-    bwd_plan = spread(bwd_micro, caps, route_rows, prob_rows)
+    fwd_total = exchange("output_plane", add(own, *near))
+    far = scatter_far("back_far", *parts[3:])
+    near = scatter_near("back_near", *parts[1:3], far)
+    bwd_total = exchange("back_plane", add(parts[0], *near))
+
+    fwd_plan = spread(fwd_micro, caps, late_routes, prob_rows)
+    bwd_plan = spread(bwd_micro, caps, late_routes, prob_rows)
     new_output = mix(fwd_plan, (fwd_total,), layer_input)
-    new_grad = mix(bwd_plan, (total_a,), grad_input)
-    new_grad = mix(bwd_plan, (own, *near_b), grad_input, 1, new_grad)
+    new_grad = mix(bwd_plan, (bwd_total,), grad_input)
     return new_output[None], new_grad[None]
 
 

time: 323 us -> 296 us (0.916)
  blocking collectives: 22.2 us -> 0 us
  waiting for transfers between devices: 99.8 us -> 112 us
  other arithmetic: 20.4 us -> 9.95 us
  local copies, waits for them, and re-layouts: 26.7 us -> 19 us
  Pallas kernels: 59 us -> 64.6 us
  starting transfers between devices: 85 us -> 81.1 us
    all_to_all x1 -> x0, blocking collectives: 22.2 us -> none  [exchange(): return lax.all_to_all(x, ('y', 'xh'), 0, 0, tiled=True)]
    all_to_all x6, waiting for transfers between devices: 28.2 us -> 37.1 us  [exchange(): return lax.all_to_all(x, ('y', 'xh'), 0, 0, tiled=True)]
    slice x6 -> x0, local copies, waits for them, and re-layouts: 7.88 us -> none  [the longest x3 4.54 us: scatter_near(): left = jnp.concatenate([left[:half], add(left[half:], far[1])], axis=0)]
    concatenate x6 -> x0, other arithmetic: 5.99 us -> none  [the longest x3 3.01 us: scatter_near(): left = jnp.concatenate([left[:half], add(left[half:], far[1])], axis=0)]
    pallas_call x1 -> x3, Pallas kernels: 13 us -> 18.8 us  [the longest x1 12.2 us: backward_side(): pl.pallas_call(backward_kernel, out_shape=tuple((jax.ShapeDtypeStruct((n,...]
    all_to_all x6, starting transfers between devices: 45.6 us -> 40.2 us  [exchange(): return lax.all_to_all(x, ('y', 'xh'), 0, 0, tiled=True)]
    convert_element_type x8 -> x2, other arithmetic: 11.5 us -> 7.09 us  [add(): return sum((t.astype(F32) for t in terms)).astype(BF16)]
    ppermute x30 -> x26, waiting for transfers between devices: 71.6 us -> 75 us  [shift(): return lax.ppermute(x, axis, [(i, (i + by) % n) for i in range(n)])]
  transfers between devices with their start and end apart: 36 -> 32, of which waited for: 18 -> 17; matrix products, arithmetic and copies ran while one was open for 12% -> 5% of each run, Pallas kernels for 18% -> 21%
where the time goes in v3:
time: 296 us; the launch traced here: 291 us
  waiting for transfers between devices  112 us (38%)
  starting transfers between devices  81.1 us (27%)
  Pallas kernels  64.6 us (22%)
  local copies, waits for them, and re-layouts  19 us (6%)
  other arithmetic  9.95 us (3%)
  between operations  4.56 us (2%)
    ppermute x26, waiting for transfers between devices, shift(): return lax.ppermute(x, axis, [(i, (i + by) % n) for i in range(n)])  75 us
    ppermute x26, starting transfers between devices, shift(): return lax.ppermute(x, axis, [(i, (i + by) % n) for i in range(n)])  40.9 us
    all_to_all x6, starting transfers between devices, exchange(): return lax.all_to_all(x, ('y', 'xh'), 0, 0, tiled=True)  40.2 us
    all_to_all x6, waiting for transfers between devices, exchange(): return lax.all_to_all(x, ('y', 'xh'), 0, 0, tiled=True)  37.1 us
    pallas_call x1, Pallas kernels, backward_side(): pl.pallas_call(backward_kernel, out_shape=tuple((jax.ShapeDtypeStruct((n,...  12.2 us
    pallas_call x1, Pallas kernels, forward_side(): pl.pallas_call(forward_kernel, out_shape=tuple((jax.ShapeDtypeStruct((n,...  12.2 us
    pallas_call x2, Pallas kernels, mix(): pl.pallas_call(functools.partial(mix_kernel, len(parts)), out_shape=jax.S...  8.72 us
    pallas_call x2, Pallas kernels, pick(): pl.pallas_call(pick_kernel, out_shape=shapes + [jax.ShapeDtypeStruct((ROW...  8.16 us
  transfers between devices with their start and end apart: 32, of which 17 were waited for; matrix products, arithmetic and copies ran while one was open for 5% of the time, Pallas kernels for 21%

profile of v3, /device:TPU:18, one launch (start us, length us, event | category | flops | bytes accessed | tf_op | source)
XLA Modules:
  0.0 291.2 jit_solution(702768886701503759)
XLA Ops:
  0.7 1.4 constant_dynamic-slice_fusion.3
  4.1 2.9 dynamic-slice_bitcast_fusion.1
  6.9 4.1 %pick.2 = (bf16[192,1792]{1,0:T(8,128)(2,1)S(1)}, bf16[192,1792]{1,0:T(8,128)(2,1)}, bf16[192,256]{1,0:T(8,128)(2,1)S(1)}) custom-call(s32[1]{0:T(128)} %bitcast.2.sel_ref, s32[8]{0:T(128)S(1)} %bitcast.54, s32[2,1,128]{2,1,0:T(1,128)S(1)} %bitcast.50, bf16[2,128,7168]{2,1,0:T(8,128)(2,1)} %bitcast.63, bf16[2,128,7168]{2,1,0:T(8,128)(2,1)} %bitcast.64), custom_call_target="tpu_custom_call" | custom-call | flops 352321536000 | bytes 3211264 | tf_op jit(solution)/shard_map/pick/pallas_call | solution.py:83
  11.1 1.9 collective-permute-start
  13.0 2.1 collective-permute-start.1
  15.1 6.4 %all-to-all-start = ((bf16[8,24,1792]{2,1,0:T(8,128)(2,1)}), bf16[8,24,1792]{2,1,0:T(8,128)(2,1)S(1)}, u32[]{:S(2)}, u32[]{:S(2)}) async-start(bf16[8,24,1792]{2,1,0:T(8,128)(2,1)} %bitcast.14), calls=%async_computation | async-start | bytes 1376256 | tf_op jit(solution)/shard_map/saved_plane_b/all_to_all | solution.py:388
  21.5 9.9 %collective-permute-done = bf16[192,1792]{1,0:T(8,128)(2,1)S(1)} collective-permute-done((bf16[192,1792]{1,0:T(8,128)(2,1)S(1)}, bf16[192,1792]{1,0:T(8,128)(2,1)S(1)}, u32[]{:S(2)}, u32[]{:S(2)}) %collective-permute-start) | collective-permute-done | bytes 688160 | tf_op jit(solution)/shard_map/saved_ring_a/ppermute | solution.py:375
  33.0 3.2 %collective-permute-start.4 = (bf16[96,1792]{1,0:T(8,128)(2,1)}, bf16[96,1792]{1,0:T(8,128)(2,1)}, u32[]{:S(2)}, u32[]{:S(2)}) collective-permute-start(bf16[96,1792]{1,0:T(8,128)(2,1)} %slice.33), channel_id=1, source_target_pairs={{0,3},{1,0},{2,1},{3,2},{4,7},{5,4},{6,5},{7,6},{8,11},{9,8},{10,9... | collective-permute-start | bytes 1032200 | tf_op jit(solution)/shard_map/saved_ring_a/ppermute | solution.py:375
  36.3 4.0 %pick.3 = (bf16[192,3584]{1,0:T(8,128)(2,1)}, bf16[192,256]{1,0:T(8,128)(2,1)}) custom-call(s32[1]{0:T(128)} %bitcast.sel_ref, s32[8]{0:T(128)S(1)} %bitcast.55, s32[2,1,128]{2,1,0:T(1,128)S(1)} %bitcast.51, bf16[1,128,7168]{2,1,0:T(8,128)(2,1)} %bitcast.16.lo_ref.hi_ref, bf16[1,128,7168]{2,1,0:T(8,128)(2,1)} %bitcast.16.lo_ref.hi_ref), custom_call_target="tpu_custom_call" | custom-call | flops 352321536000 | bytes 3211264 | tf_op jit(solution)/shard_map/pick/pallas_call | solution.py:83
  40.3 3.5 %collective-permute-done.3 = bf16[96,1792]{1,0:T(8,128)(2,1)} collective-permute-done((bf16[96,1792]{1,0:T(8,128)(2,1)}, bf16[96,1792]{1,0:T(8,128)(2,1)}, u32[]{:S(2)}, u32[]{:S(2)}) %collective-permute-start.3) | collective-permute-done | bytes 344096 | tf_op jit(solution)/shard_map/saved_ring_a/ppermute | solution.py:375
  45.6 2.9 dynamic-slice_bitcast_fusion
  48.4 6.6 %all-to-all-start.3 = ((bf16[8,24,3584]{2,1,0:T(8,128)(2,1)}), bf16[8,24,3584]{2,1,0:T(8,128)(2,1)}, u32[]{:S(2)}, u32[]{:S(2)}) async-start(bf16[8,24,3584]{2,1,0:T(8,128)(2,1)} %bitcast.27), calls=%async_computation.3 | async-start | bytes 2752512 | tf_op jit(solution)/shard_map/input_plane/all_to_all | solution.py:388
  55.0 1.9 collective-permute-start.6
  56.9 2.2 collective-permute-start.7
  59.1 27.8 %all-to-all-done.3 = bf16[8,24,3584]{2,1,0:T(8,128)(2,1)} async-done(((bf16[8,24,3584]{2,1,0:T(8,128)(2,1)}), bf16[8,24,3584]{2,1,0:T(8,128)(2,1)}, u32[]{:S(2)}, u32[]{:S(2)}) %all-to-all-start.3) | async-done | bytes 1376288 | tf_op jit(solution)/shard_map/input_plane/all_to_all | solution.py:388
  87.9 2.7 collective-permute-start.11
  90.6 3.2 %pick_again.1 = bf16[192,3584]{1,0:T(8,128)(2,1)} custom-call(bf16[192,256]{1,0:T(8,128)(2,1)S(1)} %get-tuple-element.47.pick_ref, bf16[128,7168]{1,0:T(8,128)(2,1)} %collective-permute-done.5.lo_ref.hi_ref.x_ref, bf16[128,7168]{1,0:T(8,128)(2,1)} %collective-permute-done.5.lo_ref.hi_ref.x_ref), custom_call_target="tpu_custom_call" | custom-call | flops 352321536000 | bytes 3211264 | tf_op jit(solution)/shard_map/pick_again/pallas_call | solution.py:109
  93.8 7.0 %all-to-all-start.1 = ((bf16[8,24,3584]{2,1,0:T(8,128)(2,1)}), bf16[8,24,3584]{2,1,0:T(8,128)(2,1)}, u32[]{:S(2)}, u32[]{:S(2)}) async-start(bf16[8,24,3584]{2,1,0:T(8,128)(2,1)} %bitcast.22), calls=%async_computation.1 | async-start | bytes 2752512 | tf_op jit(solution)/shard_map/grad_plane/all_to_all | solution.py:388
  100.8 11.1 %collective-permute-done.10.x1 = bf16[192,3584]{1,0:T(8,128)(2,1)} collective-permute-done((bf16[192,3584]{1,0:T(8,128)(2,1)}, bf16[192,3584]{1,0:T(8,128)(2,1)}, u32[]{:S(2)}, u32[]{:S(2)}) %collective-permute-start.10) | collective-permute-done | bytes 1376288 | tf_op jit(solution)/shard_map/input_ring/ppermute | solution.py:375
  113.0 1.3 slice.28
  115.5 3.3 %collective-permute-start.13 = (bf16[96,3584]{1,0:T(8,128)(2,1)S(1)}, bf16[96,3584]{1,0:T(8,128)(2,1)S(1)}, u32[]{:S(2)}, u32[]{:S(2)}) collective-permute-start(bf16[96,3584]{1,0:T(8,128)(2,1)S(1)} %slice.29), channel_id=1, source_target_pairs={{0,3},{1,0},{2,1},{3,2},{4,7},{5,4},{6,5},{7,6},{8,11},{9,8},{10,9... | collective-permute-start | bytes 2064392 | tf_op jit(solution)/shard_map/input_ring/ppermute | solution.py:375
  120.3 3.2 %collective-permute-start.9 = (bf16[96,1792]{1,0:T(8,128)(2,1)}, bf16[96,1792]{1,0:T(8,128)(2,1)}, u32[]{:S(2)}, u32[]{:S(2)}) collective-permute-start(bf16[96,1792]{1,0:T(8,128)(2,1)} %slice.35), channel_id=1, source_target_pairs={{0,3},{1,0},{2,1},{3,2},{4,7},{5,4},{6,5},{7,6},{8,11},{9,8},{10,9... | collective-permute-start | bytes 1032200 | tf_op jit(solution)/shard_map/saved_ring_b/ppermute | solution.py:375
  124.7 1.7 pad_maximum_fusion
  126.5 7.0 %all-to-all-start.2 = ((bf16[8,96,1792]{2,1,0:T(8,128)(2,1)}), bf16[8,96,1792]{2,1,0:T(8,128)(2,1)}, u32[]{:S(2)}, u32[]{:S(2)}) async-start(bf16[8,96,1792]{2,1,0:T(8,128)(2,1)} %bitcast.56), calls=%async_computation.2 | async-start | bytes 5505024 | tf_op jit(solution)/shard_map/saved_plane_a/all_to_all | solution.py:388
  134.8 2.8 collective-permute-start.19
  140.6 12.2 %forward_side.1 = (bf16[192,3584]{1,0:T(8,128)(2,1)S(1)}, bf16[192,3584]{1,0:T(8,128)(2,1)}, bf16[192,3584]{1,0:T(8,128)(2,1)}, bf16[96,3584]{1,0:T(8,128)(2,1)}, bf16[96,3584]{1,0:T(8,128)(2,1)}) custom-call(bf16[192,3584]{1,0:T(8,128)(2,1)} %bitcast.28.x0, bf16[192,3584]{1,0:T(8,128)(2,1)} %collective-permute-done.10.x1, ...), custom_call_target="tpu_custom_call" | custom-call | flops 5637144576000 | bytes 22020096 | tf_op jit(solution)/shard_map/forward_side/pallas_call | solution.py:247
  153.1 7.8 %saved_side.1 = (f32[512,256]{1,0:T(8,128)S(1)}, f32[512,256]{1,0:T(8,128)S(1)}) custom-call(bf16[8,96,1792]{2,1,0:T(8,128)(2,1)} %all-to-all-done.2.refs_0_, bf16[192,1792]{1,0:T(8,128)(2,1)S(1)} %bitcast.46, bf16[192,1792]{1,0:T(8,128)(2,1)S(1)} %copy-done.7, bf16[192,1792]{1,0:T(8,128)(2,1)S(1)} %copy-done.10, ...), custom_call_target="tpu_custom_call" | custom-call | flops 3758096384000 | bytes 12845056 | tf_op jit(solution)/shard_map/saved_side/pallas_call | solution.py:208
  165.1 3.8 %collective-permute-start.21 = (bf16[96,3584]{1,0:T(8,128)(2,1)S(1)}, bf16[96,3584]{1,0:T(8,128)(2,1)S(1)}, u32[]{:S(2)}, u32[]{:S(2)}) collective-permute-start(bf16[96,3584]{1,0:T(8,128)(2,1)S(1)} %slice.31), channel_id=1, source_target_pairs={{0,3},{1,0},{2,1},{3,2},{4,7},{5,4},{6,5},{7,6},{8,11},{9,8},{10,9... | collective-permute-start | bytes 2064392 | tf_op jit(solution)/shard_map/grad_ring/ppermute | solution.py:375
  168.8 3.2 %collective-permute-start.15 = (bf16[96,3584]{1,0:T(8,128)(2,1)}, bf16[96,3584]{1,0:T(8,128)(2,1)}, u32[]{:S(2)}, u32[]{:S(2)}) collective-permute-start(bf16[96,3584]{1,0:T(8,128)(2,1)} %get-tuple-element.62), channel_id=1, source_target_pairs={{0,3},{1,0},{2,1},{3,2},{4,7},{5,4},{6,5},{7,6},{8,11},{9,8},{10,9... | collective-permute-start | bytes 2064392 | tf_op jit(solution)/shard_map/output_far/ppermute | solution.py:375
  172.1 9.6 %collective-permute-done.20.x3 = bf16[96,3584]{1,0:T(8,128)(2,1)S(1)} collective-permute-done((bf16[96,3584]{1,0:T(8,128)(2,1)S(1)}, bf16[96,3584]{1,0:T(8,128)(2,1)S(1)}, u32[]{:S(2)}, u32[]{:S(2)}) %collective-permute-start.20) | collective-permute-done | bytes 688160 | tf_op jit(solution)/shard_map/grad_ring/ppermute | solution.py:375
  182.6 12.2 %backward_side.1 = (bf16[192,3584]{1,0:T(8,128)(2,1)}, bf16[192,3584]{1,0:T(8,128)(2,1)}, bf16[192,3584]{1,0:T(8,128)(2,1)}, bf16[96,3584]{1,0:T(8,128)(2,1)}, bf16[96,3584]{1,0:T(8,128)(2,1)}) custom-call(bf16[192,3584]{1,0:T(8,128)(2,1)} %bitcast.23.x0, bf16[192,3584]{1,0:T(8,128)(2,1)} %collective-permute-done.18.x1, ...), custom_call_target="tpu_custom_call" | custom-call | flops 5637144576000 | bytes 22020096 | tf_op jit(solution)/shard_map/backward_side/pallas_call | solution.py:293
  195.7 3.1 %collective-permute-start.23 = (bf16[96,3584]{1,0:T(8,128)(2,1)}, bf16[96,3584]{1,0:T(8,128)(2,1)}, u32[]{:S(2)}, u32[]{:S(2)}) collective-permute-start(bf16[96,3584]{1,0:T(8,128)(2,1)} %get-tuple-element.75), channel_id=1, source_target_pairs={{0,3},{1,0},{2,1},{3,2},{4,7},{5,4},{6,5},{7,6},{8,11},{9,8},{10,9... | collective-permute-start | bytes 2064392 | tf_op jit(solution)/shard_map/back_far/ppermute | solution.py:375
  198.9 3.4 %near.2 = (bf16[192,3584]{1,0:T(8,128)(2,1)}, bf16[192,3584]{1,0:T(8,128)(2,1)}) custom-call(bf16[192,3584]{1,0:T(8,128)(2,1)} %get-tuple-element.59.left_ref, bf16[192,3584]{1,0:T(8,128)(2,1)} %get-tuple-element.60.right_ref, bf16[96,3584]{1,0:T(8,128)(2,1)} %collective-permute-done.14.lo_ref, bf16[96,3584]{1,0:T(8,128)(2,1)} %collective-permute-done.15.hi_ref), custom_call_target="tpu_custom_call" | custom-call | flops 999999995904 | bytes 6881280 | tf_op jit(solution)/shard_map/output_near/near/pallas_call | solution.py:425
  202.2 1.9 collective-permute-start.17
  204.3 11.2 %collective-permute-done.22.lo_ref = bf16[96,3584]{1,0:T(8,128)(2,1)} collective-permute-done((bf16[96,3584]{1,0:T(8,128)(2,1)}, bf16[96,3584]{1,0:T(8,128)(2,1)}, u32[]{:S(2)}, u32[]{:S(2)}) %collective-permute-start.22) | collective-permute-done | bytes 688160 | tf_op jit(solution)/shard_map/back_far/ppermute | solution.py:375
  215.4 3.2 %near.3 = (bf16[192,3584]{1,0:T(8,128)(2,1)S(1)}, bf16[192,3584]{1,0:T(8,128)(2,1)}) custom-call(bf16[192,3584]{1,0:T(8,128)(2,1)} %get-tuple-element.72.left_ref, bf16[192,3584]{1,0:T(8,128)(2,1)} %get-tuple-element.73.right_ref, bf16[96,3584]{1,0:T(8,128)(2,1)} %collective-permute-done.22.lo_ref, bf16[96,3584]{1,0:T(8,128)(2,1)} %collective-permute-done.23.hi_ref), custom_call_target="tpu_custom_call" | custom-call | flops 999999995904 | bytes 6881280 | tf_op jit(solution)/shard_map/back_near/near/pallas_call | solution.py:425
  218.6 3.3 %collective-permute-start.25 = (bf16[192,3584]{1,0:T(8,128)(2,1)}, bf16[192,3584]{1,0:T(8,128)(2,1)}, u32[]{:S(2)}, u32[]{:S(2)}) collective-permute-start(bf16[192,3584]{1,0:T(8,128)(2,1)} %get-tuple-element.77), channel_id=1, source_target_pairs={{0,3},{1,0},{2,1},{3,2},{4,7},{5,4},{6,5},{7,6},{8,11},{9,8},{10,9... | collective-permute-start | bytes 4128776 | tf_op jit(solution)/shard_map/back_near/ppermute | solution.py:375
  221.9 22.6 %collective-permute-done.17 = bf16[192,3584]{1,0:T(8,128)(2,1)} collective-permute-done((bf16[192,3584]{1,0:T(8,128)(2,1)}, bf16[192,3584]{1,0:T(8,128)(2,1)}, u32[]{:S(2)}, u32[]{:S(2)}) %collective-permute-start.17) | collective-permute-done | bytes 1376288 | tf_op jit(solution)/shard_map/output_near/ppermute | solution.py:375
  244.9 3.3 %add_convert_fusion.1 = bf16[192,3584]{1,0:T(8,128)(2,1)} fusion(bf16[192,3584]{1,0:T(8,128)(2,1)} %collective-permute-done.17, bf16[192,3584]{1,0:T(8,128)(2,1)} %collective-permute-done.16, bf16[192,3584]{1,0:T(8,128)(2,1)S(1)} %get-tuple-element.58), kind=kLoop, calls=%fused_computation.2 | loop fusion | flops 4128768 | bytes 5505024 | tf_op jit(solution)/shard_map/convert_element_type | solution.py:402
  248.2 6.2 %all-to-all-start.4 = ((bf16[8,24,3584]{2,1,0:T(8,128)(2,1)}), bf16[8,24,3584]{2,1,0:T(8,128)(2,1)S(1)}, u32[]{:S(2)}, u32[]{:S(2)}) async-start(bf16[8,24,3584]{2,1,0:T(8,128)(2,1)} %bitcast.57), calls=%async_computation.4 | async-start | bytes 2752512 | tf_op jit(solution)/shard_map/output_plane/all_to_all | solution.py:388
  254.4 2.8 spread.2
  257.3 2.8 spread.3
  260.1 3.7 %collective-permute-done.25 = bf16[192,3584]{1,0:T(8,128)(2,1)} collective-permute-done((bf16[192,3584]{1,0:T(8,128)(2,1)}, bf16[192,3584]{1,0:T(8,128)(2,1)}, u32[]{:S(2)}, u32[]{:S(2)}) %collective-permute-start.25) | collective-permute-done | bytes 1376288 | tf_op jit(solution)/shard_map/back_near/ppermute | solution.py:375
  263.8 3.8 %add_convert_fusion = bf16[192,3584]{1,0:T(8,128)(2,1)} fusion(bf16[192,3584]{1,0:T(8,128)(2,1)} %collective-permute-done.25, bf16[192,3584]{1,0:T(8,128)(2,1)} %collective-permute-done.24, bf16[192,3584]{1,0:T(8,128)(2,1)} %get-tuple-element.71), kind=kLoop, calls=%fused_computation.1 | loop fusion | flops 4128768 | bytes 5505024 | tf_op jit(solution)/shard_map/convert_element_type | solution.py:402
  267.6 7.0 %all-to-all-start.5 = ((bf16[8,24,3584]{2,1,0:T(8,128)(2,1)}), bf16[8,24,3584]{2,1,0:T(8,128)(2,1)}, u32[]{:S(2)}, u32[]{:S(2)}) async-start(bf16[8,24,3584]{2,1,0:T(8,128)(2,1)} %bitcast.33), calls=%async_computation.5 | async-start | bytes 2752512 | tf_op jit(solution)/shard_map/back_plane/all_to_all | solution.py:388
  274.6 4.2 %mix.2 = bf16[128,7168]{1,0:T(8,128)(2,1)} custom-call(bf16[2,128,192]{2,1,0:T(8,128)(2,1)S(1)} %copy-done.18, f32[128,128]{1,0:T(8,128)S(1)} %copy-done.20, bf16[128,7168]{1,0:T(8,128)(2,1)} %collective-permute-done.2.x_ref, bf16[192,3584]{1,0:T(8,128)(2,1)S(1)} %bitcast.43), custom_call_target="tpu_custom_call" | custom-call | flops 352321536000 | bytes 5046272 | tf_op jit(solution)/shard_map/mix/pallas_call | solution.py:352
  278.8 7.9 %all-to-all-done.5 = bf16[8,24,3584]{2,1,0:T(8,128)(2,1)} async-done(((bf16[8,24,3584]{2,1,0:T(8,128)(2,1)}), bf16[8,24,3584]{2,1,0:T(8,128)(2,1)}, u32[]{:S(2)}, u32[]{:S(2)}) %all-to-all-start.5) | async-done | bytes 1376288 | tf_op jit(solution)/shard_map/back_plane/all_to_all | solution.py:388
  286.8 4.5 %mix.3 = bf16[128,7168]{1,0:T(8,128)(2,1)} custom-call(bf16[2,128,192]{2,1,0:T(8,128)(2,1)S(1)} %copy-done.17, f32[128,128]{1,0:T(8,128)S(1)} %copy-done.19, bf16[128,7168]{1,0:T(8,128)(2,1)} %collective-permute-done.5.lo_ref.hi_ref.x_ref, bf16[192,3584]{1,0:T(8,128)(2,1)} %bitcast.34.refs_0_), custom_call_target="tpu_custom_call" | custom-call | flops 352321536000 | bytes 5046272 | tf_op jit(solution)/shard_map/mix/pallas_call | solution.py:352
  (93 shorter events, 18.8 us)
Async XLA Ops:
  6.9 29.4 %collective-permute-start.2 = (bf16[128,7168]{1,0:T(8,128)(2,1)}, bf16[128,7168]{1,0:T(8,128)(2,1)}, u32[]{:S(2)}, u32[]{:S(2)}) collective-permute-start(bf16[128,7168]{1,0:T(8,128)(2,1)} %dynamic-slice_bitcast_fusion.1), channel_id=1, source_target_pairs={{0,32},{32,64},{64,96},{96,0},{1,33},{33,65},{65,97},{97,1},{2,34}... | collective-permute-start | bytes 5505032 | tf_op jit(solution)/shard_map/ppermute | solution.py:375
  11.1 22.0 %copy-start.3 = (bf16[192,1792]{1,0:T(8,128)(2,1)}, bf16[192,1792]{1,0:T(8,128)(2,1)S(1)}, u32[]{:S(2)}) copy-start(bf16[192,1792]{1,0:T(8,128)(2,1)S(1)} %get-tuple-element.41) | copy-start | bytes 2064388
  11.1 20.3 %collective-permute-start = (bf16[192,1792]{1,0:T(8,128)(2,1)S(1)}, bf16[192,1792]{1,0:T(8,128)(2,1)S(1)}, u32[]{:S(2)}, u32[]{:S(2)}) collective-permute-start(bf16[192,1792]{1,0:T(8,128)(2,1)S(1)} %get-tuple-element.41), channel_id=1, source_target_pairs={{0,1},{1,2},{2,3},{3,0},{4,5},{5,6},{6,7},{7,4},{8,9},{9,10},{10,1... | collective-permute-start | bytes 2064392 | tf_op jit(solution)/shard_map/saved_ring_a/ppermute | solution.py:375
  13.0 19.2 %collective-permute-start.1 = (bf16[192,1792]{1,0:T(8,128)(2,1)S(1)}, bf16[192,1792]{1,0:T(8,128)(2,1)S(1)}, u32[]{:S(2)}, u32[]{:S(2)}) collective-permute-start(bf16[192,1792]{1,0:T(8,128)(2,1)S(1)} %get-tuple-element.41), channel_id=1, source_target_pairs={{0,3},{1,0},{2,1},{3,2},{4,7},{5,4},{6,5},{7,6},{8,11},{9,8},{10,9... | collective-permute-start | bytes 2064392 | tf_op jit(solution)/shard_map/saved_ring_a/ppermute | solution.py:375
  15.1 21.2 %all-to-all-start = ((bf16[8,24,1792]{2,1,0:T(8,128)(2,1)}), bf16[8,24,1792]{2,1,0:T(8,128)(2,1)S(1)}, u32[]{:S(2)}, u32[]{:S(2)}) async-start(bf16[8,24,1792]{2,1,0:T(8,128)(2,1)} %bitcast.14), calls=%async_computation | async-start | bytes 1376256 | tf_op jit(solution)/shard_map/saved_plane_b/all_to_all | solution.py:388
  31.3 9.0 %copy-start.21 = (bf16[192,1792]{1,0:T(8,128)(2,1)}, bf16[192,1792]{1,0:T(8,128)(2,1)S(1)}, u32[]{:S(2)}) copy-start(bf16[192,1792]{1,0:T(8,128)(2,1)S(1)} %collective-permute-done) | copy-start | bytes 2064388
  32.2 11.6 %collective-permute-start.3 = (bf16[96,1792]{1,0:T(8,128)(2,1)}, bf16[96,1792]{1,0:T(8,128)(2,1)}, u32[]{:S(2)}, u32[]{:S(2)}) collective-permute-start(bf16[96,1792]{1,0:T(8,128)(2,1)} %slice.32), channel_id=1, source_target_pairs={{0,1},{1,2},{2,3},{3,0},{4,5},{5,6},{6,7},{7,4},{8,9},{9,10},{10,1... | collective-permute-start | bytes 1032200 | tf_op jit(solution)/shard_map/saved_ring_a/ppermute | solution.py:375
  32.2 8.1 %copy-start.23 = (bf16[192,1792]{1,0:T(8,128)(2,1)}, bf16[192,1792]{1,0:T(8,128)(2,1)S(1)}, u32[]{:S(2)}) copy-start(bf16[192,1792]{1,0:T(8,128)(2,1)S(1)} %collective-permute-done.1) | copy-start | bytes 2064388
  33.0 10.8 %collective-permute-start.4 = (bf16[96,1792]{1,0:T(8,128)(2,1)}, bf16[96,1792]{1,0:T(8,128)(2,1)}, u32[]{:S(2)}, u32[]{:S(2)}) collective-permute-start(bf16[96,1792]{1,0:T(8,128)(2,1)} %slice.33), channel_id=1, source_target_pairs={{0,3},{1,0},{2,1},{3,2},{4,7},{5,4},{6,5},{7,6},{8,11},{9,8},{10,9... | collective-permute-start | bytes 1032200 | tf_op jit(solution)/shard_map/saved_ring_a/ppermute | solution.py:375
  48.4 42.2 %collective-permute-start.5 = (bf16[128,7168]{1,0:T(8,128)(2,1)}, bf16[128,7168]{1,0:T(8,128)(2,1)}, u32[]{:S(2)}, u32[]{:S(2)}) collective-permute-start(bf16[128,7168]{1,0:T(8,128)(2,1)} %dynamic-slice_bitcast_fusion), channel_id=1, source_target_pairs={{0,96},{32,0},{64,32},{96,64},{1,97},{33,1},{65,33},{97,65},{2,98}... | collective-permute-start | bytes 5505032 | tf_op jit(solution)/shard_map/ppermute | solution.py:375
  48.4 6.6 %copy-start.1 = (bf16[8,24,1792]{2,1,0:T(8,128)(2,1)S(1)}, bf16[8,24,1792]{2,1,0:T(8,128)(2,1)}, u32[]{:S(2)}) copy-start(bf16[8,24,1792]{2,1,0:T(8,128)(2,1)} %copy-done) | copy-start | bytes 2064388
  48.4 38.5 %all-to-all-start.3 = ((bf16[8,24,3584]{2,1,0:T(8,128)(2,1)}), bf16[8,24,3584]{2,1,0:T(8,128)(2,1)}, u32[]{:S(2)}, u32[]{:S(2)}) async-start(bf16[8,24,3584]{2,1,0:T(8,128)(2,1)} %bitcast.27), calls=%async_computation.3 | async-start | bytes 2752512 | tf_op jit(solution)/shard_map/input_plane/all_to_all | solution.py:388
  55.0 35.6 %collective-permute-start.6 = (bf16[192,1792]{1,0:T(8,128)(2,1)S(1)}, bf16[192,1792]{1,0:T(8,128)(2,1)S(1)}, u32[]{:S(2)}, u32[]{:S(2)}) collective-permute-start(bf16[192,1792]{1,0:T(8,128)(2,1)S(1)} %bitcast.44), channel_id=1, source_target_pairs={{0,1},{1,2},{2,3},{3,0},{4,5},{5,6},{6,7},{7,4},{8,9},{9,10},{10,1... | collective-permute-start | bytes 2064392 | tf_op jit(solution)/shard_map/saved_ring_b/ppermute | solution.py:375
  56.9 33.6 %collective-permute-start.7 = (bf16[192,1792]{1,0:T(8,128)(2,1)S(1)}, bf16[192,1792]{1,0:T(8,128)(2,1)S(1)}, u32[]{:S(2)}, u32[]{:S(2)}) collective-permute-start(bf16[192,1792]{1,0:T(8,128)(2,1)S(1)} %bitcast.45), channel_id=1, source_target_pairs={{0,3},{1,0},{2,1},{3,2},{4,7},{5,4},{6,5},{7,6},{8,11},{9,8},{10,9... | collective-permute-start | bytes 2064392 | tf_op jit(solution)/shard_map/saved_ring_b/ppermute | solution.py:375
  87.0 24.9 %collective-permute-start.10 = (bf16[192,3584]{1,0:T(8,128)(2,1)}, bf16[192,3584]{1,0:T(8,128)(2,1)}, u32[]{:S(2)}, u32[]{:S(2)}) collective-permute-start(bf16[192,3584]{1,0:T(8,128)(2,1)} %bitcast.28.x0), channel_id=1, source_target_pairs={{0,1},{1,2},{2,3},{3,0},{4,5},{5,6},{6,7},{7,4},{8,9},{9,10},{10,1... | collective-permute-start | bytes 4128776 | tf_op jit(solution)/shard_map/input_ring/ppermute | solution.py:375
  87.9 24.0 %collective-permute-start.11 = (bf16[192,3584]{1,0:T(8,128)(2,1)}, bf16[192,3584]{1,0:T(8,128)(2,1)}, u32[]{:S(2)}, u32[]{:S(2)}) collective-permute-start(bf16[192,3584]{1,0:T(8,128)(2,1)} %bitcast.28.x0), channel_id=1, source_target_pairs={{0,3},{1,0},{2,1},{3,2},{4,7},{5,4},{6,5},{7,6},{8,11},{9,8},{10,9... | collective-permute-start | bytes 4128776 | tf_op jit(solution)/shard_map/input_ring/ppermute | solution.py:375
  93.8 19.2 %all-to-all-start.1 = ((bf16[8,24,3584]{2,1,0:T(8,128)(2,1)}), bf16[8,24,3584]{2,1,0:T(8,128)(2,1)}, u32[]{:S(2)}, u32[]{:S(2)}) async-start(bf16[8,24,3584]{2,1,0:T(8,128)(2,1)} %bitcast.22), calls=%async_computation.1 | async-start | bytes 2752512 | tf_op jit(solution)/shard_map/grad_plane/all_to_all | solution.py:388
  113.0 5.8 %copy-start.6 = (bf16[192,1792]{1,0:T(8,128)(2,1)S(1)}, bf16[192,1792]{1,0:T(8,128)(2,1)}, u32[]{:S(2)}) copy-start(bf16[192,1792]{1,0:T(8,128)(2,1)} %copy-done.5) | copy-start | bytes 2064388
  113.0 6.6 %copy-start.9 = (bf16[192,1792]{1,0:T(8,128)(2,1)S(1)}, bf16[192,1792]{1,0:T(8,128)(2,1)}, u32[]{:S(2)}) copy-start(bf16[192,1792]{1,0:T(8,128)(2,1)} %copy-done.8) | copy-start | bytes 2064388
  114.3 19.7 %collective-permute-start.12 = (bf16[96,3584]{1,0:T(8,128)(2,1)S(1)}, bf16[96,3584]{1,0:T(8,128)(2,1)S(1)}, u32[]{:S(2)}, u32[]{:S(2)}) collective-permute-start(bf16[96,3584]{1,0:T(8,128)(2,1)S(1)} %slice.28), channel_id=1, source_target_pairs={{0,1},{1,2},{2,3},{3,0},{4,5},{5,6},{6,7},{7,4},{8,9},{9,10},{10,1... | collective-permute-start | bytes 2064392 | tf_op jit(solution)/shard_map/input_ring/ppermute | solution.py:375
  115.5 9.2 %copy-start.4 = (bf16[192,1792]{1,0:T(8,128)(2,1)S(1)}, bf16[192,1792]{1,0:T(8,128)(2,1)}, u32[]{:S(2)}) copy-start(bf16[192,1792]{1,0:T(8,128)(2,1)} %copy-done.3) | copy-start | bytes 2064388
  115.5 9.2 %copy-start.22 = (bf16[192,1792]{1,0:T(8,128)(2,1)S(1)}, bf16[192,1792]{1,0:T(8,128)(2,1)}, u32[]{:S(2)}) copy-start(bf16[192,1792]{1,0:T(8,128)(2,1)} %copy-done.21) | copy-start | bytes 2064388
  115.5 9.2 %copy-start.24 = (bf16[192,1792]{1,0:T(8,128)(2,1)S(1)}, bf16[192,1792]{1,0:T(8,128)(2,1)}, u32[]{:S(2)}) copy-start(bf16[192,1792]{1,0:T(8,128)(2,1)} %copy-done.23) | copy-start | bytes 2064388
  115.5 22.1 %collective-permute-start.13 = (bf16[96,3584]{1,0:T(8,128)(2,1)S(1)}, bf16[96,3584]{1,0:T(8,128)(2,1)S(1)}, u32[]{:S(2)}, u32[]{:S(2)}) collective-permute-start(bf16[96,3584]{1,0:T(8,128)(2,1)S(1)} %slice.29), channel_id=1, source_target_pairs={{0,3},{1,0},{2,1},{3,2},{4,7},{5,4},{6,5},{7,6},{8,11},{9,8},{10,9... | collective-permute-start | bytes 2064392 | tf_op jit(solution)/shard_map/input_ring/ppermute | solution.py:375
  119.6 33.3 %collective-permute-start.8 = (bf16[96,1792]{1,0:T(8,128)(2,1)}, bf16[96,1792]{1,0:T(8,128)(2,1)}, u32[]{:S(2)}, u32[]{:S(2)}) collective-permute-start(bf16[96,1792]{1,0:T(8,128)(2,1)} %slice.34), channel_id=1, source_target_pairs={{0,1},{1,2},{2,3},{3,0},{4,5},{5,6},{6,7},{7,4},{8,9},{9,10},{10,1... | collective-permute-start | bytes 1032200 | tf_op jit(solution)/shard_map/saved_ring_b/ppermute | solution.py:375
  120.3 32.5 %collective-permute-start.9 = (bf16[96,1792]{1,0:T(8,128)(2,1)}, bf16[96,1792]{1,0:T(8,128)(2,1)}, u32[]{:S(2)}, u32[]{:S(2)}) collective-permute-start(bf16[96,1792]{1,0:T(8,128)(2,1)} %slice.35), channel_id=1, source_target_pairs={{0,3},{1,0},{2,1},{3,2},{4,7},{5,4},{6,5},{7,6},{8,11},{9,8},{10,9... | collective-permute-start | bytes 1032200 | tf_op jit(solution)/shard_map/saved_ring_b/ppermute | solution.py:375
  126.5 35.0 %collective-permute-start.18 = (bf16[192,3584]{1,0:T(8,128)(2,1)}, bf16[192,3584]{1,0:T(8,128)(2,1)}, u32[]{:S(2)}, u32[]{:S(2)}) collective-permute-start(bf16[192,3584]{1,0:T(8,128)(2,1)} %bitcast.23.x0), channel_id=1, source_target_pairs={{0,1},{1,2},{2,3},{3,0},{4,5},{5,6},{6,7},{7,4},{8,9},{9,10},{10,1... | collective-permute-start | bytes 4128776 | tf_op jit(solution)/shard_map/grad_ring/ppermute | solution.py:375
  126.5 26.6 %all-to-all-start.2 = ((bf16[8,96,1792]{2,1,0:T(8,128)(2,1)}), bf16[8,96,1792]{2,1,0:T(8,128)(2,1)}, u32[]{:S(2)}, u32[]{:S(2)}) async-start(bf16[8,96,1792]{2,1,0:T(8,128)(2,1)} %bitcast.56), calls=%async_computation.2 | async-start | bytes 5505024 | tf_op jit(solution)/shard_map/saved_plane_a/all_to_all | solution.py:388
  134.8 27.9 %collective-permute-start.19 = (bf16[192,3584]{1,0:T(8,128)(2,1)}, bf16[192,3584]{1,0:T(8,128)(2,1)}, u32[]{:S(2)}, u32[]{:S(2)}) collective-permute-start(bf16[192,3584]{1,0:T(8,128)(2,1)} %bitcast.23.x0), channel_id=1, source_target_pairs={{0,3},{1,0},{2,1},{3,2},{4,7},{5,4},{6,5},{7,6},{8,11},{9,8},{10,9... | collective-permute-start | bytes 4128776 | tf_op jit(solution)/shard_map/grad_ring/ppermute | solution.py:375
  140.6 12.5 %copy-start.2 = (bf16[8,24,1792]{2,1,0:T(8,128)(2,1)S(1)}, bf16[8,24,1792]{2,1,0:T(8,128)(2,1)}, u32[]{:S(2)}) copy-start(bf16[8,24,1792]{2,1,0:T(8,128)(2,1)} %copy-done) | copy-start | bytes 2064388
  140.6 12.5 %copy-start.7 = (bf16[192,1792]{1,0:T(8,128)(2,1)S(1)}, bf16[192,1792]{1,0:T(8,128)(2,1)}, u32[]{:S(2)}) copy-start(bf16[192,1792]{1,0:T(8,128)(2,1)} %copy-done.5) | copy-start | bytes 2064388
  140.6 12.5 %copy-start.10 = (bf16[192,1792]{1,0:T(8,128)(2,1)S(1)}, bf16[192,1792]{1,0:T(8,128)(2,1)}, u32[]{:S(2)}) copy-start(bf16[192,1792]{1,0:T(8,128)(2,1)} %copy-done.8) | copy-start | bytes 2064388
  163.8 17.9 %collective-permute-start.20 = (bf16[96,3584]{1,0:T(8,128)(2,1)S(1)}, bf16[96,3584]{1,0:T(8,128)(2,1)S(1)}, u32[]{:S(2)}, u32[]{:S(2)}) collective-permute-start(bf16[96,3584]{1,0:T(8,128)(2,1)S(1)} %slice.30), channel_id=1, source_target_pairs={{0,1},{1,2},{2,3},{3,0},{4,5},{5,6},{6,7},{7,4},{8,9},{9,10},{10,1... | collective-permute-start | bytes 2064392 | tf_op jit(solution)/shard_map/grad_ring/ppermute | solution.py:375
  165.1 17.5 %collective-permute-start.21 = (bf16[96,3584]{1,0:T(8,128)(2,1)S(1)}, bf16[96,3584]{1,0:T(8,128)(2,1)S(1)}, u32[]{:S(2)}, u32[]{:S(2)}) collective-permute-start(bf16[96,3584]{1,0:T(8,128)(2,1)S(1)} %slice.31), channel_id=1, source_target_pairs={{0,3},{1,0},{2,1},{3,2},{4,7},{5,4},{6,5},{7,6},{8,11},{9,8},{10,9... | collective-permute-start | bytes 2064392 | tf_op jit(solution)/shard_map/grad_ring/ppermute | solution.py:375
  168.8 30.0 %collective-permute-start.14 = (bf16[96,3584]{1,0:T(8,128)(2,1)}, bf16[96,3584]{1,0:T(8,128)(2,1)}, u32[]{:S(2)}, u32[]{:S(2)}) collective-permute-start(bf16[96,3584]{1,0:T(8,128)(2,1)} %get-tuple-element.61), channel_id=1, source_target_pairs={{0,1},{1,2},{2,3},{3,0},{4,5},{5,6},{6,7},{7,4},{8,9},{9,10},{10,1... | collective-permute-start | bytes 2064392 | tf_op jit(solution)/shard_map/output_far/ppermute | solution.py:375
  168.8 30.0 %collective-permute-start.15 = (bf16[96,3584]{1,0:T(8,128)(2,1)}, bf16[96,3584]{1,0:T(8,128)(2,1)}, u32[]{:S(2)}, u32[]{:S(2)}) collective-permute-start(bf16[96,3584]{1,0:T(8,128)(2,1)} %get-tuple-element.62), channel_id=1, source_target_pairs={{0,3},{1,0},{2,1},{3,2},{4,7},{5,4},{6,5},{7,6},{8,11},{9,8},{10,9... | collective-permute-start | bytes 2064392 | tf_op jit(solution)/shard_map/output_far/ppermute | solution.py:375
  194.8 20.7 %collective-permute-start.22 = (bf16[96,3584]{1,0:T(8,128)(2,1)}, bf16[96,3584]{1,0:T(8,128)(2,1)}, u32[]{:S(2)}, u32[]{:S(2)}) collective-permute-start(bf16[96,3584]{1,0:T(8,128)(2,1)} %get-tuple-element.74), channel_id=1, source_target_pairs={{0,1},{1,2},{2,3},{3,0},{4,5},{5,6},{6,7},{7,4},{8,9},{9,10},{10,1... | collective-permute-start | bytes 2064392 | tf_op jit(solution)/shard_map/back_far/ppermute | solution.py:375
  195.7 19.7 %collective-permute-start.23 = (bf16[96,3584]{1,0:T(8,128)(2,1)}, bf16[96,3584]{1,0:T(8,128)(2,1)}, u32[]{:S(2)}, u32[]{:S(2)}) collective-permute-start(bf16[96,3584]{1,0:T(8,128)(2,1)} %get-tuple-element.75), channel_id=1, source_target_pairs={{0,3},{1,0},{2,1},{3,2},{4,7},{5,4},{6,5},{7,6},{8,11},{9,8},{10,9... | collective-permute-start | bytes 2064392 | tf_op jit(solution)/shard_map/back_far/ppermute | solution.py:375
  202.2 42.3 %collective-permute-start.17 = (bf16[192,3584]{1,0:T(8,128)(2,1)}, bf16[192,3584]{1,0:T(8,128)(2,1)}, u32[]{:S(2)}, u32[]{:S(2)}) collective-permute-start(bf16[192,3584]{1,0:T(8,128)(2,1)} %get-tuple-element.64), channel_id=1, source_target_pairs={{0,3},{1,0},{2,1},{3,2},{4,7},{5,4},{6,5},{7,6},{8,11},{9,8},{10,9... | collective-permute-start | bytes 4128776 | tf_op jit(solution)/shard_map/output_near/ppermute | solution.py:375
  204.2 40.7 %collective-permute-start.16 = (bf16[192,3584]{1,0:T(8,128)(2,1)}, bf16[192,3584]{1,0:T(8,128)(2,1)}, u32[]{:S(2)}, u32[]{:S(2)}) collective-permute-start(bf16[192,3584]{1,0:T(8,128)(2,1)} %get-tuple-element.63), channel_id=1, source_target_pairs={{0,1},{1,2},{2,3},{3,0},{4,5},{5,6},{6,7},{7,4},{8,9},{9,10},{10,1... | collective-permute-start | bytes 4128776 | tf_op jit(solution)/shard_map/output_near/ppermute | solution.py:375
  218.6 45.1 %collective-permute-start.25 = (bf16[192,3584]{1,0:T(8,128)(2,1)}, bf16[192,3584]{1,0:T(8,128)(2,1)}, u32[]{:S(2)}, u32[]{:S(2)}) collective-permute-start(bf16[192,3584]{1,0:T(8,128)(2,1)} %get-tuple-element.77), channel_id=1, source_target_pairs={{0,3},{1,0},{2,1},{3,2},{4,7},{5,4},{6,5},{7,6},{8,11},{9,8},{10,9... | collective-permute-start | bytes 4128776 | tf_op jit(solution)/shard_map/back_near/ppermute | solution.py:375
  221.9 41.8 %collective-permute-start.24 = (bf16[192,3584]{1,0:T(8,128)(2,1)S(1)}, bf16[192,3584]{1,0:T(8,128)(2,1)}, u32[]{:S(2)}, u32[]{:S(2)}) collective-permute-start(bf16[192,3584]{1,0:T(8,128)(2,1)S(1)} %get-tuple-element.76), channel_id=1, source_target_pairs={{0,1},{1,2},{2,3},{3,0},{4,5},{5,6},{6,7},{7,4},{8,9},{9,10},{10,1... | collective-permute-start | bytes 4128776 | tf_op jit(solution)/shard_map/back_near/ppermute | solution.py:375
  248.2 19.3 %all-to-all-start.4 = ((bf16[8,24,3584]{2,1,0:T(8,128)(2,1)}), bf16[8,24,3584]{2,1,0:T(8,128)(2,1)S(1)}, u32[]{:S(2)}, u32[]{:S(2)}) async-start(bf16[8,24,3584]{2,1,0:T(8,128)(2,1)} %bitcast.57), calls=%async_computation.4 | async-start | bytes 2752512 | tf_op jit(solution)/shard_map/output_plane/all_to_all | solution.py:388
  267.5 7.0 %copy-start.18 = (bf16[2,128,192]{2,1,0:T(8,128)(2,1)S(1)}, bf16[2,128,192]{2,1,0:T(8,128)(2,1)}, u32[]{:S(2)}) copy-start(bf16[2,128,192]{2,1,0:T(8,128)(2,1)} %get-tuple-element.54.spread_ref) | copy-start | bytes 294916
  267.5 7.0 %copy-start.20 = (f32[128,128]{1,0:T(8,128)S(1)}, f32[128,128]{1,0:T(8,128)}, u32[]{:S(2)}) copy-start(f32[128,128]{1,0:T(8,128)} %get-tuple-element.55.prob_ref) | copy-start | bytes 196612
  267.6 19.2 %all-to-all-start.5 = ((bf16[8,24,3584]{2,1,0:T(8,128)(2,1)}), bf16[8,24,3584]{2,1,0:T(8,128)(2,1)}, u32[]{:S(2)}, u32[]{:S(2)}) async-start(bf16[8,24,3584]{2,1,0:T(8,128)(2,1)} %bitcast.33), calls=%async_computation.5 | async-start | bytes 2752512 | tf_op jit(solution)/shard_map/back_plane/all_to_all | solution.py:388
  274.6 12.2 %copy-start.17 = (bf16[2,128,192]{2,1,0:T(8,128)(2,1)S(1)}, bf16[2,128,192]{2,1,0:T(8,128)(2,1)}, u32[]{:S(2)}) copy-start(bf16[2,128,192]{2,1,0:T(8,128)(2,1)} %get-tuple-element.65.spread_ref) | copy-start | bytes 294916
  274.6 12.2 %copy-start.19 = (f32[128,128]{1,0:T(8,128)S(1)}, f32[128,128]{1,0:T(8,128)}, u32[]{:S(2)}) copy-start(f32[128,128]{1,0:T(8,128)} %get-tuple-element.66.prob_ref) | copy-start | bytes 196612
  (9 other events, 20.2 us)

commit v4 on v3

--- a/solution.py
+++ b/solution.py
@@ -18,6 +18,7 @@
 ROWS = EXPERTS * MSG
 TILE = 1792
 STEPS = HALF // TILE
+SLICE = 3584
 NEAR = 10**6
 F32 = jnp.float32
 BF16 = jnp.bfloat16
@@ -347,7 +348,7 @@
 
 
 def mix(plan, parts, x, first=0, into=None):
-    tiles = parts[0].shape[1] // TILE
+    tiles = parts[0].shape[1] // SLICE
     into = () if into is None else (into,)
     return pl.pallas_call(
         functools.partial(mix_kernel, len(parts)),
@@ -356,15 +357,15 @@
         in_specs=[
             pl.BlockSpec((1, TOK, ROWS), lambda n, h: (h, 0, 0)),
             pl.BlockSpec((TOK, TOK), lambda n, h: (0, 0)),
-            pl.BlockSpec((TOK, TILE), lambda n, h: (0, h * STEPS + first + n)),
+            pl.BlockSpec((TOK, SLICE), lambda n, h: (0, h * (HALF // SLICE) + first + n)),
         ]
-        + [pl.BlockSpec((ROWS, TILE), lambda n, h: (0, n)) for _ in parts]
+        + [pl.BlockSpec((ROWS, SLICE), lambda n, h: (0, n)) for _ in parts]
         + [pl.BlockSpec(memory_space=pl.ANY) for _ in into],
-        out_specs=pl.BlockSpec((TOK, TILE), lambda n, h: (0, h * STEPS + first + n)),
+        out_specs=pl.BlockSpec((TOK, SLICE), lambda n, h: (0, h * (HALF // SLICE) + first + n)),
         input_output_aliases={3 + len(parts): 0} if into else {},
         compiler_params=pltpu.CompilerParams(vmem_limit_bytes=VMEM),
         cost_estimate=pl.CostEstimate(
-            flops=SPAN * 4 * ROWS * TOK * TILE * tiles, bytes_accessed=2 * (4 * TOK + ROWS) * TILE * tiles, transcendentals=0
+            flops=SPAN * 4 * ROWS * TOK * SLICE * tiles, bytes_accessed=2 * (4 * TOK + ROWS) * SLICE * tiles, transcendentals=0
         ),
         name="mix",
     )(*plan, x, *parts, *into)
@@ -464,10 +465,11 @@
     saved_a, saved_b, bwd_pick = pick(after(bwd_micro, outgoing), caps, route_rows, saved_inputs[0], True)
     own, left, right, far_lo, far_hi = gather_ring("saved_ring_a", saved_a)
     plane_b = exchange("saved_plane_b", saved_b)
+    left, right, back_index = lax.optimization_barrier((left, right, roster[before, 1]))
     fwd_rows, _ = pick(fwd_micro, caps, route_rows, after(layer_input, plane_b, left, right)[None], False)
     kept_b = gather_ring("saved_ring_b", plane_b)
     _, left_b, right_b, lo_b, hi_b = kept_b
-    back_index, fwd_rows, far_lo, far_hi = lax.optimization_barrier((roster[before, 1], fwd_rows, far_lo, far_hi))
+    fwd_rows, far_lo, far_hi = lax.optimization_barrier((fwd_rows, far_lo, far_hi))
     kept_b = (plane_b, left_b, right_b, lo_b, hi_b)
     grad_input = shift(take(grad_boundary[0], back_index), "pipe", -1)
     input_plane = exchange("input_plane", fwd_rows)

time: 296 us -> 290 us (0.980)
  blocking collectives: 0 us -> 18.6 us
  waiting for transfers between devices: 112 us -> 96.9 us
  starting transfers between devices: 81.1 us -> 73.7 us
  Pallas kernels: 64.6 us -> 61.4 us
    all_to_all x6 -> x5, waiting for transfers between devices: 37.1 us -> 17.4 us  [exchange(): return lax.all_to_all(x, ('y', 'xh'), 0, 0, tiled=True)]
    all_to_all x0 -> x1, blocking collectives: none -> 18.6 us  [exchange(): return lax.all_to_all(x, ('y', 'xh'), 0, 0, tiled=True)]
    all_to_all x6 -> x5, starting transfers between devices: 40.2 us -> 34.2 us  [exchange(): return lax.all_to_all(x, ('y', 'xh'), 0, 0, tiled=True)]
    ppermute x26, waiting for transfers between devices: 75 us -> 79.4 us  [shift(): return lax.ppermute(x, axis, [(i, (i + by) % n) for i in range(n)])]
  transfers between devices with their start and end apart: 32 -> 31, of which waited for: 17 -> 13; matrix products, arithmetic and copies ran while one was open for 5% -> 6% of each run, Pallas kernels for 21% -> 20%
where the time goes in v4:
time: 290 us; the launch traced here: 286 us
  waiting for transfers between devices  96.9 us (33%)
  starting transfers between devices  73.7 us (25%)
  Pallas kernels  61.4 us (21%)
  local copies, waits for them, and re-layouts  20.6 us (7%)
  blocking collectives  18.6 us (6%)
  other arithmetic  9.97 us (3%)
  between operations  4.83 us (2%)
    ppermute x26, waiting for transfers between devices, shift(): return lax.ppermute(x, axis, [(i, (i + by) % n) for i in range(n)])  79.4 us
    ppermute x26, starting transfers between devices, shift(): return lax.ppermute(x, axis, [(i, (i + by) % n) for i in range(n)])  39.6 us
    all_to_all x5, starting transfers between devices, exchange(): return lax.all_to_all(x, ('y', 'xh'), 0, 0, tiled=True)  34.2 us
    all_to_all x1, blocking collectives, exchange(): return lax.all_to_all(x, ('y', 'xh'), 0, 0, tiled=True)  18.6 us
    all_to_all x5, waiting for transfers between devices, exchange(): return lax.all_to_all(x, ('y', 'xh'), 0, 0, tiled=True)  17.4 us
    pallas_call x1, Pallas kernels, backward_side(): pl.pallas_call(backward_kernel, out_shape=tuple((jax.ShapeDtypeStruct((n,...  12.2 us
    pallas_call x1, Pallas kernels, forward_side(): pl.pallas_call(forward_kernel, out_shape=tuple((jax.ShapeDtypeStruct((n,...  12.2 us
    pallas_call x2, Pallas kernels, pick(): pl.pallas_call(pick_kernel, out_shape=shapes + [jax.ShapeDtypeStruct((ROW...  8.41 us
  transfers between devices with their start and end apart: 31, of which 13 were waited for; matrix products, arithmetic and copies ran while one was open for 6% of the time, Pallas kernels for 20%

profile of v4, /device:TPU:18, one launch (start us, length us, event | category | flops | bytes accessed | tf_op | source)
XLA Modules:
  0.0 286.0 jit_solution(14524498836291065174)
XLA Ops:
  0.7 1.5 constant_dynamic-slice_fusion.2
  4.1 2.9 dynamic-slice_bitcast_fusion.1
  7.0 4.2 %pick.2 = (bf16[192,1792]{1,0:T(8,128)(2,1)S(1)}, bf16[192,1792]{1,0:T(8,128)(2,1)}, bf16[192,256]{1,0:T(8,128)(2,1)S(1)}) custom-call(s32[1]{0:T(128)} %bitcast.2.sel_ref, s32[8]{0:T(128)S(1)} %bitcast.55, s32[2,1,128]{2,1,0:T(1,128)S(1)} %bitcast.51, bf16[2,128,7168]{2,1,0:T(8,128)(2,1)} %bitcast.64, bf16[2,128,7168]{2,1,0:T(8,128)(2,1)} %bitcast.65), custom_call_target="tpu_custom_call" | custom-call | flops 352321536000 | bytes 3211264 | tf_op jit(solution)/shard_map/pick/pallas_call | solution.py:84
  11.2 1.9 collective-permute-start
  13.2 2.1 collective-permute-start.1
  15.3 6.4 %all-to-all-start = ((bf16[8,24,1792]{2,1,0:T(8,128)(2,1)}), bf16[8,24,1792]{2,1,0:T(8,128)(2,1)S(1)}, u32[]{:S(2)}, u32[]{:S(2)}) async-start(bf16[8,24,1792]{2,1,0:T(8,128)(2,1)} %bitcast.14), calls=%async_computation | async-start | bytes 1376256 | tf_op jit(solution)/shard_map/saved_plane_b/all_to_all | solution.py:389
  21.7 9.9 %collective-permute-done = bf16[192,1792]{1,0:T(8,128)(2,1)S(1)} collective-permute-done((bf16[192,1792]{1,0:T(8,128)(2,1)S(1)}, bf16[192,1792]{1,0:T(8,128)(2,1)S(1)}, u32[]{:S(2)}, u32[]{:S(2)}) %collective-permute-start) | collective-permute-done | bytes 688160 | tf_op jit(solution)/shard_map/saved_ring_a/ppermute | solution.py:376
  35.6 2.0 collective-permute-start.4
  38.3 2.8 dynamic-slice_bitcast_fusion
  41.1 4.2 %pick.3 = (bf16[192,3584]{1,0:T(8,128)(2,1)}, bf16[192,256]{1,0:T(8,128)(2,1)}) custom-call(s32[1]{0:T(128)} %bitcast.sel_ref, s32[8]{0:T(128)S(1)} %bitcast.56, s32[2,1,128]{2,1,0:T(1,128)S(1)} %bitcast.52, bf16[1,128,7168]{2,1,0:T(8,128)(2,1)} %bitcast.16.lo_ref.hi_ref, bf16[1,128,7168]{2,1,0:T(8,128)(2,1)} %bitcast.16.lo_ref.hi_ref), custom_call_target="tpu_custom_call" | custom-call | flops 352321536000 | bytes 3211264 | tf_op jit(solution)/shard_map/pick/pallas_call | solution.py:84
  45.3 7.0 %all-to-all-start.3 = ((bf16[8,24,3584]{2,1,0:T(8,128)(2,1)}), bf16[8,24,3584]{2,1,0:T(8,128)(2,1)}, u32[]{:S(2)}, u32[]{:S(2)}) async-start(bf16[8,24,3584]{2,1,0:T(8,128)(2,1)} %bitcast.27), calls=%async_computation.3 | async-start | bytes 2752512 | tf_op jit(solution)/shard_map/input_plane/all_to_all | solution.py:389
  52.3 1.6 collective-permute-start.6
  53.9 1.8 collective-permute-start.7
  55.7 14.6 %collective-permute-done.6.refs_2_ = bf16[192,1792]{1,0:T(8,128)(2,1)S(1)} collective-permute-done((bf16[192,1792]{1,0:T(8,128)(2,1)S(1)}, bf16[192,1792]{1,0:T(8,128)(2,1)S(1)}, u32[]{:S(2)}, u32[]{:S(2)}) %collective-permute-start.6) | collective-permute-done | bytes 688160 | tf_op jit(solution)/shard_map/saved_ring_b/ppermute | solution.py:376
  72.0 7.4 %all-to-all-done.3 = bf16[8,24,3584]{2,1,0:T(8,128)(2,1)} async-done(((bf16[8,24,3584]{2,1,0:T(8,128)(2,1)}), bf16[8,24,3584]{2,1,0:T(8,128)(2,1)}, u32[]{:S(2)}, u32[]{:S(2)}) %all-to-all-start.3) | async-done | bytes 1376288 | tf_op jit(solution)/shard_map/input_plane/all_to_all | solution.py:389
  80.1 2.6 collective-permute-start.11
  82.7 2.0 pick_again.1
  84.6 18.6 %all_to_all.60 = bf16[8,24,3584]{2,1,0:T(8,128)(2,1)} all-to-all(bf16[8,24,3584]{2,1,0:T(8,128)(2,1)S(1)} %bitcast.44), channel_id=1, replica_groups=mesh['pipe'=4,'y'=4,'xh'=2,'z'=4] {'y','xh'}, dimensions={0} | all-to-all | bytes 2752512 | tf_op jit(solution)/shard_map/grad_plane/all_to_all | solution.py:389
  103.3 5.4 %collective-permute-done.10.x1 = bf16[192,3584]{1,0:T(8,128)(2,1)} collective-permute-done((bf16[192,3584]{1,0:T(8,128)(2,1)}, bf16[192,3584]{1,0:T(8,128)(2,1)}, u32[]{:S(2)}, u32[]{:S(2)}) %collective-permute-start.10) | collective-permute-done | bytes 1376288 | tf_op jit(solution)/shard_map/input_ring/ppermute | solution.py:376
  108.7 1.3 slice.28
  111.2 3.3 %collective-permute-start.13 = (bf16[96,3584]{1,0:T(8,128)(2,1)S(1)}, bf16[96,3584]{1,0:T(8,128)(2,1)S(1)}, u32[]{:S(2)}, u32[]{:S(2)}) collective-permute-start(bf16[96,3584]{1,0:T(8,128)(2,1)S(1)} %slice.29), channel_id=1, source_target_pairs={{0,3},{1,0},{2,1},{3,2},{4,7},{5,4},{6,5},{7,6},{8,11},{9,8},{10,9... | collective-permute-start | bytes 2064392 | tf_op jit(solution)/shard_map/input_ring/ppermute | solution.py:376
  116.0 3.2 %collective-permute-start.9 = (bf16[96,1792]{1,0:T(8,128)(2,1)}, bf16[96,1792]{1,0:T(8,128)(2,1)}, u32[]{:S(2)}, u32[]{:S(2)}) collective-permute-start(bf16[96,1792]{1,0:T(8,128)(2,1)} %slice.35), channel_id=1, source_target_pairs={{0,3},{1,0},{2,1},{3,2},{4,7},{5,4},{6,5},{7,6},{8,11},{9,8},{10,9... | collective-permute-start | bytes 1032200 | tf_op jit(solution)/shard_map/saved_ring_b/ppermute | solution.py:376
  120.4 1.7 pad_maximum_fusion
  122.1 7.2 %all-to-all-start.2 = ((bf16[8,96,1792]{2,1,0:T(8,128)(2,1)}), bf16[8,96,1792]{2,1,0:T(8,128)(2,1)}, u32[]{:S(2)}, u32[]{:S(2)}) async-start(bf16[8,96,1792]{2,1,0:T(8,128)(2,1)} %bitcast.57), calls=%async_computation.2 | async-start | bytes 5505024 | tf_op jit(solution)/shard_map/saved_plane_a/all_to_all | solution.py:389
  130.4 3.0 %collective-permute-start.19 = (bf16[192,3584]{1,0:T(8,128)(2,1)}, bf16[192,3584]{1,0:T(8,128)(2,1)}, u32[]{:S(2)}, u32[]{:S(2)}) collective-permute-start(bf16[192,3584]{1,0:T(8,128)(2,1)} %bitcast.23.x0), channel_id=1, source_target_pairs={{0,3},{1,0},{2,1},{3,2},{4,7},{5,4},{6,5},{7,6},{8,11},{9,8},{10,9... | collective-permute-start | bytes 4128776 | tf_op jit(solution)/shard_map/grad_ring/ppermute | solution.py:376
  136.5 12.2 %forward_side.1 = (bf16[192,3584]{1,0:T(8,128)(2,1)S(1)}, bf16[192,3584]{1,0:T(8,128)(2,1)}, bf16[192,3584]{1,0:T(8,128)(2,1)}, bf16[96,3584]{1,0:T(8,128)(2,1)}, bf16[96,3584]{1,0:T(8,128)(2,1)}) custom-call(bf16[192,3584]{1,0:T(8,128)(2,1)} %bitcast.28.x0, bf16[192,3584]{1,0:T(8,128)(2,1)} %collective-permute-done.10.x1, ...), custom_call_target="tpu_custom_call" | custom-call | flops 5637144576000 | bytes 22020096 | tf_op jit(solution)/shard_map/forward_side/pallas_call | solution.py:248
  149.5 7.8 %saved_side.1 = (f32[512,256]{1,0:T(8,128)S(1)}, f32[512,256]{1,0:T(8,128)S(1)}) custom-call(bf16[8,96,1792]{2,1,0:T(8,128)(2,1)} %all-to-all-done.2.refs_0_, bf16[192,1792]{1,0:T(8,128)(2,1)S(1)} %bitcast.47, bf16[192,1792]{1,0:T(8,128)(2,1)S(1)} %copy-done.7, bf16[192,1792]{1,0:T(8,128)(2,1)S(1)} %copy-done.10, ...), custom_call_target="tpu_custom_call" | custom-call | flops 3758096384000 | bytes 12845056 | tf_op jit(solution)/shard_map/saved_side/pallas_call | solution.py:209
  160.7 3.3 %collective-permute-start.21 = (bf16[96,3584]{1,0:T(8,128)(2,1)S(1)}, bf16[96,3584]{1,0:T(8,128)(2,1)S(1)}, u32[]{:S(2)}, u32[]{:S(2)}) collective-permute-start(bf16[96,3584]{1,0:T(8,128)(2,1)S(1)} %slice.31), channel_id=1, source_target_pairs={{0,3},{1,0},{2,1},{3,2},{4,7},{5,4},{6,5},{7,6},{8,11},{9,8},{10,9... | collective-permute-start | bytes 2064392 | tf_op jit(solution)/shard_map/grad_ring/ppermute | solution.py:376
  164.0 3.2 %collective-permute-start.15 = (bf16[96,3584]{1,0:T(8,128)(2,1)}, bf16[96,3584]{1,0:T(8,128)(2,1)}, u32[]{:S(2)}, u32[]{:S(2)}) collective-permute-start(bf16[96,3584]{1,0:T(8,128)(2,1)} %get-tuple-element.66), channel_id=1, source_target_pairs={{0,3},{1,0},{2,1},{3,2},{4,7},{5,4},{6,5},{7,6},{8,11},{9,8},{10,9... | collective-permute-start | bytes 2064392 | tf_op jit(solution)/shard_map/output_far/ppermute | solution.py:376
  167.2 11.0 %collective-permute-done.20.x3 = bf16[96,3584]{1,0:T(8,128)(2,1)S(1)} collective-permute-done((bf16[96,3584]{1,0:T(8,128)(2,1)S(1)}, bf16[96,3584]{1,0:T(8,128)(2,1)S(1)}, u32[]{:S(2)}, u32[]{:S(2)}) %collective-permute-start.20) | collective-permute-done | bytes 688160 | tf_op jit(solution)/shard_map/grad_ring/ppermute | solution.py:376
  178.2 12.2 %backward_side.1 = (bf16[192,3584]{1,0:T(8,128)(2,1)}, bf16[192,3584]{1,0:T(8,128)(2,1)}, bf16[192,3584]{1,0:T(8,128)(2,1)}, bf16[96,3584]{1,0:T(8,128)(2,1)}, bf16[96,3584]{1,0:T(8,128)(2,1)}) custom-call(bf16[192,3584]{1,0:T(8,128)(2,1)} %bitcast.23.x0, bf16[192,3584]{1,0:T(8,128)(2,1)} %collective-permute-done.18.x1, ...), custom_call_target="tpu_custom_call" | custom-call | flops 5637144576000 | bytes 22020096 | tf_op jit(solution)/shard_map/backward_side/pallas_call | solution.py:294
  191.0 3.4 %collective-permute-start.23 = (bf16[96,3584]{1,0:T(8,128)(2,1)}, bf16[96,3584]{1,0:T(8,128)(2,1)}, u32[]{:S(2)}, u32[]{:S(2)}) collective-permute-start(bf16[96,3584]{1,0:T(8,128)(2,1)} %get-tuple-element.79), channel_id=1, source_target_pairs={{0,3},{1,0},{2,1},{3,2},{4,7},{5,4},{6,5},{7,6},{8,11},{9,8},{10,9... | collective-permute-start | bytes 2064392 | tf_op jit(solution)/shard_map/back_far/ppermute | solution.py:376
  194.5 3.4 %near.2 = (bf16[192,3584]{1,0:T(8,128)(2,1)}, bf16[192,3584]{1,0:T(8,128)(2,1)}) custom-call(bf16[192,3584]{1,0:T(8,128)(2,1)} %get-tuple-element.63.left_ref, bf16[192,3584]{1,0:T(8,128)(2,1)} %get-tuple-element.64.right_ref, bf16[96,3584]{1,0:T(8,128)(2,1)} %collective-permute-done.14.lo_ref, bf16[96,3584]{1,0:T(8,128)(2,1)} %collective-permute-done.15.hi_ref), custom_call_target="tpu_custom_call" | custom-call | flops 999999995904 | bytes 6881280 | tf_op jit(solution)/shard_map/output_near/near/pallas_call | solution.py:426
  197.9 1.9 collective-permute-start.17
  199.9 11.2 %collective-permute-done.22.lo_ref = bf16[96,3584]{1,0:T(8,128)(2,1)} collective-permute-done((bf16[96,3584]{1,0:T(8,128)(2,1)}, bf16[96,3584]{1,0:T(8,128)(2,1)}, u32[]{:S(2)}, u32[]{:S(2)}) %collective-permute-start.22) | collective-permute-done | bytes 688160 | tf_op jit(solution)/shard_map/back_far/ppermute | solution.py:376
  211.1 3.2 %near.3 = (bf16[192,3584]{1,0:T(8,128)(2,1)S(1)}, bf16[192,3584]{1,0:T(8,128)(2,1)}) custom-call(bf16[192,3584]{1,0:T(8,128)(2,1)} %get-tuple-element.76.left_ref, bf16[192,3584]{1,0:T(8,128)(2,1)} %get-tuple-element.77.right_ref, bf16[96,3584]{1,0:T(8,128)(2,1)} %collective-permute-done.22.lo_ref, bf16[96,3584]{1,0:T(8,128)(2,1)} %collective-permute-done.23.hi_ref), custom_call_target="tpu_custom_call" | custom-call | flops 999999995904 | bytes 6881280 | tf_op jit(solution)/shard_map/back_near/near/pallas_call | solution.py:426
  214.3 3.3 %collective-permute-start.25 = (bf16[192,3584]{1,0:T(8,128)(2,1)}, bf16[192,3584]{1,0:T(8,128)(2,1)}, u32[]{:S(2)}, u32[]{:S(2)}) collective-permute-start(bf16[192,3584]{1,0:T(8,128)(2,1)} %get-tuple-element.81), channel_id=1, source_target_pairs={{0,3},{1,0},{2,1},{3,2},{4,7},{5,4},{6,5},{7,6},{8,11},{9,8},{10,9... | collective-permute-start | bytes 4128776 | tf_op jit(solution)/shard_map/back_near/ppermute | solution.py:376
  217.6 22.6 %collective-permute-done.17 = bf16[192,3584]{1,0:T(8,128)(2,1)} collective-permute-done((bf16[192,3584]{1,0:T(8,128)(2,1)}, bf16[192,3584]{1,0:T(8,128)(2,1)}, u32[]{:S(2)}, u32[]{:S(2)}) %collective-permute-start.17) | collective-permute-done | bytes 1376288 | tf_op jit(solution)/shard_map/output_near/ppermute | solution.py:376
  240.5 3.3 %add_convert_fusion.1 = bf16[192,3584]{1,0:T(8,128)(2,1)} fusion(bf16[192,3584]{1,0:T(8,128)(2,1)} %collective-permute-done.17, bf16[192,3584]{1,0:T(8,128)(2,1)} %collective-permute-done.16, bf16[192,3584]{1,0:T(8,128)(2,1)S(1)} %get-tuple-element.62), kind=kLoop, calls=%fused_computation.2 | loop fusion | flops 4128768 | bytes 5505024 | tf_op jit(solution)/shard_map/convert_element_type | solution.py:403
  243.9 6.4 %all-to-all-start.4 = ((bf16[8,24,3584]{2,1,0:T(8,128)(2,1)}), bf16[8,24,3584]{2,1,0:T(8,128)(2,1)S(1)}, u32[]{:S(2)}, u32[]{:S(2)}) async-start(bf16[8,24,3584]{2,1,0:T(8,128)(2,1)} %bitcast.58), calls=%async_computation.4 | async-start | bytes 2752512 | tf_op jit(solution)/shard_map/output_plane/all_to_all | solution.py:389
  250.3 2.9 %spread.2 = (bf16[2,128,192]{2,1,0:T(8,128)(2,1)}, f32[128,128]{1,0:T(8,128)}) custom-call(s32[1]{0:T(128)} %bitcast.sel_ref, s32[8]{0:T(128)} %bitcast.53, s32[2,1,128]{2,1,0:T(1,128)} %bitcast.49, f32[2,1,128]{2,1,0:T(1,128)} %bitcast.62), custom_call_target="tpu_custom_call" | custom-call | tf_op jit(solution)/shard_map/spread/pallas_call | solution.py:326
  253.2 2.9 %spread.3 = (bf16[2,128,192]{2,1,0:T(8,128)(2,1)}, f32[128,128]{1,0:T(8,128)}) custom-call(s32[1]{0:T(128)} %bitcast.2.sel_ref, s32[8]{0:T(128)} %bitcast.54, s32[2,1,128]{2,1,0:T(1,128)} %bitcast.50, f32[2,1,128]{2,1,0:T(1,128)} %bitcast.63), custom_call_target="tpu_custom_call" | custom-call | tf_op jit(solution)/shard_map/spread/pallas_call | solution.py:326
  256.1 3.3 %collective-permute-done.25 = bf16[192,3584]{1,0:T(8,128)(2,1)} collective-permute-done((bf16[192,3584]{1,0:T(8,128)(2,1)}, bf16[192,3584]{1,0:T(8,128)(2,1)}, u32[]{:S(2)}, u32[]{:S(2)}) %collective-permute-start.25) | collective-permute-done | bytes 1376288 | tf_op jit(solution)/shard_map/back_near/ppermute | solution.py:376
  259.4 3.8 %add_convert_fusion = bf16[192,3584]{1,0:T(8,128)(2,1)} fusion(bf16[192,3584]{1,0:T(8,128)(2,1)} %collective-permute-done.25, bf16[192,3584]{1,0:T(8,128)(2,1)} %collective-permute-done.24, bf16[192,3584]{1,0:T(8,128)(2,1)} %get-tuple-element.75), kind=kLoop, calls=%fused_computation.1 | loop fusion | flops 4128768 | bytes 5505024 | tf_op jit(solution)/shard_map/convert_element_type | solution.py:403
  263.2 7.2 %all-to-all-start.5 = ((bf16[8,24,3584]{2,1,0:T(8,128)(2,1)}), bf16[8,24,3584]{2,1,0:T(8,128)(2,1)}, u32[]{:S(2)}, u32[]{:S(2)}) async-start(bf16[8,24,3584]{2,1,0:T(8,128)(2,1)} %bitcast.33), calls=%async_computation.5 | async-start | bytes 2752512 | tf_op jit(solution)/shard_map/back_plane/all_to_all | solution.py:389
  270.5 3.0 %mix.2 = bf16[128,7168]{1,0:T(8,128)(2,1)} custom-call(bf16[2,128,192]{2,1,0:T(8,128)(2,1)S(1)} %copy-done.18, f32[128,128]{1,0:T(8,128)S(1)} %copy-done.20, bf16[128,7168]{1,0:T(8,128)(2,1)} %collective-permute-done.2.x_ref, bf16[192,3584]{1,0:T(8,128)(2,1)S(1)} %bitcast.43), custom_call_target="tpu_custom_call" | custom-call | flops 352321536000 | bytes 5046272 | tf_op jit(solution)/shard_map/mix/pallas_call | solution.py:353
  273.4 9.2 %all-to-all-done.5 = bf16[8,24,3584]{2,1,0:T(8,128)(2,1)} async-done(((bf16[8,24,3584]{2,1,0:T(8,128)(2,1)}), bf16[8,24,3584]{2,1,0:T(8,128)(2,1)}, u32[]{:S(2)}, u32[]{:S(2)}) %all-to-all-start.5) | async-done | bytes 1376288 | tf_op jit(solution)/shard_map/back_plane/all_to_all | solution.py:389
  282.6 3.4 %mix.3 = bf16[128,7168]{1,0:T(8,128)(2,1)} custom-call(bf16[2,128,192]{2,1,0:T(8,128)(2,1)S(1)} %copy-done.17, f32[128,128]{1,0:T(8,128)S(1)} %copy-done.19, bf16[128,7168]{1,0:T(8,128)(2,1)} %collective-permute-done.5.lo_ref.hi_ref.x_ref, bf16[192,3584]{1,0:T(8,128)(2,1)} %bitcast.34.refs_0_), custom_call_target="tpu_custom_call" | custom-call | flops 352321536000 | bytes 5046272 | tf_op jit(solution)/shard_map/mix/pallas_call | solution.py:353
  (92 shorter events, 18.5 us)
Async XLA Ops:
  7.0 34.2 %collective-permute-start.2 = (bf16[128,7168]{1,0:T(8,128)(2,1)}, bf16[128,7168]{1,0:T(8,128)(2,1)}, u32[]{:S(2)}, u32[]{:S(2)}) collective-permute-start(bf16[128,7168]{1,0:T(8,128)(2,1)} %dynamic-slice_bitcast_fusion.1), channel_id=1, source_target_pairs={{0,32},{32,64},{64,96},{96,0},{1,33},{33,65},{65,97},{97,1},{2,34}... | collective-permute-start | bytes 5505032 | tf_op jit(solution)/shard_map/ppermute | solution.py:376
  11.2 24.4 %copy-start.3 = (bf16[192,1792]{1,0:T(8,128)(2,1)}, bf16[192,1792]{1,0:T(8,128)(2,1)S(1)}, u32[]{:S(2)}) copy-start(bf16[192,1792]{1,0:T(8,128)(2,1)S(1)} %get-tuple-element.43) | copy-start | bytes 2064388
  11.2 20.3 %collective-permute-start = (bf16[192,1792]{1,0:T(8,128)(2,1)S(1)}, bf16[192,1792]{1,0:T(8,128)(2,1)S(1)}, u32[]{:S(2)}, u32[]{:S(2)}) collective-permute-start(bf16[192,1792]{1,0:T(8,128)(2,1)S(1)} %get-tuple-element.43), channel_id=1, source_target_pairs={{0,1},{1,2},{2,3},{3,0},{4,5},{5,6},{6,7},{7,4},{8,9},{9,10},{10,1... | collective-permute-start | bytes 2064392 | tf_op jit(solution)/shard_map/saved_ring_a/ppermute | solution.py:376
  13.2 18.4 %collective-permute-start.1 = (bf16[192,1792]{1,0:T(8,128)(2,1)S(1)}, bf16[192,1792]{1,0:T(8,128)(2,1)S(1)}, u32[]{:S(2)}, u32[]{:S(2)}) collective-permute-start(bf16[192,1792]{1,0:T(8,128)(2,1)S(1)} %get-tuple-element.43), channel_id=1, source_target_pairs={{0,3},{1,0},{2,1},{3,2},{4,7},{5,4},{6,5},{7,6},{8,11},{9,8},{10,9... | collective-permute-start | bytes 2064392 | tf_op jit(solution)/shard_map/saved_ring_a/ppermute | solution.py:376
  15.3 25.8 %all-to-all-start = ((bf16[8,24,1792]{2,1,0:T(8,128)(2,1)}), bf16[8,24,1792]{2,1,0:T(8,128)(2,1)S(1)}, u32[]{:S(2)}, u32[]{:S(2)}) async-start(bf16[8,24,1792]{2,1,0:T(8,128)(2,1)} %bitcast.14), calls=%async_computation | async-start | bytes 1376256 | tf_op jit(solution)/shard_map/saved_plane_b/all_to_all | solution.py:389
  31.5 9.6 %copy-start.21 = (bf16[192,1792]{1,0:T(8,128)(2,1)}, bf16[192,1792]{1,0:T(8,128)(2,1)S(1)}, u32[]{:S(2)}) copy-start(bf16[192,1792]{1,0:T(8,128)(2,1)S(1)} %collective-permute-done) | copy-start | bytes 2064388
  31.5 9.6 %copy-start.23 = (bf16[192,1792]{1,0:T(8,128)(2,1)}, bf16[192,1792]{1,0:T(8,128)(2,1)S(1)}, u32[]{:S(2)}) copy-start(bf16[192,1792]{1,0:T(8,128)(2,1)S(1)} %collective-permute-done.1) | copy-start | bytes 2064388
  33.6 11.7 %collective-permute-start.3 = (bf16[96,1792]{1,0:T(8,128)(2,1)}, bf16[96,1792]{1,0:T(8,128)(2,1)}, u32[]{:S(2)}, u32[]{:S(2)}) collective-permute-start(bf16[96,1792]{1,0:T(8,128)(2,1)} %slice.32), channel_id=1, source_target_pairs={{0,1},{1,2},{2,3},{3,0},{4,5},{5,6},{6,7},{7,4},{8,9},{9,10},{10,1... | collective-permute-start | bytes 1032200 | tf_op jit(solution)/shard_map/saved_ring_a/ppermute | solution.py:376
  35.6 9.7 %collective-permute-start.4 = (bf16[96,1792]{1,0:T(8,128)(2,1)}, bf16[96,1792]{1,0:T(8,128)(2,1)}, u32[]{:S(2)}, u32[]{:S(2)}) collective-permute-start(bf16[96,1792]{1,0:T(8,128)(2,1)} %slice.33), channel_id=1, source_target_pairs={{0,3},{1,0},{2,1},{3,2},{4,7},{5,4},{6,5},{7,6},{8,11},{9,8},{10,9... | collective-permute-start | bytes 1032200 | tf_op jit(solution)/shard_map/saved_ring_a/ppermute | solution.py:376
  41.1 30.9 %collective-permute-start.5 = (bf16[128,7168]{1,0:T(8,128)(2,1)}, bf16[128,7168]{1,0:T(8,128)(2,1)}, u32[]{:S(2)}, u32[]{:S(2)}) collective-permute-start(bf16[128,7168]{1,0:T(8,128)(2,1)} %dynamic-slice_bitcast_fusion), channel_id=1, source_target_pairs={{0,96},{32,0},{64,32},{96,64},{1,97},{33,1},{65,33},{97,65},{2,98}... | collective-permute-start | bytes 5505032 | tf_op jit(solution)/shard_map/ppermute | solution.py:376
  41.1 4.2 %copy-start = (bf16[8,24,1792]{2,1,0:T(8,128)(2,1)}, bf16[8,24,1792]{2,1,0:T(8,128)(2,1)S(1)}, u32[]{:S(2)}) copy-start(bf16[8,24,1792]{2,1,0:T(8,128)(2,1)S(1)} %all-to-all-done) | copy-start | bytes 2064388
  45.3 7.0 %copy-start.1 = (bf16[8,24,1792]{2,1,0:T(8,128)(2,1)S(1)}, bf16[8,24,1792]{2,1,0:T(8,128)(2,1)}, u32[]{:S(2)}) copy-start(bf16[8,24,1792]{2,1,0:T(8,128)(2,1)} %copy-done) | copy-start | bytes 2064388
  45.3 34.1 %all-to-all-start.3 = ((bf16[8,24,3584]{2,1,0:T(8,128)(2,1)}), bf16[8,24,3584]{2,1,0:T(8,128)(2,1)}, u32[]{:S(2)}, u32[]{:S(2)}) async-start(bf16[8,24,3584]{2,1,0:T(8,128)(2,1)} %bitcast.27), calls=%async_computation.3 | async-start | bytes 2752512 | tf_op jit(solution)/shard_map/input_plane/all_to_all | solution.py:389
  52.3 18.0 %collective-permute-start.6 = (bf16[192,1792]{1,0:T(8,128)(2,1)S(1)}, bf16[192,1792]{1,0:T(8,128)(2,1)S(1)}, u32[]{:S(2)}, u32[]{:S(2)}) collective-permute-start(bf16[192,1792]{1,0:T(8,128)(2,1)S(1)} %bitcast.45), channel_id=1, source_target_pairs={{0,1},{1,2},{2,3},{3,0},{4,5},{5,6},{6,7},{7,4},{8,9},{9,10},{10,1... | collective-permute-start | bytes 2064392 | tf_op jit(solution)/shard_map/saved_ring_b/ppermute | solution.py:376
  53.9 16.4 %collective-permute-start.7 = (bf16[192,1792]{1,0:T(8,128)(2,1)S(1)}, bf16[192,1792]{1,0:T(8,128)(2,1)S(1)}, u32[]{:S(2)}, u32[]{:S(2)}) collective-permute-start(bf16[192,1792]{1,0:T(8,128)(2,1)S(1)} %bitcast.46), channel_id=1, source_target_pairs={{0,3},{1,0},{2,1},{3,2},{4,7},{5,4},{6,5},{7,6},{8,11},{9,8},{10,9... | collective-permute-start | bytes 2064392 | tf_op jit(solution)/shard_map/saved_ring_b/ppermute | solution.py:376
  79.4 29.2 %collective-permute-start.10 = (bf16[192,3584]{1,0:T(8,128)(2,1)}, bf16[192,3584]{1,0:T(8,128)(2,1)}, u32[]{:S(2)}, u32[]{:S(2)}) collective-permute-start(bf16[192,3584]{1,0:T(8,128)(2,1)} %bitcast.28.x0), channel_id=1, source_target_pairs={{0,1},{1,2},{2,3},{3,0},{4,5},{5,6},{6,7},{7,4},{8,9},{9,10},{10,1... | collective-permute-start | bytes 4128776 | tf_op jit(solution)/shard_map/input_ring/ppermute | solution.py:376
  80.1 28.5 %collective-permute-start.11 = (bf16[192,3584]{1,0:T(8,128)(2,1)}, bf16[192,3584]{1,0:T(8,128)(2,1)}, u32[]{:S(2)}, u32[]{:S(2)}) collective-permute-start(bf16[192,3584]{1,0:T(8,128)(2,1)} %bitcast.28.x0), channel_id=1, source_target_pairs={{0,3},{1,0},{2,1},{3,2},{4,7},{5,4},{6,5},{7,6},{8,11},{9,8},{10,9... | collective-permute-start | bytes 4128776 | tf_op jit(solution)/shard_map/input_ring/ppermute | solution.py:376
  108.7 5.8 %copy-start.6 = (bf16[192,1792]{1,0:T(8,128)(2,1)S(1)}, bf16[192,1792]{1,0:T(8,128)(2,1)}, u32[]{:S(2)}) copy-start(bf16[192,1792]{1,0:T(8,128)(2,1)} %copy-done.5) | copy-start | bytes 2064388
  108.7 6.6 %copy-start.9 = (bf16[192,1792]{1,0:T(8,128)(2,1)S(1)}, bf16[192,1792]{1,0:T(8,128)(2,1)}, u32[]{:S(2)}) copy-start(bf16[192,1792]{1,0:T(8,128)(2,1)} %copy-done.8) | copy-start | bytes 2064388
  109.9 19.7 %collective-permute-start.12 = (bf16[96,3584]{1,0:T(8,128)(2,1)S(1)}, bf16[96,3584]{1,0:T(8,128)(2,1)S(1)}, u32[]{:S(2)}, u32[]{:S(2)}) collective-permute-start(bf16[96,3584]{1,0:T(8,128)(2,1)S(1)} %slice.28), channel_id=1, source_target_pairs={{0,1},{1,2},{2,3},{3,0},{4,5},{5,6},{6,7},{7,4},{8,9},{9,10},{10,1... | collective-permute-start | bytes 2064392 | tf_op jit(solution)/shard_map/input_ring/ppermute | solution.py:376
  111.1 9.2 %copy-start.4 = (bf16[192,1792]{1,0:T(8,128)(2,1)S(1)}, bf16[192,1792]{1,0:T(8,128)(2,1)}, u32[]{:S(2)}) copy-start(bf16[192,1792]{1,0:T(8,128)(2,1)} %copy-done.3) | copy-start | bytes 2064388
  111.2 9.2 %copy-start.22 = (bf16[192,1792]{1,0:T(8,128)(2,1)S(1)}, bf16[192,1792]{1,0:T(8,128)(2,1)}, u32[]{:S(2)}) copy-start(bf16[192,1792]{1,0:T(8,128)(2,1)} %copy-done.21) | copy-start | bytes 2064388
  111.2 9.2 %copy-start.24 = (bf16[192,1792]{1,0:T(8,128)(2,1)S(1)}, bf16[192,1792]{1,0:T(8,128)(2,1)}, u32[]{:S(2)}) copy-start(bf16[192,1792]{1,0:T(8,128)(2,1)} %copy-done.23) | copy-start | bytes 2064388
  111.2 22.3 %collective-permute-start.13 = (bf16[96,3584]{1,0:T(8,128)(2,1)S(1)}, bf16[96,3584]{1,0:T(8,128)(2,1)S(1)}, u32[]{:S(2)}, u32[]{:S(2)}) collective-permute-start(bf16[96,3584]{1,0:T(8,128)(2,1)S(1)} %slice.29), channel_id=1, source_target_pairs={{0,3},{1,0},{2,1},{3,2},{4,7},{5,4},{6,5},{7,6},{8,11},{9,8},{10,9... | collective-permute-start | bytes 2064392 | tf_op jit(solution)/shard_map/input_ring/ppermute | solution.py:376
  115.2 33.4 %collective-permute-start.8 = (bf16[96,1792]{1,0:T(8,128)(2,1)}, bf16[96,1792]{1,0:T(8,128)(2,1)}, u32[]{:S(2)}, u32[]{:S(2)}) collective-permute-start(bf16[96,1792]{1,0:T(8,128)(2,1)} %slice.34), channel_id=1, source_target_pairs={{0,1},{1,2},{2,3},{3,0},{4,5},{5,6},{6,7},{7,4},{8,9},{9,10},{10,1... | collective-permute-start | bytes 1032200 | tf_op jit(solution)/shard_map/saved_ring_b/ppermute | solution.py:376
  116.0 32.7 %collective-permute-start.9 = (bf16[96,1792]{1,0:T(8,128)(2,1)}, bf16[96,1792]{1,0:T(8,128)(2,1)}, u32[]{:S(2)}, u32[]{:S(2)}) collective-permute-start(bf16[96,1792]{1,0:T(8,128)(2,1)} %slice.35), channel_id=1, source_target_pairs={{0,3},{1,0},{2,1},{3,2},{4,7},{5,4},{6,5},{7,6},{8,11},{9,8},{10,9... | collective-permute-start | bytes 1032200 | tf_op jit(solution)/shard_map/saved_ring_b/ppermute | solution.py:376
  122.1 36.2 %collective-permute-start.18 = (bf16[192,3584]{1,0:T(8,128)(2,1)}, bf16[192,3584]{1,0:T(8,128)(2,1)}, u32[]{:S(2)}, u32[]{:S(2)}) collective-permute-start(bf16[192,3584]{1,0:T(8,128)(2,1)} %bitcast.23.x0), channel_id=1, source_target_pairs={{0,1},{1,2},{2,3},{3,0},{4,5},{5,6},{6,7},{7,4},{8,9},{9,10},{10,1... | collective-permute-start | bytes 4128776 | tf_op jit(solution)/shard_map/grad_ring/ppermute | solution.py:376
  122.1 27.4 %all-to-all-start.2 = ((bf16[8,96,1792]{2,1,0:T(8,128)(2,1)}), bf16[8,96,1792]{2,1,0:T(8,128)(2,1)}, u32[]{:S(2)}, u32[]{:S(2)}) async-start(bf16[8,96,1792]{2,1,0:T(8,128)(2,1)} %bitcast.57), calls=%async_computation.2 | async-start | bytes 5505024 | tf_op jit(solution)/shard_map/saved_plane_a/all_to_all | solution.py:389
  130.4 27.9 %collective-permute-start.19 = (bf16[192,3584]{1,0:T(8,128)(2,1)}, bf16[192,3584]{1,0:T(8,128)(2,1)}, u32[]{:S(2)}, u32[]{:S(2)}) collective-permute-start(bf16[192,3584]{1,0:T(8,128)(2,1)} %bitcast.23.x0), channel_id=1, source_target_pairs={{0,3},{1,0},{2,1},{3,2},{4,7},{5,4},{6,5},{7,6},{8,11},{9,8},{10,9... | collective-permute-start | bytes 4128776 | tf_op jit(solution)/shard_map/grad_ring/ppermute | solution.py:376
  136.5 13.1 %copy-start.2 = (bf16[8,24,1792]{2,1,0:T(8,128)(2,1)S(1)}, bf16[8,24,1792]{2,1,0:T(8,128)(2,1)}, u32[]{:S(2)}) copy-start(bf16[8,24,1792]{2,1,0:T(8,128)(2,1)} %copy-done) | copy-start | bytes 2064388
  136.5 13.1 %copy-start.7 = (bf16[192,1792]{1,0:T(8,128)(2,1)S(1)}, bf16[192,1792]{1,0:T(8,128)(2,1)}, u32[]{:S(2)}) copy-start(bf16[192,1792]{1,0:T(8,128)(2,1)} %copy-done.5) | copy-start | bytes 2064388
  136.5 13.1 %copy-start.10 = (bf16[192,1792]{1,0:T(8,128)(2,1)S(1)}, bf16[192,1792]{1,0:T(8,128)(2,1)}, u32[]{:S(2)}) copy-start(bf16[192,1792]{1,0:T(8,128)(2,1)} %copy-done.8) | copy-start | bytes 2064388
  159.5 18.7 %collective-permute-start.20 = (bf16[96,3584]{1,0:T(8,128)(2,1)S(1)}, bf16[96,3584]{1,0:T(8,128)(2,1)S(1)}, u32[]{:S(2)}, u32[]{:S(2)}) collective-permute-start(bf16[96,3584]{1,0:T(8,128)(2,1)S(1)} %slice.30), channel_id=1, source_target_pairs={{0,1},{1,2},{2,3},{3,0},{4,5},{5,6},{6,7},{7,4},{8,9},{9,10},{10,1... | collective-permute-start | bytes 2064392 | tf_op jit(solution)/shard_map/grad_ring/ppermute | solution.py:376
  160.7 17.5 %collective-permute-start.21 = (bf16[96,3584]{1,0:T(8,128)(2,1)S(1)}, bf16[96,3584]{1,0:T(8,128)(2,1)S(1)}, u32[]{:S(2)}, u32[]{:S(2)}) collective-permute-start(bf16[96,3584]{1,0:T(8,128)(2,1)S(1)} %slice.31), channel_id=1, source_target_pairs={{0,3},{1,0},{2,1},{3,2},{4,7},{5,4},{6,5},{7,6},{8,11},{9,8},{10,9... | collective-permute-start | bytes 2064392 | tf_op jit(solution)/shard_map/grad_ring/ppermute | solution.py:376
  164.0 30.5 %collective-permute-start.14 = (bf16[96,3584]{1,0:T(8,128)(2,1)}, bf16[96,3584]{1,0:T(8,128)(2,1)}, u32[]{:S(2)}, u32[]{:S(2)}) collective-permute-start(bf16[96,3584]{1,0:T(8,128)(2,1)} %get-tuple-element.65), channel_id=1, source_target_pairs={{0,1},{1,2},{2,3},{3,0},{4,5},{5,6},{6,7},{7,4},{8,9},{9,10},{10,1... | collective-permute-start | bytes 2064392 | tf_op jit(solution)/shard_map/output_far/ppermute | solution.py:376
  164.0 30.5 %collective-permute-start.15 = (bf16[96,3584]{1,0:T(8,128)(2,1)}, bf16[96,3584]{1,0:T(8,128)(2,1)}, u32[]{:S(2)}, u32[]{:S(2)}) collective-permute-start(bf16[96,3584]{1,0:T(8,128)(2,1)} %get-tuple-element.66), channel_id=1, source_target_pairs={{0,3},{1,0},{2,1},{3,2},{4,7},{5,4},{6,5},{7,6},{8,11},{9,8},{10,9... | collective-permute-start | bytes 2064392 | tf_op jit(solution)/shard_map/output_far/ppermute | solution.py:376
  190.4 20.6 %collective-permute-start.22 = (bf16[96,3584]{1,0:T(8,128)(2,1)}, bf16[96,3584]{1,0:T(8,128)(2,1)}, u32[]{:S(2)}, u32[]{:S(2)}) collective-permute-start(bf16[96,3584]{1,0:T(8,128)(2,1)} %get-tuple-element.78), channel_id=1, source_target_pairs={{0,1},{1,2},{2,3},{3,0},{4,5},{5,6},{6,7},{7,4},{8,9},{9,10},{10,1... | collective-permute-start | bytes 2064392 | tf_op jit(solution)/shard_map/back_far/ppermute | solution.py:376
  191.0 20.0 %collective-permute-start.23 = (bf16[96,3584]{1,0:T(8,128)(2,1)}, bf16[96,3584]{1,0:T(8,128)(2,1)}, u32[]{:S(2)}, u32[]{:S(2)}) collective-permute-start(bf16[96,3584]{1,0:T(8,128)(2,1)} %get-tuple-element.79), channel_id=1, source_target_pairs={{0,3},{1,0},{2,1},{3,2},{4,7},{5,4},{6,5},{7,6},{8,11},{9,8},{10,9... | collective-permute-start | bytes 2064392 | tf_op jit(solution)/shard_map/back_far/ppermute | solution.py:376
  197.9 42.3 %collective-permute-start.17 = (bf16[192,3584]{1,0:T(8,128)(2,1)}, bf16[192,3584]{1,0:T(8,128)(2,1)}, u32[]{:S(2)}, u32[]{:S(2)}) collective-permute-start(bf16[192,3584]{1,0:T(8,128)(2,1)} %get-tuple-element.68), channel_id=1, source_target_pairs={{0,3},{1,0},{2,1},{3,2},{4,7},{5,4},{6,5},{7,6},{8,11},{9,8},{10,9... | collective-permute-start | bytes 4128776 | tf_op jit(solution)/shard_map/output_near/ppermute | solution.py:376
  199.8 40.7 %collective-permute-start.16 = (bf16[192,3584]{1,0:T(8,128)(2,1)}, bf16[192,3584]{1,0:T(8,128)(2,1)}, u32[]{:S(2)}, u32[]{:S(2)}) collective-permute-start(bf16[192,3584]{1,0:T(8,128)(2,1)} %get-tuple-element.67), channel_id=1, source_target_pairs={{0,1},{1,2},{2,3},{3,0},{4,5},{5,6},{6,7},{7,4},{8,9},{9,10},{10,1... | collective-permute-start | bytes 4128776 | tf_op jit(solution)/shard_map/output_near/ppermute | solution.py:376
  214.3 45.2 %collective-permute-start.25 = (bf16[192,3584]{1,0:T(8,128)(2,1)}, bf16[192,3584]{1,0:T(8,128)(2,1)}, u32[]{:S(2)}, u32[]{:S(2)}) collective-permute-start(bf16[192,3584]{1,0:T(8,128)(2,1)} %get-tuple-element.81), channel_id=1, source_target_pairs={{0,3},{1,0},{2,1},{3,2},{4,7},{5,4},{6,5},{7,6},{8,11},{9,8},{10,9... | collective-permute-start | bytes 4128776 | tf_op jit(solution)/shard_map/back_near/ppermute | solution.py:376
  217.6 41.9 %collective-permute-start.24 = (bf16[192,3584]{1,0:T(8,128)(2,1)S(1)}, bf16[192,3584]{1,0:T(8,128)(2,1)}, u32[]{:S(2)}, u32[]{:S(2)}) collective-permute-start(bf16[192,3584]{1,0:T(8,128)(2,1)S(1)} %get-tuple-element.80), channel_id=1, source_target_pairs={{0,1},{1,2},{2,3},{3,0},{4,5},{5,6},{6,7},{7,4},{8,9},{9,10},{10,1... | collective-permute-start | bytes 4128776 | tf_op jit(solution)/shard_map/back_near/ppermute | solution.py:376
  243.9 19.4 %all-to-all-start.4 = ((bf16[8,24,3584]{2,1,0:T(8,128)(2,1)}), bf16[8,24,3584]{2,1,0:T(8,128)(2,1)S(1)}, u32[]{:S(2)}, u32[]{:S(2)}) async-start(bf16[8,24,3584]{2,1,0:T(8,128)(2,1)} %bitcast.58), calls=%async_computation.4 | async-start | bytes 2752512 | tf_op jit(solution)/shard_map/output_plane/all_to_all | solution.py:389
  263.2 7.2 %copy-start.18 = (bf16[2,128,192]{2,1,0:T(8,128)(2,1)S(1)}, bf16[2,128,192]{2,1,0:T(8,128)(2,1)}, u32[]{:S(2)}) copy-start(bf16[2,128,192]{2,1,0:T(8,128)(2,1)} %get-tuple-element.58.spread_ref) | copy-start | bytes 294916
  263.2 7.2 %copy-start.20 = (f32[128,128]{1,0:T(8,128)S(1)}, f32[128,128]{1,0:T(8,128)}, u32[]{:S(2)}) copy-start(f32[128,128]{1,0:T(8,128)} %get-tuple-element.59.prob_ref) | copy-start | bytes 196612
  263.2 19.4 %all-to-all-start.5 = ((bf16[8,24,3584]{2,1,0:T(8,128)(2,1)}), bf16[8,24,3584]{2,1,0:T(8,128)(2,1)}, u32[]{:S(2)}, u32[]{:S(2)}) async-start(bf16[8,24,3584]{2,1,0:T(8,128)(2,1)} %bitcast.33), calls=%async_computation.5 | async-start | bytes 2752512 | tf_op jit(solution)/shard_map/back_plane/all_to_all | solution.py:389
  270.5 12.2 %copy-start.17 = (bf16[2,128,192]{2,1,0:T(8,128)(2,1)S(1)}, bf16[2,128,192]{2,1,0:T(8,128)(2,1)}, u32[]{:S(2)}) copy-start(bf16[2,128,192]{2,1,0:T(8,128)(2,1)} %get-tuple-element.69.spread_ref) | copy-start | bytes 294916
  270.5 12.2 %copy-start.19 = (f32[128,128]{1,0:T(8,128)S(1)}, f32[128,128]{1,0:T(8,128)}, u32[]{:S(2)}) copy-start(f32[128,128]{1,0:T(8,128)} %get-tuple-element.70.prob_ref) | copy-start | bytes 196612
  (8 other events, 11.4 us)

commit v5 on v4

--- a/solution.py
+++ b/solution.py
@@ -106,15 +106,15 @@
 
 
 def pick_again(picker, x):
-    tile = HALF // 2
+    tile = HALF
     return pl.pallas_call(
         pick_again_kernel,
         out_shape=jax.ShapeDtypeStruct((ROWS, HALF), BF16),
-        grid=(2,),
+        grid=(1,),
         in_specs=[
             pl.BlockSpec((ROWS, 2 * TOK), lambda i: (0, 0)),
             pl.BlockSpec((TOK, tile), lambda i: (0, i)),
-            pl.BlockSpec((TOK, tile), lambda i: (0, i + 2)),
+            pl.BlockSpec((TOK, tile), lambda i: (0, i + 1)),
         ],
         out_specs=pl.BlockSpec((ROWS, tile), lambda i: (0, i)),
         compiler_params=pltpu.CompilerParams(vmem_limit_bytes=VMEM),

time: 290 us -> 290 us (level)
  no operation moved by 1% of the time
where the time goes in v5:
time: 290 us; the launch traced here: 286 us
  waiting for transfers between devices  96.9 us (33%)
  starting transfers between devices  73.7 us (25%)
  Pallas kernels  61.4 us (21%)
  local copies, waits for them, and re-layouts  20.6 us (7%)
  blocking collectives  18.6 us (6%)
  other arithmetic  9.97 us (3%)
  between operations  4.83 us (2%)
    ppermute x26, waiting for transfers between devices, shift(): return lax.ppermute(x, axis, [(i, (i + by) % n) for i in range(n)])  79.4 us
    ppermute x26, starting transfers between devices, shift(): return lax.ppermute(x, axis, [(i, (i + by) % n) for i in range(n)])  39.6 us
    all_to_all x5, starting transfers between devices, exchange(): return lax.all_to_all(x, ('y', 'xh'), 0, 0, tiled=True)  34.2 us
    all_to_all x1, blocking collectives, exchange(): return lax.all_to_all(x, ('y', 'xh'), 0, 0, tiled=True)  18.6 us
    all_to_all x5, waiting for transfers between devices, exchange(): return lax.all_to_all(x, ('y', 'xh'), 0, 0, tiled=True)  17.4 us
    pallas_call x1, Pallas kernels, backward_side(): pl.pallas_call(backward_kernel, out_shape=tuple((jax.ShapeDtypeStruct((n,...  12.2 us
    pallas_call x1, Pallas kernels, forward_side(): pl.pallas_call(forward_kernel, out_shape=tuple((jax.ShapeDtypeStruct((n,...  12.2 us
    pallas_call x2, Pallas kernels, pick(): pl.pallas_call(pick_kernel, out_shape=shapes + [jax.ShapeDtypeStruct((ROW...  8.41 us
  transfers between devices with their start and end apart: 31, of which 13 were waited for; matrix products, arithmetic and copies ran while one was open for 6% of the time, Pallas kernels for 20%

profile of v5, /device:TPU:18, one launch (start us, length us, event | category | flops | bytes accessed | tf_op | source)
XLA Modules:
  0.0 286.0 jit_solution(6852677859720820078)
XLA Ops:
  0.7 1.5 constant_dynamic-slice_fusion.2
  4.1 2.9 dynamic-slice_bitcast_fusion.1
  7.0 4.2 %pick.2 = (bf16[192,1792]{1,0:T(8,128)(2,1)S(1)}, bf16[192,1792]{1,0:T(8,128)(2,1)}, bf16[192,256]{1,0:T(8,128)(2,1)S(1)}) custom-call(s32[1]{0:T(128)} %bitcast.2.sel_ref, s32[8]{0:T(128)S(1)} %bitcast.55, s32[2,1,128]{2,1,0:T(1,128)S(1)} %bitcast.51, bf16[2,128,7168]{2,1,0:T(8,128)(2,1)} %bitcast.64, bf16[2,128,7168]{2,1,0:T(8,128)(2,1)} %bitcast.65), custom_call_target="tpu_custom_call" | custom-call | flops 352321536000 | bytes 3211264 | tf_op jit(solution)/shard_map/pick/pallas_call | solution.py:84
  11.2 1.9 collective-permute-start
  13.2 2.1 collective-permute-start.1
  15.3 6.4 %all-to-all-start = ((bf16[8,24,1792]{2,1,0:T(8,128)(2,1)}), bf16[8,24,1792]{2,1,0:T(8,128)(2,1)S(1)}, u32[]{:S(2)}, u32[]{:S(2)}) async-start(bf16[8,24,1792]{2,1,0:T(8,128)(2,1)} %bitcast.14), calls=%async_computation | async-start | bytes 1376256 | tf_op jit(solution)/shard_map/saved_plane_b/all_to_all | solution.py:389
  21.7 9.9 %collective-permute-done = bf16[192,1792]{1,0:T(8,128)(2,1)S(1)} collective-permute-done((bf16[192,1792]{1,0:T(8,128)(2,1)S(1)}, bf16[192,1792]{1,0:T(8,128)(2,1)S(1)}, u32[]{:S(2)}, u32[]{:S(2)}) %collective-permute-start) | collective-permute-done | bytes 688160 | tf_op jit(solution)/shard_map/saved_ring_a/ppermute | solution.py:376
  35.6 2.0 collective-permute-start.4
  38.3 2.8 dynamic-slice_bitcast_fusion
  41.1 4.2 %pick.3 = (bf16[192,3584]{1,0:T(8,128)(2,1)}, bf16[192,256]{1,0:T(8,128)(2,1)}) custom-call(s32[1]{0:T(128)} %bitcast.sel_ref, s32[8]{0:T(128)S(1)} %bitcast.56, s32[2,1,128]{2,1,0:T(1,128)S(1)} %bitcast.52, bf16[1,128,7168]{2,1,0:T(8,128)(2,1)} %bitcast.16.lo_ref.hi_ref, bf16[1,128,7168]{2,1,0:T(8,128)(2,1)} %bitcast.16.lo_ref.hi_ref), custom_call_target="tpu_custom_call" | custom-call | flops 352321536000 | bytes 3211264 | tf_op jit(solution)/shard_map/pick/pallas_call | solution.py:84
  45.3 7.0 %all-to-all-start.3 = ((bf16[8,24,3584]{2,1,0:T(8,128)(2,1)}), bf16[8,24,3584]{2,1,0:T(8,128)(2,1)}, u32[]{:S(2)}, u32[]{:S(2)}) async-start(bf16[8,24,3584]{2,1,0:T(8,128)(2,1)} %bitcast.27), calls=%async_computation.3 | async-start | bytes 2752512 | tf_op jit(solution)/shard_map/input_plane/all_to_all | solution.py:389
  52.3 1.6 collective-permute-start.6
  53.9 1.8 collective-permute-start.7
  55.7 14.6 %collective-permute-done.6.refs_2_ = bf16[192,1792]{1,0:T(8,128)(2,1)S(1)} collective-permute-done((bf16[192,1792]{1,0:T(8,128)(2,1)S(1)}, bf16[192,1792]{1,0:T(8,128)(2,1)S(1)}, u32[]{:S(2)}, u32[]{:S(2)}) %collective-permute-start.6) | collective-permute-done | bytes 688160 | tf_op jit(solution)/shard_map/saved_ring_b/ppermute | solution.py:376
  72.0 7.4 %all-to-all-done.3 = bf16[8,24,3584]{2,1,0:T(8,128)(2,1)} async-done(((bf16[8,24,3584]{2,1,0:T(8,128)(2,1)}), bf16[8,24,3584]{2,1,0:T(8,128)(2,1)}, u32[]{:S(2)}, u32[]{:S(2)}) %all-to-all-start.3) | async-done | bytes 1376288 | tf_op jit(solution)/shard_map/input_plane/all_to_all | solution.py:389
  80.1 2.6 collective-permute-start.11
  82.7 2.0 pick_again.1
  84.6 18.6 %all_to_all.60 = bf16[8,24,3584]{2,1,0:T(8,128)(2,1)} all-to-all(bf16[8,24,3584]{2,1,0:T(8,128)(2,1)S(1)} %bitcast.44), channel_id=1, replica_groups=mesh['pipe'=4,'y'=4,'xh'=2,'z'=4] {'y','xh'}, dimensions={0} | all-to-all | bytes 2752512 | tf_op jit(solution)/shard_map/grad_plane/all_to_all | solution.py:389
  103.3 5.4 %collective-permute-done.10.x1 = bf16[192,3584]{1,0:T(8,128)(2,1)} collective-permute-done((bf16[192,3584]{1,0:T(8,128)(2,1)}, bf16[192,3584]{1,0:T(8,128)(2,1)}, u32[]{:S(2)}, u32[]{:S(2)}) %collective-permute-start.10) | collective-permute-done | bytes 1376288 | tf_op jit(solution)/shard_map/input_ring/ppermute | solution.py:376
  108.7 1.3 slice.28
  111.2 3.3 %collective-permute-start.13 = (bf16[96,3584]{1,0:T(8,128)(2,1)S(1)}, bf16[96,3584]{1,0:T(8,128)(2,1)S(1)}, u32[]{:S(2)}, u32[]{:S(2)}) collective-permute-start(bf16[96,3584]{1,0:T(8,128)(2,1)S(1)} %slice.29), channel_id=1, source_target_pairs={{0,3},{1,0},{2,1},{3,2},{4,7},{5,4},{6,5},{7,6},{8,11},{9,8},{10,9... | collective-permute-start | bytes 2064392 | tf_op jit(solution)/shard_map/input_ring/ppermute | solution.py:376
  116.0 3.2 %collective-permute-start.9 = (bf16[96,1792]{1,0:T(8,128)(2,1)}, bf16[96,1792]{1,0:T(8,128)(2,1)}, u32[]{:S(2)}, u32[]{:S(2)}) collective-permute-start(bf16[96,1792]{1,0:T(8,128)(2,1)} %slice.35), channel_id=1, source_target_pairs={{0,3},{1,0},{2,1},{3,2},{4,7},{5,4},{6,5},{7,6},{8,11},{9,8},{10,9... | collective-permute-start | bytes 1032200 | tf_op jit(solution)/shard_map/saved_ring_b/ppermute | solution.py:376
  120.4 1.7 pad_maximum_fusion
  122.1 7.2 %all-to-all-start.2 = ((bf16[8,96,1792]{2,1,0:T(8,128)(2,1)}), bf16[8,96,1792]{2,1,0:T(8,128)(2,1)}, u32[]{:S(2)}, u32[]{:S(2)}) async-start(bf16[8,96,1792]{2,1,0:T(8,128)(2,1)} %bitcast.57), calls=%async_computation.2 | async-start | bytes 5505024 | tf_op jit(solution)/shard_map/saved_plane_a/all_to_all | solution.py:389
  130.4 3.0 %collective-permute-start.19 = (bf16[192,3584]{1,0:T(8,128)(2,1)}, bf16[192,3584]{1,0:T(8,128)(2,1)}, u32[]{:S(2)}, u32[]{:S(2)}) collective-permute-start(bf16[192,3584]{1,0:T(8,128)(2,1)} %bitcast.23.x0), channel_id=1, source_target_pairs={{0,3},{1,0},{2,1},{3,2},{4,7},{5,4},{6,5},{7,6},{8,11},{9,8},{10,9... | collective-permute-start | bytes 4128776 | tf_op jit(solution)/shard_map/grad_ring/ppermute | solution.py:376
  136.5 12.2 %forward_side.1 = (bf16[192,3584]{1,0:T(8,128)(2,1)S(1)}, bf16[192,3584]{1,0:T(8,128)(2,1)}, bf16[192,3584]{1,0:T(8,128)(2,1)}, bf16[96,3584]{1,0:T(8,128)(2,1)}, bf16[96,3584]{1,0:T(8,128)(2,1)}) custom-call(bf16[192,3584]{1,0:T(8,128)(2,1)} %bitcast.28.x0, bf16[192,3584]{1,0:T(8,128)(2,1)} %collective-permute-done.10.x1, ...), custom_call_target="tpu_custom_call" | custom-call | flops 5637144576000 | bytes 22020096 | tf_op jit(solution)/shard_map/forward_side/pallas_call | solution.py:248
  149.5 7.8 %saved_side.1 = (f32[512,256]{1,0:T(8,128)S(1)}, f32[512,256]{1,0:T(8,128)S(1)}) custom-call(bf16[8,96,1792]{2,1,0:T(8,128)(2,1)} %all-to-all-done.2.refs_0_, bf16[192,1792]{1,0:T(8,128)(2,1)S(1)} %bitcast.47, bf16[192,1792]{1,0:T(8,128)(2,1)S(1)} %copy-done.7, bf16[192,1792]{1,0:T(8,128)(2,1)S(1)} %copy-done.10, ...), custom_call_target="tpu_custom_call" | custom-call | flops 3758096384000 | bytes 12845056 | tf_op jit(solution)/shard_map/saved_side/pallas_call | solution.py:209
  160.7 3.3 %collective-permute-start.21 = (bf16[96,3584]{1,0:T(8,128)(2,1)S(1)}, bf16[96,3584]{1,0:T(8,128)(2,1)S(1)}, u32[]{:S(2)}, u32[]{:S(2)}) collective-permute-start(bf16[96,3584]{1,0:T(8,128)(2,1)S(1)} %slice.31), channel_id=1, source_target_pairs={{0,3},{1,0},{2,1},{3,2},{4,7},{5,4},{6,5},{7,6},{8,11},{9,8},{10,9... | collective-permute-start | bytes 2064392 | tf_op jit(solution)/shard_map/grad_ring/ppermute | solution.py:376
  164.0 3.2 %collective-permute-start.15 = (bf16[96,3584]{1,0:T(8,128)(2,1)}, bf16[96,3584]{1,0:T(8,128)(2,1)}, u32[]{:S(2)}, u32[]{:S(2)}) collective-permute-start(bf16[96,3584]{1,0:T(8,128)(2,1)} %get-tuple-element.66), channel_id=1, source_target_pairs={{0,3},{1,0},{2,1},{3,2},{4,7},{5,4},{6,5},{7,6},{8,11},{9,8},{10,9... | collective-permute-start | bytes 2064392 | tf_op jit(solution)/shard_map/output_far/ppermute | solution.py:376
  167.2 11.0 %collective-permute-done.20.x3 = bf16[96,3584]{1,0:T(8,128)(2,1)S(1)} collective-permute-done((bf16[96,3584]{1,0:T(8,128)(2,1)S(1)}, bf16[96,3584]{1,0:T(8,128)(2,1)S(1)}, u32[]{:S(2)}, u32[]{:S(2)}) %collective-permute-start.20) | collective-permute-done | bytes 688160 | tf_op jit(solution)/shard_map/grad_ring/ppermute | solution.py:376
  178.2 12.2 %backward_side.1 = (bf16[192,3584]{1,0:T(8,128)(2,1)}, bf16[192,3584]{1,0:T(8,128)(2,1)}, bf16[192,3584]{1,0:T(8,128)(2,1)}, bf16[96,3584]{1,0:T(8,128)(2,1)}, bf16[96,3584]{1,0:T(8,128)(2,1)}) custom-call(bf16[192,3584]{1,0:T(8,128)(2,1)} %bitcast.23.x0, bf16[192,3584]{1,0:T(8,128)(2,1)} %collective-permute-done.18.x1, ...), custom_call_target="tpu_custom_call" | custom-call | flops 5637144576000 | bytes 22020096 | tf_op jit(solution)/shard_map/backward_side/pallas_call | solution.py:294
  191.0 3.4 %collective-permute-start.23 = (bf16[96,3584]{1,0:T(8,128)(2,1)}, bf16[96,3584]{1,0:T(8,128)(2,1)}, u32[]{:S(2)}, u32[]{:S(2)}) collective-permute-start(bf16[96,3584]{1,0:T(8,128)(2,1)} %get-tuple-element.79), channel_id=1, source_target_pairs={{0,3},{1,0},{2,1},{3,2},{4,7},{5,4},{6,5},{7,6},{8,11},{9,8},{10,9... | collective-permute-start | bytes 2064392 | tf_op jit(solution)/shard_map/back_far/ppermute | solution.py:376
  194.5 3.4 %near.2 = (bf16[192,3584]{1,0:T(8,128)(2,1)}, bf16[192,3584]{1,0:T(8,128)(2,1)}) custom-call(bf16[192,3584]{1,0:T(8,128)(2,1)} %get-tuple-element.63.left_ref, bf16[192,3584]{1,0:T(8,128)(2,1)} %get-tuple-element.64.right_ref, bf16[96,3584]{1,0:T(8,128)(2,1)} %collective-permute-done.14.lo_ref, bf16[96,3584]{1,0:T(8,128)(2,1)} %collective-permute-done.15.hi_ref), custom_call_target="tpu_custom_call" | custom-call | flops 999999995904 | bytes 6881280 | tf_op jit(solution)/shard_map/output_near/near/pallas_call | solution.py:426
  197.9 1.9 collective-permute-start.17
  199.9 11.2 %collective-permute-done.22.lo_ref = bf16[96,3584]{1,0:T(8,128)(2,1)} collective-permute-done((bf16[96,3584]{1,0:T(8,128)(2,1)}, bf16[96,3584]{1,0:T(8,128)(2,1)}, u32[]{:S(2)}, u32[]{:S(2)}) %collective-permute-start.22) | collective-permute-done | bytes 688160 | tf_op jit(solution)/shard_map/back_far/ppermute | solution.py:376
  211.1 3.2 %near.3 = (bf16[192,3584]{1,0:T(8,128)(2,1)S(1)}, bf16[192,3584]{1,0:T(8,128)(2,1)}) custom-call(bf16[192,3584]{1,0:T(8,128)(2,1)} %get-tuple-element.76.left_ref, bf16[192,3584]{1,0:T(8,128)(2,1)} %get-tuple-element.77.right_ref, bf16[96,3584]{1,0:T(8,128)(2,1)} %collective-permute-done.22.lo_ref, bf16[96,3584]{1,0:T(8,128)(2,1)} %collective-permute-done.23.hi_ref), custom_call_target="tpu_custom_call" | custom-call | flops 999999995904 | bytes 6881280 | tf_op jit(solution)/shard_map/back_near/near/pallas_call | solution.py:426
  214.3 3.3 %collective-permute-start.25 = (bf16[192,3584]{1,0:T(8,128)(2,1)}, bf16[192,3584]{1,0:T(8,128)(2,1)}, u32[]{:S(2)}, u32[]{:S(2)}) collective-permute-start(bf16[192,3584]{1,0:T(8,128)(2,1)} %get-tuple-element.81), channel_id=1, source_target_pairs={{0,3},{1,0},{2,1},{3,2},{4,7},{5,4},{6,5},{7,6},{8,11},{9,8},{10,9... | collective-permute-start | bytes 4128776 | tf_op jit(solution)/shard_map/back_near/ppermute | solution.py:376
  217.6 22.6 %collective-permute-done.17 = bf16[192,3584]{1,0:T(8,128)(2,1)} collective-permute-done((bf16[192,3584]{1,0:T(8,128)(2,1)}, bf16[192,3584]{1,0:T(8,128)(2,1)}, u32[]{:S(2)}, u32[]{:S(2)}) %collective-permute-start.17) | collective-permute-done | bytes 1376288 | tf_op jit(solution)/shard_map/output_near/ppermute | solution.py:376
  240.5 3.3 %add_convert_fusion.1 = bf16[192,3584]{1,0:T(8,128)(2,1)} fusion(bf16[192,3584]{1,0:T(8,128)(2,1)} %collective-permute-done.17, bf16[192,3584]{1,0:T(8,128)(2,1)} %collective-permute-done.16, bf16[192,3584]{1,0:T(8,128)(2,1)S(1)} %get-tuple-element.62), kind=kLoop, calls=%fused_computation.2 | loop fusion | flops 4128768 | bytes 5505024 | tf_op jit(solution)/shard_map/convert_element_type | solution.py:403
  243.9 6.4 %all-to-all-start.4 = ((bf16[8,24,3584]{2,1,0:T(8,128)(2,1)}), bf16[8,24,3584]{2,1,0:T(8,128)(2,1)S(1)}, u32[]{:S(2)}, u32[]{:S(2)}) async-start(bf16[8,24,3584]{2,1,0:T(8,128)(2,1)} %bitcast.58), calls=%async_computation.4 | async-start | bytes 2752512 | tf_op jit(solution)/shard_map/output_plane/all_to_all | solution.py:389
  250.3 2.9 %spread.2 = (bf16[2,128,192]{2,1,0:T(8,128)(2,1)}, f32[128,128]{1,0:T(8,128)}) custom-call(s32[1]{0:T(128)} %bitcast.sel_ref, s32[8]{0:T(128)} %bitcast.53, s32[2,1,128]{2,1,0:T(1,128)} %bitcast.49, f32[2,1,128]{2,1,0:T(1,128)} %bitcast.62), custom_call_target="tpu_custom_call" | custom-call | tf_op jit(solution)/shard_map/spread/pallas_call | solution.py:326
  253.2 2.9 %spread.3 = (bf16[2,128,192]{2,1,0:T(8,128)(2,1)}, f32[128,128]{1,0:T(8,128)}) custom-call(s32[1]{0:T(128)} %bitcast.2.sel_ref, s32[8]{0:T(128)} %bitcast.54, s32[2,1,128]{2,1,0:T(1,128)} %bitcast.50, f32[2,1,128]{2,1,0:T(1,128)} %bitcast.63), custom_call_target="tpu_custom_call" | custom-call | tf_op jit(solution)/shard_map/spread/pallas_call | solution.py:326
  256.1 3.3 %collective-permute-done.25 = bf16[192,3584]{1,0:T(8,128)(2,1)} collective-permute-done((bf16[192,3584]{1,0:T(8,128)(2,1)}, bf16[192,3584]{1,0:T(8,128)(2,1)}, u32[]{:S(2)}, u32[]{:S(2)}) %collective-permute-start.25) | collective-permute-done | bytes 1376288 | tf_op jit(solution)/shard_map/back_near/ppermute | solution.py:376
  259.4 3.8 %add_convert_fusion = bf16[192,3584]{1,0:T(8,128)(2,1)} fusion(bf16[192,3584]{1,0:T(8,128)(2,1)} %collective-permute-done.25, bf16[192,3584]{1,0:T(8,128)(2,1)} %collective-permute-done.24, bf16[192,3584]{1,0:T(8,128)(2,1)} %get-tuple-element.75), kind=kLoop, calls=%fused_computation.1 | loop fusion | flops 4128768 | bytes 5505024 | tf_op jit(solution)/shard_map/convert_element_type | solution.py:403
  263.2 7.2 %all-to-all-start.5 = ((bf16[8,24,3584]{2,1,0:T(8,128)(2,1)}), bf16[8,24,3584]{2,1,0:T(8,128)(2,1)}, u32[]{:S(2)}, u32[]{:S(2)}) async-start(bf16[8,24,3584]{2,1,0:T(8,128)(2,1)} %bitcast.33), calls=%async_computation.5 | async-start | bytes 2752512 | tf_op jit(solution)/shard_map/back_plane/all_to_all | solution.py:389
  270.5 3.0 %mix.2 = bf16[128,7168]{1,0:T(8,128)(2,1)} custom-call(bf16[2,128,192]{2,1,0:T(8,128)(2,1)S(1)} %copy-done.18, f32[128,128]{1,0:T(8,128)S(1)} %copy-done.20, bf16[128,7168]{1,0:T(8,128)(2,1)} %collective-permute-done.2.x_ref, bf16[192,3584]{1,0:T(8,128)(2,1)S(1)} %bitcast.43), custom_call_target="tpu_custom_call" | custom-call | flops 352321536000 | bytes 5046272 | tf_op jit(solution)/shard_map/mix/pallas_call | solution.py:353
  273.4 9.2 %all-to-all-done.5 = bf16[8,24,3584]{2,1,0:T(8,128)(2,1)} async-done(((bf16[8,24,3584]{2,1,0:T(8,128)(2,1)}), bf16[8,24,3584]{2,1,0:T(8,128)(2,1)}, u32[]{:S(2)}, u32[]{:S(2)}) %all-to-all-start.5) | async-done | bytes 1376288 | tf_op jit(solution)/shard_map/back_plane/all_to_all | solution.py:389
  282.6 3.4 %mix.3 = bf16[128,7168]{1,0:T(8,128)(2,1)} custom-call(bf16[2,128,192]{2,1,0:T(8,128)(2,1)S(1)} %copy-done.17, f32[128,128]{1,0:T(8,128)S(1)} %copy-done.19, bf16[128,7168]{1,0:T(8,128)(2,1)} %collective-permute-done.5.lo_ref.hi_ref.x_ref, bf16[192,3584]{1,0:T(8,128)(2,1)} %bitcast.34.refs_0_), custom_call_target="tpu_custom_call" | custom-call | flops 352321536000 | bytes 5046272 | tf_op jit(solution)/shard_map/mix/pallas_call | solution.py:353
  (92 shorter events, 18.5 us)
Async XLA Ops:
  7.0 34.2 %collective-permute-start.2 = (bf16[128,7168]{1,0:T(8,128)(2,1)}, bf16[128,7168]{1,0:T(8,128)(2,1)}, u32[]{:S(2)}, u32[]{:S(2)}) collective-permute-start(bf16[128,7168]{1,0:T(8,128)(2,1)} %dynamic-slice_bitcast_fusion.1), channel_id=1, source_target_pairs={{0,32},{32,64},{64,96},{96,0},{1,33},{33,65},{65,97},{97,1},{2,34}... | collective-permute-start | bytes 5505032 | tf_op jit(solution)/shard_map/ppermute | solution.py:376
  11.2 24.4 %copy-start.3 = (bf16[192,1792]{1,0:T(8,128)(2,1)}, bf16[192,1792]{1,0:T(8,128)(2,1)S(1)}, u32[]{:S(2)}) copy-start(bf16[192,1792]{1,0:T(8,128)(2,1)S(1)} %get-tuple-element.43) | copy-start | bytes 2064388
  11.2 20.3 %collective-permute-start = (bf16[192,1792]{1,0:T(8,128)(2,1)S(1)}, bf16[192,1792]{1,0:T(8,128)(2,1)S(1)}, u32[]{:S(2)}, u32[]{:S(2)}) collective-permute-start(bf16[192,1792]{1,0:T(8,128)(2,1)S(1)} %get-tuple-element.43), channel_id=1, source_target_pairs={{0,1},{1,2},{2,3},{3,0},{4,5},{5,6},{6,7},{7,4},{8,9},{9,10},{10,1... | collective-permute-start | bytes 2064392 | tf_op jit(solution)/shard_map/saved_ring_a/ppermute | solution.py:376
  13.2 18.4 %collective-permute-start.1 = (bf16[192,1792]{1,0:T(8,128)(2,1)S(1)}, bf16[192,1792]{1,0:T(8,128)(2,1)S(1)}, u32[]{:S(2)}, u32[]{:S(2)}) collective-permute-start(bf16[192,1792]{1,0:T(8,128)(2,1)S(1)} %get-tuple-element.43), channel_id=1, source_target_pairs={{0,3},{1,0},{2,1},{3,2},{4,7},{5,4},{6,5},{7,6},{8,11},{9,8},{10,9... | collective-permute-start | bytes 2064392 | tf_op jit(solution)/shard_map/saved_ring_a/ppermute | solution.py:376
  15.3 25.8 %all-to-all-start = ((bf16[8,24,1792]{2,1,0:T(8,128)(2,1)}), bf16[8,24,1792]{2,1,0:T(8,128)(2,1)S(1)}, u32[]{:S(2)}, u32[]{:S(2)}) async-start(bf16[8,24,1792]{2,1,0:T(8,128)(2,1)} %bitcast.14), calls=%async_computation | async-start | bytes 1376256 | tf_op jit(solution)/shard_map/saved_plane_b/all_to_all | solution.py:389
  31.5 9.6 %copy-start.21 = (bf16[192,1792]{1,0:T(8,128)(2,1)}, bf16[192,1792]{1,0:T(8,128)(2,1)S(1)}, u32[]{:S(2)}) copy-start(bf16[192,1792]{1,0:T(8,128)(2,1)S(1)} %collective-permute-done) | copy-start | bytes 2064388
  31.5 9.6 %copy-start.23 = (bf16[192,1792]{1,0:T(8,128)(2,1)}, bf16[192,1792]{1,0:T(8,128)(2,1)S(1)}, u32[]{:S(2)}) copy-start(bf16[192,1792]{1,0:T(8,128)(2,1)S(1)} %collective-permute-done.1) | copy-start | bytes 2064388
  33.6 11.7 %collective-permute-start.3 = (bf16[96,1792]{1,0:T(8,128)(2,1)}, bf16[96,1792]{1,0:T(8,128)(2,1)}, u32[]{:S(2)}, u32[]{:S(2)}) collective-permute-start(bf16[96,1792]{1,0:T(8,128)(2,1)} %slice.32), channel_id=1, source_target_pairs={{0,1},{1,2},{2,3},{3,0},{4,5},{5,6},{6,7},{7,4},{8,9},{9,10},{10,1... | collective-permute-start | bytes 1032200 | tf_op jit(solution)/shard_map/saved_ring_a/ppermute | solution.py:376
  35.6 9.7 %collective-permute-start.4 = (bf16[96,1792]{1,0:T(8,128)(2,1)}, bf16[96,1792]{1,0:T(8,128)(2,1)}, u32[]{:S(2)}, u32[]{:S(2)}) collective-permute-start(bf16[96,1792]{1,0:T(8,128)(2,1)} %slice.33), channel_id=1, source_target_pairs={{0,3},{1,0},{2,1},{3,2},{4,7},{5,4},{6,5},{7,6},{8,11},{9,8},{10,9... | collective-permute-start | bytes 1032200 | tf_op jit(solution)/shard_map/saved_ring_a/ppermute | solution.py:376
  41.1 30.9 %collective-permute-start.5 = (bf16[128,7168]{1,0:T(8,128)(2,1)}, bf16[128,7168]{1,0:T(8,128)(2,1)}, u32[]{:S(2)}, u32[]{:S(2)}) collective-permute-start(bf16[128,7168]{1,0:T(8,128)(2,1)} %dynamic-slice_bitcast_fusion), channel_id=1, source_target_pairs={{0,96},{32,0},{64,32},{96,64},{1,97},{33,1},{65,33},{97,65},{2,98}... | collective-permute-start | bytes 5505032 | tf_op jit(solution)/shard_map/ppermute | solution.py:376
  41.1 4.2 %copy-start = (bf16[8,24,1792]{2,1,0:T(8,128)(2,1)}, bf16[8,24,1792]{2,1,0:T(8,128)(2,1)S(1)}, u32[]{:S(2)}) copy-start(bf16[8,24,1792]{2,1,0:T(8,128)(2,1)S(1)} %all-to-all-done) | copy-start | bytes 2064388
  45.3 7.0 %copy-start.1 = (bf16[8,24,1792]{2,1,0:T(8,128)(2,1)S(1)}, bf16[8,24,1792]{2,1,0:T(8,128)(2,1)}, u32[]{:S(2)}) copy-start(bf16[8,24,1792]{2,1,0:T(8,128)(2,1)} %copy-done) | copy-start | bytes 2064388
  45.3 34.1 %all-to-all-start.3 = ((bf16[8,24,3584]{2,1,0:T(8,128)(2,1)}), bf16[8,24,3584]{2,1,0:T(8,128)(2,1)}, u32[]{:S(2)}, u32[]{:S(2)}) async-start(bf16[8,24,3584]{2,1,0:T(8,128)(2,1)} %bitcast.27), calls=%async_computation.3 | async-start | bytes 2752512 | tf_op jit(solution)/shard_map/input_plane/all_to_all | solution.py:389
  52.3 18.0 %collective-permute-start.6 = (bf16[192,1792]{1,0:T(8,128)(2,1)S(1)}, bf16[192,1792]{1,0:T(8,128)(2,1)S(1)}, u32[]{:S(2)}, u32[]{:S(2)}) collective-permute-start(bf16[192,1792]{1,0:T(8,128)(2,1)S(1)} %bitcast.45), channel_id=1, source_target_pairs={{0,1},{1,2},{2,3},{3,0},{4,5},{5,6},{6,7},{7,4},{8,9},{9,10},{10,1... | collective-permute-start | bytes 2064392 | tf_op jit(solution)/shard_map/saved_ring_b/ppermute | solution.py:376
  53.9 16.4 %collective-permute-start.7 = (bf16[192,1792]{1,0:T(8,128)(2,1)S(1)}, bf16[192,1792]{1,0:T(8,128)(2,1)S(1)}, u32[]{:S(2)}, u32[]{:S(2)}) collective-permute-start(bf16[192,1792]{1,0:T(8,128)(2,1)S(1)} %bitcast.46), channel_id=1, source_target_pairs={{0,3},{1,0},{2,1},{3,2},{4,7},{5,4},{6,5},{7,6},{8,11},{9,8},{10,9... | collective-permute-start | bytes 2064392 | tf_op jit(solution)/shard_map/saved_ring_b/ppermute | solution.py:376
  79.4 29.2 %collective-permute-start.10 = (bf16[192,3584]{1,0:T(8,128)(2,1)}, bf16[192,3584]{1,0:T(8,128)(2,1)}, u32[]{:S(2)}, u32[]{:S(2)}) collective-permute-start(bf16[192,3584]{1,0:T(8,128)(2,1)} %bitcast.28.x0), channel_id=1, source_target_pairs={{0,1},{1,2},{2,3},{3,0},{4,5},{5,6},{6,7},{7,4},{8,9},{9,10},{10,1... | collective-permute-start | bytes 4128776 | tf_op jit(solution)/shard_map/input_ring/ppermute | solution.py:376
  80.1 28.5 %collective-permute-start.11 = (bf16[192,3584]{1,0:T(8,128)(2,1)}, bf16[192,3584]{1,0:T(8,128)(2,1)}, u32[]{:S(2)}, u32[]{:S(2)}) collective-permute-start(bf16[192,3584]{1,0:T(8,128)(2,1)} %bitcast.28.x0), channel_id=1, source_target_pairs={{0,3},{1,0},{2,1},{3,2},{4,7},{5,4},{6,5},{7,6},{8,11},{9,8},{10,9... | collective-permute-start | bytes 4128776 | tf_op jit(solution)/shard_map/input_ring/ppermute | solution.py:376
  108.7 5.8 %copy-start.6 = (bf16[192,1792]{1,0:T(8,128)(2,1)S(1)}, bf16[192,1792]{1,0:T(8,128)(2,1)}, u32[]{:S(2)}) copy-start(bf16[192,1792]{1,0:T(8,128)(2,1)} %copy-done.5) | copy-start | bytes 2064388
  108.7 6.6 %copy-start.9 = (bf16[192,1792]{1,0:T(8,128)(2,1)S(1)}, bf16[192,1792]{1,0:T(8,128)(2,1)}, u32[]{:S(2)}) copy-start(bf16[192,1792]{1,0:T(8,128)(2,1)} %copy-done.8) | copy-start | bytes 2064388
  109.9 19.7 %collective-permute-start.12 = (bf16[96,3584]{1,0:T(8,128)(2,1)S(1)}, bf16[96,3584]{1,0:T(8,128)(2,1)S(1)}, u32[]{:S(2)}, u32[]{:S(2)}) collective-permute-start(bf16[96,3584]{1,0:T(8,128)(2,1)S(1)} %slice.28), channel_id=1, source_target_pairs={{0,1},{1,2},{2,3},{3,0},{4,5},{5,6},{6,7},{7,4},{8,9},{9,10},{10,1... | collective-permute-start | bytes 2064392 | tf_op jit(solution)/shard_map/input_ring/ppermute | solution.py:376
  111.1 9.2 %copy-start.4 = (bf16[192,1792]{1,0:T(8,128)(2,1)S(1)}, bf16[192,1792]{1,0:T(8,128)(2,1)}, u32[]{:S(2)}) copy-start(bf16[192,1792]{1,0:T(8,128)(2,1)} %copy-done.3) | copy-start | bytes 2064388
  111.2 9.2 %copy-start.22 = (bf16[192,1792]{1,0:T(8,128)(2,1)S(1)}, bf16[192,1792]{1,0:T(8,128)(2,1)}, u32[]{:S(2)}) copy-start(bf16[192,1792]{1,0:T(8,128)(2,1)} %copy-done.21) | copy-start | bytes 2064388
  111.2 9.2 %copy-start.24 = (bf16[192,1792]{1,0:T(8,128)(2,1)S(1)}, bf16[192,1792]{1,0:T(8,128)(2,1)}, u32[]{:S(2)}) copy-start(bf16[192,1792]{1,0:T(8,128)(2,1)} %copy-done.23) | copy-start | bytes 2064388
  111.2 22.3 %collective-permute-start.13 = (bf16[96,3584]{1,0:T(8,128)(2,1)S(1)}, bf16[96,3584]{1,0:T(8,128)(2,1)S(1)}, u32[]{:S(2)}, u32[]{:S(2)}) collective-permute-start(bf16[96,3584]{1,0:T(8,128)(2,1)S(1)} %slice.29), channel_id=1, source_target_pairs={{0,3},{1,0},{2,1},{3,2},{4,7},{5,4},{6,5},{7,6},{8,11},{9,8},{10,9... | collective-permute-start | bytes 2064392 | tf_op jit(solution)/shard_map/input_ring/ppermute | solution.py:376
  115.2 33.4 %collective-permute-start.8 = (bf16[96,1792]{1,0:T(8,128)(2,1)}, bf16[96,1792]{1,0:T(8,128)(2,1)}, u32[]{:S(2)}, u32[]{:S(2)}) collective-permute-start(bf16[96,1792]{1,0:T(8,128)(2,1)} %slice.34), channel_id=1, source_target_pairs={{0,1},{1,2},{2,3},{3,0},{4,5},{5,6},{6,7},{7,4},{8,9},{9,10},{10,1... | collective-permute-start | bytes 1032200 | tf_op jit(solution)/shard_map/saved_ring_b/ppermute | solution.py:376
  116.0 32.7 %collective-permute-start.9 = (bf16[96,1792]{1,0:T(8,128)(2,1)}, bf16[96,1792]{1,0:T(8,128)(2,1)}, u32[]{:S(2)}, u32[]{:S(2)}) collective-permute-start(bf16[96,1792]{1,0:T(8,128)(2,1)} %slice.35), channel_id=1, source_target_pairs={{0,3},{1,0},{2,1},{3,2},{4,7},{5,4},{6,5},{7,6},{8,11},{9,8},{10,9... | collective-permute-start | bytes 1032200 | tf_op jit(solution)/shard_map/saved_ring_b/ppermute | solution.py:376
  122.1 36.2 %collective-permute-start.18 = (bf16[192,3584]{1,0:T(8,128)(2,1)}, bf16[192,3584]{1,0:T(8,128)(2,1)}, u32[]{:S(2)}, u32[]{:S(2)}) collective-permute-start(bf16[192,3584]{1,0:T(8,128)(2,1)} %bitcast.23.x0), channel_id=1, source_target_pairs={{0,1},{1,2},{2,3},{3,0},{4,5},{5,6},{6,7},{7,4},{8,9},{9,10},{10,1... | collective-permute-start | bytes 4128776 | tf_op jit(solution)/shard_map/grad_ring/ppermute | solution.py:376
  122.1 27.4 %all-to-all-start.2 = ((bf16[8,96,1792]{2,1,0:T(8,128)(2,1)}), bf16[8,96,1792]{2,1,0:T(8,128)(2,1)}, u32[]{:S(2)}, u32[]{:S(2)}) async-start(bf16[8,96,1792]{2,1,0:T(8,128)(2,1)} %bitcast.57), calls=%async_computation.2 | async-start | bytes 5505024 | tf_op jit(solution)/shard_map/saved_plane_a/all_to_all | solution.py:389
  130.4 27.9 %collective-permute-start.19 = (bf16[192,3584]{1,0:T(8,128)(2,1)}, bf16[192,3584]{1,0:T(8,128)(2,1)}, u32[]{:S(2)}, u32[]{:S(2)}) collective-permute-start(bf16[192,3584]{1,0:T(8,128)(2,1)} %bitcast.23.x0), channel_id=1, source_target_pairs={{0,3},{1,0},{2,1},{3,2},{4,7},{5,4},{6,5},{7,6},{8,11},{9,8},{10,9... | collective-permute-start | bytes 4128776 | tf_op jit(solution)/shard_map/grad_ring/ppermute | solution.py:376
  136.5 13.1 %copy-start.2 = (bf16[8,24,1792]{2,1,0:T(8,128)(2,1)S(1)}, bf16[8,24,1792]{2,1,0:T(8,128)(2,1)}, u32[]{:S(2)}) copy-start(bf16[8,24,1792]{2,1,0:T(8,128)(2,1)} %copy-done) | copy-start | bytes 2064388
  136.5 13.1 %copy-start.7 = (bf16[192,1792]{1,0:T(8,128)(2,1)S(1)}, bf16[192,1792]{1,0:T(8,128)(2,1)}, u32[]{:S(2)}) copy-start(bf16[192,1792]{1,0:T(8,128)(2,1)} %copy-done.5) | copy-start | bytes 2064388
  136.5 13.1 %copy-start.10 = (bf16[192,1792]{1,0:T(8,128)(2,1)S(1)}, bf16[192,1792]{1,0:T(8,128)(2,1)}, u32[]{:S(2)}) copy-start(bf16[192,1792]{1,0:T(8,128)(2,1)} %copy-done.8) | copy-start | bytes 2064388
  159.5 18.7 %collective-permute-start.20 = (bf16[96,3584]{1,0:T(8,128)(2,1)S(1)}, bf16[96,3584]{1,0:T(8,128)(2,1)S(1)}, u32[]{:S(2)}, u32[]{:S(2)}) collective-permute-start(bf16[96,3584]{1,0:T(8,128)(2,1)S(1)} %slice.30), channel_id=1, source_target_pairs={{0,1},{1,2},{2,3},{3,0},{4,5},{5,6},{6,7},{7,4},{8,9},{9,10},{10,1... | collective-permute-start | bytes 2064392 | tf_op jit(solution)/shard_map/grad_ring/ppermute | solution.py:376
  160.7 17.5 %collective-permute-start.21 = (bf16[96,3584]{1,0:T(8,128)(2,1)S(1)}, bf16[96,3584]{1,0:T(8,128)(2,1)S(1)}, u32[]{:S(2)}, u32[]{:S(2)}) collective-permute-start(bf16[96,3584]{1,0:T(8,128)(2,1)S(1)} %slice.31), channel_id=1, source_target_pairs={{0,3},{1,0},{2,1},{3,2},{4,7},{5,4},{6,5},{7,6},{8,11},{9,8},{10,9... | collective-permute-start | bytes 2064392 | tf_op jit(solution)/shard_map/grad_ring/ppermute | solution.py:376
  164.0 30.5 %collective-permute-start.14 = (bf16[96,3584]{1,0:T(8,128)(2,1)}, bf16[96,3584]{1,0:T(8,128)(2,1)}, u32[]{:S(2)}, u32[]{:S(2)}) collective-permute-start(bf16[96,3584]{1,0:T(8,128)(2,1)} %get-tuple-element.65), channel_id=1, source_target_pairs={{0,1},{1,2},{2,3},{3,0},{4,5},{5,6},{6,7},{7,4},{8,9},{9,10},{10,1... | collective-permute-start | bytes 2064392 | tf_op jit(solution)/shard_map/output_far/ppermute | solution.py:376
  164.0 30.5 %collective-permute-start.15 = (bf16[96,3584]{1,0:T(8,128)(2,1)}, bf16[96,3584]{1,0:T(8,128)(2,1)}, u32[]{:S(2)}, u32[]{:S(2)}) collective-permute-start(bf16[96,3584]{1,0:T(8,128)(2,1)} %get-tuple-element.66), channel_id=1, source_target_pairs={{0,3},{1,0},{2,1},{3,2},{4,7},{5,4},{6,5},{7,6},{8,11},{9,8},{10,9... | collective-permute-start | bytes 2064392 | tf_op jit(solution)/shard_map/output_far/ppermute | solution.py:376
  190.4 20.6 %collective-permute-start.22 = (bf16[96,3584]{1,0:T(8,128)(2,1)}, bf16[96,3584]{1,0:T(8,128)(2,1)}, u32[]{:S(2)}, u32[]{:S(2)}) collective-permute-start(bf16[96,3584]{1,0:T(8,128)(2,1)} %get-tuple-element.78), channel_id=1, source_target_pairs={{0,1},{1,2},{2,3},{3,0},{4,5},{5,6},{6,7},{7,4},{8,9},{9,10},{10,1... | collective-permute-start | bytes 2064392 | tf_op jit(solution)/shard_map/back_far/ppermute | solution.py:376
  191.0 20.0 %collective-permute-start.23 = (bf16[96,3584]{1,0:T(8,128)(2,1)}, bf16[96,3584]{1,0:T(8,128)(2,1)}, u32[]{:S(2)}, u32[]{:S(2)}) collective-permute-start(bf16[96,3584]{1,0:T(8,128)(2,1)} %get-tuple-element.79), channel_id=1, source_target_pairs={{0,3},{1,0},{2,1},{3,2},{4,7},{5,4},{6,5},{7,6},{8,11},{9,8},{10,9... | collective-permute-start | bytes 2064392 | tf_op jit(solution)/shard_map/back_far/ppermute | solution.py:376
  197.9 42.3 %collective-permute-start.17 = (bf16[192,3584]{1,0:T(8,128)(2,1)}, bf16[192,3584]{1,0:T(8,128)(2,1)}, u32[]{:S(2)}, u32[]{:S(2)}) collective-permute-start(bf16[192,3584]{1,0:T(8,128)(2,1)} %get-tuple-element.68), channel_id=1, source_target_pairs={{0,3},{1,0},{2,1},{3,2},{4,7},{5,4},{6,5},{7,6},{8,11},{9,8},{10,9... | collective-permute-start | bytes 4128776 | tf_op jit(solution)/shard_map/output_near/ppermute | solution.py:376
  199.8 40.7 %collective-permute-start.16 = (bf16[192,3584]{1,0:T(8,128)(2,1)}, bf16[192,3584]{1,0:T(8,128)(2,1)}, u32[]{:S(2)}, u32[]{:S(2)}) collective-permute-start(bf16[192,3584]{1,0:T(8,128)(2,1)} %get-tuple-element.67), channel_id=1, source_target_pairs={{0,1},{1,2},{2,3},{3,0},{4,5},{5,6},{6,7},{7,4},{8,9},{9,10},{10,1... | collective-permute-start | bytes 4128776 | tf_op jit(solution)/shard_map/output_near/ppermute | solution.py:376
  214.3 45.2 %collective-permute-start.25 = (bf16[192,3584]{1,0:T(8,128)(2,1)}, bf16[192,3584]{1,0:T(8,128)(2,1)}, u32[]{:S(2)}, u32[]{:S(2)}) collective-permute-start(bf16[192,3584]{1,0:T(8,128)(2,1)} %get-tuple-element.81), channel_id=1, source_target_pairs={{0,3},{1,0},{2,1},{3,2},{4,7},{5,4},{6,5},{7,6},{8,11},{9,8},{10,9... | collective-permute-start | bytes 4128776 | tf_op jit(solution)/shard_map/back_near/ppermute | solution.py:376
  217.6 41.9 %collective-permute-start.24 = (bf16[192,3584]{1,0:T(8,128)(2,1)S(1)}, bf16[192,3584]{1,0:T(8,128)(2,1)}, u32[]{:S(2)}, u32[]{:S(2)}) collective-permute-start(bf16[192,3584]{1,0:T(8,128)(2,1)S(1)} %get-tuple-element.80), channel_id=1, source_target_pairs={{0,1},{1,2},{2,3},{3,0},{4,5},{5,6},{6,7},{7,4},{8,9},{9,10},{10,1... | collective-permute-start | bytes 4128776 | tf_op jit(solution)/shard_map/back_near/ppermute | solution.py:376
  243.9 19.4 %all-to-all-start.4 = ((bf16[8,24,3584]{2,1,0:T(8,128)(2,1)}), bf16[8,24,3584]{2,1,0:T(8,128)(2,1)S(1)}, u32[]{:S(2)}, u32[]{:S(2)}) async-start(bf16[8,24,3584]{2,1,0:T(8,128)(2,1)} %bitcast.58), calls=%async_computation.4 | async-start | bytes 2752512 | tf_op jit(solution)/shard_map/output_plane/all_to_all | solution.py:389
  263.2 7.2 %copy-start.18 = (bf16[2,128,192]{2,1,0:T(8,128)(2,1)S(1)}, bf16[2,128,192]{2,1,0:T(8,128)(2,1)}, u32[]{:S(2)}) copy-start(bf16[2,128,192]{2,1,0:T(8,128)(2,1)} %get-tuple-element.58.spread_ref) | copy-start | bytes 294916
  263.2 7.2 %copy-start.20 = (f32[128,128]{1,0:T(8,128)S(1)}, f32[128,128]{1,0:T(8,128)}, u32[]{:S(2)}) copy-start(f32[128,128]{1,0:T(8,128)} %get-tuple-element.59.prob_ref) | copy-start | bytes 196612
  263.2 19.4 %all-to-all-start.5 = ((bf16[8,24,3584]{2,1,0:T(8,128)(2,1)}), bf16[8,24,3584]{2,1,0:T(8,128)(2,1)}, u32[]{:S(2)}, u32[]{:S(2)}) async-start(bf16[8,24,3584]{2,1,0:T(8,128)(2,1)} %bitcast.33), calls=%async_computation.5 | async-start | bytes 2752512 | tf_op jit(solution)/shard_map/back_plane/all_to_all | solution.py:389
  270.5 12.2 %copy-start.17 = (bf16[2,128,192]{2,1,0:T(8,128)(2,1)S(1)}, bf16[2,128,192]{2,1,0:T(8,128)(2,1)}, u32[]{:S(2)}) copy-start(bf16[2,128,192]{2,1,0:T(8,128)(2,1)} %get-tuple-element.69.spread_ref) | copy-start | bytes 294916
  270.5 12.2 %copy-start.19 = (f32[128,128]{1,0:T(8,128)S(1)}, f32[128,128]{1,0:T(8,128)}, u32[]{:S(2)}) copy-start(f32[128,128]{1,0:T(8,128)} %get-tuple-element.70.prob_ref) | copy-start | bytes 196612
  (8 other events, 11.4 us)
